TPU v7x, 32 devices: a whole 2x2x4 slice. The times are simulated.
32 devices in a mesh: ctx: 16 (over z, y, x), wt: 2 (over core).
Axes of the slice: x: 2, y: 2, z: 4, core: 2. Of those that a mesh axis runs over, the one named last changes fastest.
Arguments:
- tokens: bfloat16 [8192, 2048], P('ctx'), may hold values from -6 to 6
- cotangent: bfloat16 [8192, 2048], P('ctx'), may hold values from -6 to 6
- mix_norm_gain: bfloat16 [2048], P('ctx'), may hold values from 0.5 to 1.5
- ssm_gate_proj: bfloat16 [2048, 3072], P('ctx', 'wt'), may hold values from -0.125 to 0.125
- ssm_input_proj: bfloat16 [2048, 3072], P('ctx', 'wt'), may hold values from -0.125 to 0.125
- ssm_bc_proj: bfloat16 [2048, 512], P('ctx'), may hold values from -0.125 to 0.125
- ssm_step_proj: bfloat16 [2048, 48], P('ctx', 'wt'), may hold values from -0.125 to 0.125
- conv_in_weight: bfloat16 [3072, 4], P('wt'), may hold values from -3 to 3
- conv_in_bias: bfloat16 [3072], P('wt'), may hold values from -3 to 3
- conv_bc_weight: bfloat16 [512, 4], P('ctx'), may hold values from -3 to 3
- conv_bc_bias: bfloat16 [512], P('ctx'), may hold values from -3 to 3
- step_bias: bfloat16 [48], P('wt'), may hold values from -12 to -5
- decay_log: bfloat16 [48], P('wt'), may hold values from 0 to 1.3984375
- skip_gain: bfloat16 [48], P('wt'), may hold values from 0.5 to 1.5
- ssm_out_proj: bfloat16 [3072, 2048], P('wt', 'ctx'), may hold values from -0.109375 to 0.109375
- query_proj: bfloat16 [2048, 1024], P('ctx', 'wt'), may hold values from -0.125 to 0.125
- key_proj: bfloat16 [2048, 256], P('ctx', 'wt'), may hold values from -0.125 to 0.125
- value_proj: bfloat16 [2048, 256], P('ctx', 'wt'), may hold values from -0.125 to 0.125
- attn_out_proj: bfloat16 [1024, 2048], P('wt', 'ctx'), may hold values from -3 to 3
- ffn_norm_gain: bfloat16 [2048], P('ctx'), may hold values from 0.5 to 1.5
- ffn_gate_proj: bfloat16 [2048, 4096], P('ctx', 'wt'), may hold values from -0.125 to 0.125
- ffn_up_proj: bfloat16 [2048, 4096], P('ctx', 'wt'), may hold values from -0.125 to 0.125
- ffn_down_proj: bfloat16 [4096, 2048], P('wt', 'ctx'), may hold values from -0.09375 to 0.09375
- extra_blocks: int32 [4], replicated, may hold values from 1 to 7, 12 in all
- seq_order: int32 [4], replicated, may hold values from 0 to 3, each once
- pad_rows: int32 [4], replicated, may hold values from 0 to 255
Outputs:
- layer_out: bfloat16 [8192, 2048], P('ctx')
- tokens_grad: bfloat16 [8192, 2048], P('ctx')
- mix_norm_gain_grad: float32 [2048], P('ctx')
- ssm_gate_proj_grad: float32 [2048, 3072], P('ctx', 'wt')
- ssm_input_proj_grad: float32 [2048, 3072], P('ctx', 'wt')
- ssm_bc_proj_grad: float32 [2048, 512], P('ctx')
- ssm_step_proj_grad: float32 [2048, 48], P('ctx', 'wt')
- conv_in_weight_grad: float32 [3072, 4], P('wt')
- conv_in_bias_grad: float32 [3072], P('wt')
- conv_bc_weight_grad: float32 [512, 4], P('ctx')
- conv_bc_bias_grad: float32 [512], P('ctx')
- step_bias_grad: float32 [48], P('wt')
- decay_log_grad: float32 [48], P('wt')
- skip_gain_grad: float32 [48], P('wt')
- ssm_out_proj_grad: float32 [3072, 2048], P('wt', 'ctx')
- query_proj_grad: float32 [2048, 1024], P('ctx', 'wt')
- key_proj_grad: float32 [2048, 256], P('ctx', 'wt')
- value_proj_grad: float32 [2048, 256], P('ctx', 'wt')
- attn_out_proj_grad: float32 [1024, 2048], P('wt', 'ctx')
- ffn_norm_gain_grad: float32 [2048], P('ctx')
- ffn_gate_proj_grad: float32 [2048, 4096], P('ctx', 'wt')
- ffn_up_proj_grad: float32 [2048, 4096], P('ctx', 'wt')
- ffn_down_proj_grad: float32 [4096, 2048], P('wt', 'ctx')
Inputs may be any that keep to these rules, and one draw needn't show every extreme that they name: Sequence s occupies extra_blocks[s] + 1 blocks of 512 rows; the entries sum to 12, and one of them is 7. `seq_order`: A permutation of the sequences.
All inputs are finite; a program needn't handle non-finite values.
Results may differ from a plain program's by a relative error of at most 0.015.
Values may be sent and summed in bfloat16 or wider, within the bound.
No kernel may reach another device: no remote copies, remote signals or barrier semaphores. Data moves between devices by JAX's collectives and lax.ppermute only.
A program may use at most 448 MiB of HBM per device.

v0:
```python
import jax
import jax.numpy as jnp
from jax import lax
from jax.experimental import pallas as pl
from jax.experimental.pallas import tpu as pltpu
from jax.sharding import PartitionSpec as P


HD = 128
KW = 4
MAXB = 8
EXTRA = 16
SCAN_ROWS = 128
ATTN_ROWS = 256


epsilon = 1e-05
rope_base = 100000000000.0
highest = lax.Precision.HIGHEST
masked_score = -1e30


def shifted(value, axis, steps):
    count = lax.axis_size(axis)
    leading, last = (max(0, -steps), min(count, count - steps))
    return lax.ppermute(value, axis, [(source, source + steps) for source in range(leading, last)])


def hop(value, code):
    if code == 0:
        return value
    count = lax.axis_size("ctx")
    return lax.ppermute(value, "ctx", [(source, source ^ code) for source in range(count)])


def swap(value):
    return lax.ppermute(value, "wt", [(0, 1), (1, 0)])


def pair_sum(value):
    rounded = lax.reduce_precision(value, 8, 7)
    return rounded + swap(rounded.astype(jnp.bfloat16)).astype(jnp.float32)


def slot_devices(count):
    high = count // 4
    return [4 * (slot % high) + slot // high for slot in range(count)]


def after(value, *gates):
    return lax.optimization_barrier((value, *gates))[0]


def spread(held, axis, codes, gates=(), merge=False):
    if merge:
        every = [code for here, _ in held for code in here]
        held = [(every, jnp.concatenate([array for _, array in held], axis=axis))]
    taken = list(held)
    for here, array in held:
        operand = after(array, *gates) if gates else array
        for code in codes:
            taken.append(([one ^ code for one in here], hop(operand, code)))
    return taken


def joined(held, axis):
    size = sum(array.shape[axis] for _, array in held) // sum(len(here) for here, _ in held)
    found = {code: (i, at) for i, (here, _) in enumerate(held) for at, code in enumerate(here)}
    runs = []
    for code in slot_devices(len(found)):
        i, at = found[code]
        if runs and runs[-1][0] == i and runs[-1][2] == at:
            runs[-1][2] = at + 1
        else:
            runs.append([i, at, at + 1])
    return jnp.concatenate(
        [lax.slice_in_dim(held[i][1], at * size, to * size, axis=axis) for i, at, to in runs],
        axis=axis,
    )


class Reduction:
    def __init__(self, parts, axis, first, gates=()):
        self.axis, self.second = (axis, 3 - first)
        self.near, self.far = (parts[0], parts[3 - first])
        low = [parts[k].astype(jnp.bfloat16) for k in (first, 3)]
        if gates:
            low = lax.optimization_barrier((*low, *gates))[:2]
        self.got = [hop(part, first) for part in low]

    def onward(self, *gates):
        far = self.far + self.got[1].astype(jnp.float32)
        self.far_low = far.astype(jnp.bfloat16)
        operand = after(self.far_low, *gates) if gates else self.far_low
        self.near = self.near + self.got[0].astype(jnp.float32)
        self.got = [hop(operand, self.second)]

    def last(self, *gates):
        high = lax.axis_size("ctx") // 4
        quarter = self.near + self.got[0].astype(jnp.float32)
        blocks = jnp.split(quarter, high, axis=self.axis)
        self.block = blocks[0]
        self.blocks_low = [block.astype(jnp.bfloat16) for block in blocks[1:]]
        operands = self.blocks_low
        if gates:
            operands = lax.optimization_barrier((*operands, *gates))[: len(operands)]
        self.got = [hop(block, 4 * (k + 1)) for k, block in enumerate(operands)]

    def total(self):
        total = self.block
        for got in self.got:
            total = total + got.astype(jnp.float32)
        return total


def summed(value):
    bit = 1
    while bit < lax.axis_size("ctx"):
        value = value + hop(value, bit)
        bit *= 2
    return value


def reordered(value, order):
    blocks = order.shape[0]
    rows, width = value.shape[0], value.shape[1] // blocks
    if width % 128:
        return jnp.take(value.reshape(rows, blocks, width), order, axis=1).reshape(rows, -1)

    steps = 4 if rows % 64 == 0 else 3
    part = rows // steps

    def body(order_ref, in_ref, out_ref):
        for slot in range(blocks):
            start = pl.multiple_of(order_ref[slot] * width, width)
            out_ref[:, slot * width : (slot + 1) * width] = in_ref[:, pl.ds(start, width)]

    block = pl.BlockSpec((part, value.shape[1]), lambda i, order_ref: (i, 0))
    return pl.pallas_call(
        body,
        out_shape=jax.ShapeDtypeStruct(value.shape, value.dtype),
        grid_spec=pltpu.PrefetchScalarGridSpec(
            num_scalar_prefetch=1, grid=(steps,), in_specs=[block], out_specs=block
        ),
        name="reordered",
    )(order, value)


def carried_states(states, decays, reverse):
    me = lax.axis_index("ctx")
    place = me % 4
    width = states.shape[1] // 4
    low = states.astype(jnp.bfloat16)

    def quarter(value, index):
        return lax.dynamic_slice_in_dim(value, index * width, width, 1)

    got = [hop(quarter(low, place ^ k), k) for k in range(4)]
    got_decay = [hop(quarter(decays, place ^ k), k) for k in range(4)]

    def in_order(pieces):
        odd = place % 2 == 1
        pieces = [jnp.where(odd, pieces[k ^ 1], pieces[k]) for k in range(4)]
        upper = place >= 2
        return [jnp.where(upper, pieces[k ^ 2], pieces[k]) for k in range(4)]

    blocks = [piece.astype(jnp.float32) for piece in in_order(got)]
    rates = in_order(got_decay)
    if reverse:
        blocks, rates = (blocks[::-1], rates[::-1])
    total, rate = (blocks[0], rates[0])
    for block, block_rate in zip(blocks[1:], rates[1:]):
        total, rate = (block + block_rate * total, block_rate * rate)
    step = -4 if reverse else 4
    total_low = total.astype(jnp.bfloat16)
    near, near_rate = (shifted(total_low, "ctx", step), shifted(rate, "ctx", step))
    far = shifted(total_low, "ctx", 2 * step)
    state = near.astype(jnp.float32) + near_rate * far.astype(jnp.float32)
    reached = []
    for block, block_rate in zip(blocks, rates):
        reached.append(state.astype(jnp.bfloat16))
        state = block + block_rate * state
    if reverse:
        reached = reached[::-1]
    mine = in_order(reached)
    back = in_order([hop(mine[k], k) for k in range(4)])
    return (jnp.concatenate(back, axis=1), mine[1])


def plain_product(left_side, right_side):
    return jnp.dot(left_side, right_side, preferred_element_type=jnp.float32)


def product_by_rows(left_side, right_side):
    return lax.dot_general(
        left_side, right_side, (((1,), (1,)), ((), ())), preferred_element_type=jnp.float32
    )


def product_of_cols(left_side, right_side):
    return lax.dot_general(
        left_side, right_side, (((0,), (0,)), ((), ())), preferred_element_type=jnp.float32
    )


def rms_scale(values, gain_vec):
    return (
        values * lax.rsqrt(jnp.mean(values * values, axis=-1, keepdims=True) + epsilon) * gain_vec
    )


def rotary_tables(positions):
    exponents = jnp.arange(HD // 2, dtype=jnp.float32) * (2.0 / HD)
    frequency = jnp.power(jnp.float32(rope_base), -exponents)
    angles = positions.astype(jnp.float32)[:, None] * frequency[None, :]
    return (jnp.cos(angles), jnp.sin(angles))


def rotate(values, cos_table, sin_table):
    half_dim = values.shape[-1] // 2
    first_half = values[..., :half_dim]
    second_half = values[..., half_dim:]
    cos_table = cos_table[:, None, :]
    sin_table = sin_table[:, None, :]
    return jnp.concatenate(
        [
            first_half * cos_table - second_half * sin_table,
            second_half * cos_table + first_half * sin_table,
        ],
        axis=-1,
    )


def convolved(rim, block, taps):
    length = block.shape[0]
    extended = jnp.concatenate([rim, block], axis=0)
    first = rim.shape[0] - (KW - 1)
    summed = taps[KW : KW + 1]
    for j in range(KW):
        summed = summed + extended[first + j : first + j + length] * taps[j : j + 1]
    return (extended, summed)


def convolved_back(extended, pre_grad, taps):
    length = pre_grad.shape[0]
    rim_rows = extended.shape[0] - length
    first = rim_rows - (KW - 1)
    zeros = jnp.zeros((8, pre_grad.shape[1]), jnp.float32)
    padded = jnp.concatenate([zeros, pre_grad, zeros], axis=0)
    total = jnp.zeros_like(extended)
    rows = []
    for j in range(KW):
        start = 8 - rim_rows + KW - 1 - j
        total = total + padded[start : start + rim_rows + length] * taps[j : j + 1]
        rows.append(
            jnp.sum(pre_grad * extended[first + j : first + j + length], axis=0, keepdims=True)
        )
    rows.append(jnp.sum(pre_grad, axis=0, keepdims=True))
    return (total, rows)


def silu_slope(value, sigmoid):
    return sigmoid * (1.0 + value * (1.0 - sigmoid))


def low_dot(left_side, right_side, left_axis, right_axis):
    return lax.dot_general(
        left_side.astype(jnp.bfloat16),
        right_side.astype(jnp.bfloat16),
        (((left_axis,), (right_axis,)), ((), ())),
        preferred_element_type=jnp.float32,
    )


def lower_gram(c_low, b_low):
    length = c_low.shape[0]
    gram = low_dot(c_low, b_low, 1, 1)
    rows = lax.broadcasted_iota(jnp.int32, (length, length), 0)
    cols = lax.broadcasted_iota(jnp.int32, (length, length), 1)
    return jnp.where(rows >= cols, gram, 0.0)


def scan_blocks(shared, length, wide):
    return [
        pl.BlockSpec((length, wide), lambda i: (0, i)),
        pl.BlockSpec((8, wide), lambda i: ((length + EXTRA) // 8 - 1, i)),
        pl.BlockSpec((8, wide), lambda i: (0, i)),
        pl.BlockSpec((length, shared), lambda i: (0, 0)),
        pl.BlockSpec((8, shared), lambda i: ((length + EXTRA) // 8 - 1, 0)),
        pl.BlockSpec((8, shared), lambda i: (0, 0)),
        pl.BlockSpec((1, length, 2), lambda i: (i, 0, 0)),
        pl.BlockSpec((1, length, 2), lambda i: (i, 0, 0)),
        pl.BlockSpec((1, 2, length), lambda i: (i, 0, 0)),
    ]


def scan_forward(first_pre, mix_pre, taps, bc_taps, step_cols, sum_cols, sum_rows, inner, shared):
    length = first_pre.shape[0] - EXTRA
    pairs = step_cols.shape[0]
    wide = inner // pairs
    size = wide // 2
    state_dim = shared // 2
    part = min(SCAN_ROWS, length)

    def body(
        in_ref, rim_ref, tap_ref, bc_ref, bc_rim_ref, bc_tap_ref, step_ref, col_ref, row_ref,
        out_ref, state_ref, bc_low_ref, gram_ref,
    ):
        @pl.when(pl.program_id(0) == 0)
        def _():
            _, pre = convolved(bc_rim_ref[...], bc_ref[...], bc_tap_ref[...])
            acts = (pre * jax.nn.sigmoid(pre)).astype(jnp.bfloat16)
            bc_low_ref[...] = acts
            gram_ref[...] = lower_gram(acts[:, state_dim:], acts[:, :state_dim])

        taps_here = tap_ref[...]
        _, pre = convolved(rim_ref[...], in_ref[...], taps_here)
        acts = pre * jax.nn.sigmoid(pre)
        tails = []
        for head in range(2):
            lanes = slice(head * size, (head + 1) * size)
            step = step_ref[0][:, head : head + 1]
            col = col_ref[0][:, head : head + 1]
            row = row_ref[0][head : head + 1, :]
            stepped = acts[:, lanes] * step
            stepped_low = stepped.astype(jnp.bfloat16)
            for at in range(0, length, part):
                end = at + part
                decay = jnp.exp(jnp.minimum(col[at:end] - row[:, :end], 0.0))
                weights = (decay * gram_ref[at:end, :end]).astype(jnp.bfloat16)
                out_ref[at:end, lanes] = low_dot(weights, stepped_low[:end], 1, 0) + (
                    taps_here[KW + 1 : KW + 2, lanes] * acts[at:end, lanes]
                )
            tails.append(stepped * jnp.exp(col[length - 1 : length] - col))
        tail = jnp.concatenate(tails, axis=1)
        state_ref[...] = low_dot(bc_low_ref[:, :state_dim], tail, 0, 0).astype(jnp.bfloat16)

    return pl.pallas_call(
        body,
        grid=(pairs,),
        out_shape=(
            jax.ShapeDtypeStruct((length, inner), jnp.float32),
            jax.ShapeDtypeStruct((state_dim, inner), jnp.bfloat16),
            jax.ShapeDtypeStruct((length, shared), jnp.bfloat16),
        ),
        in_specs=scan_blocks(shared, length, wide),
        out_specs=(
            pl.BlockSpec((length, wide), lambda i: (0, i)),
            pl.BlockSpec((state_dim, wide), lambda i: (0, i)),
            pl.BlockSpec((length, shared), lambda i: (0, 0)),
        ),
        scratch_shapes=[pltpu.VMEM((length, length), jnp.float32)],
        compiler_params=pltpu.CompilerParams(vmem_limit_bytes=48 << 20),
        name="scan_forward",
    )(first_pre, first_pre, taps, mix_pre, mix_pre, bc_taps, step_cols, sum_cols, sum_rows)


def scan_gated(intra, state_in, bc_low, sum_cols, second_pre, gate_at):
    length, inner = intra.shape
    pairs = sum_cols.shape[0]
    wide = inner // pairs
    size = wide // 2
    state_dim = bc_low.shape[1] // 2

    def body(intra_ref, state_ref, c_ref, col_ref, gate_ref, out_ref, act_ref):
        carried = low_dot(c_ref[...], state_ref[...], 1, 0)
        gate = gate_ref[...]
        silu = gate * jax.nn.sigmoid(gate)
        for head in range(2):
            lanes = slice(head * size, (head + 1) * size)
            growth = jnp.exp(col_ref[0][:, head : head + 1])
            whole = intra_ref[:, lanes] + carried[:, lanes] * growth
            out_ref[:, lanes] = whole
            act_ref[:, lanes] = (whole * silu[:, lanes]).astype(jnp.bfloat16)

    block = pl.BlockSpec((length, wide), lambda i: (0, i))
    return pl.pallas_call(
        body,
        grid=(pairs,),
        out_shape=(
            jax.ShapeDtypeStruct((length, inner), jnp.float32),
            jax.ShapeDtypeStruct((length, inner), jnp.bfloat16),
        ),
        in_specs=[
            block,
            pl.BlockSpec((state_dim, wide), lambda i: (0, i)),
            pl.BlockSpec((length, state_dim), lambda i: (0, 1)),
            pl.BlockSpec((1, length, 2), lambda i: (i, 0, 0)),
            pl.BlockSpec((length, wide), lambda i: (0, gate_at // wide + i)),
        ],
        out_specs=(block, block),
        compiler_params=pltpu.CompilerParams(vmem_limit_bytes=48 << 20),
        name="scan_gated",
    )(intra, state_in, bc_low, sum_cols, second_pre)


def scan_gated_back(out_grads, whole, bc_low, sum_cols, second_pre, gate_at):
    length, inner = whole.shape
    pairs = sum_cols.shape[0]
    wide = inner // pairs
    size = wide // 2
    state_dim = bc_low.shape[1] // 2

    def body(grad_ref, whole_ref, c_ref, col_ref, gate_ref, gate_grad_ref, state_ref):
        gate = gate_ref[...]
        sigmoid = jax.nn.sigmoid(gate)
        grad = grad_ref[...]
        gate_grad = grad * whole_ref[...] * silu_slope(gate, sigmoid)
        gate_grad_ref[:length] = gate_grad.astype(jnp.bfloat16)
        gate_grad_ref[length:] = jnp.zeros((EXTRA, wide), jnp.bfloat16)
        inside = grad * (gate * sigmoid)
        grown = [
            inside[:, head * size : (head + 1) * size] * jnp.exp(col_ref[0][:, head : head + 1])
            for head in range(2)
        ]
        state_ref[...] = low_dot(c_ref[...], jnp.concatenate(grown, axis=1), 0, 0).astype(
            jnp.bfloat16
        )

    block = pl.BlockSpec((length, wide), lambda i: (0, i))
    return pl.pallas_call(
        body,
        grid=(pairs,),
        out_shape=(
            jax.ShapeDtypeStruct((length + EXTRA, inner), jnp.bfloat16),
            jax.ShapeDtypeStruct((state_dim, inner), jnp.bfloat16),
        ),
        in_specs=[
            block,
            block,
            pl.BlockSpec((length, state_dim), lambda i: (0, 1)),
            pl.BlockSpec((1, length, 2), lambda i: (i, 0, 0)),
            pl.BlockSpec((length, wide), lambda i: (0, gate_at // wide + i)),
        ],
        out_specs=(
            pl.BlockSpec((length + EXTRA, wide), lambda i: (0, i)),
            pl.BlockSpec((state_dim, wide), lambda i: (0, i)),
        ),
        compiler_params=pltpu.CompilerParams(vmem_limit_bytes=48 << 20),
        name="scan_gated_back",
    )(out_grads, whole, bc_low, sum_cols, second_pre)


def scan_back(
    first_pre, mix_pre, taps, bc_taps, step_cols, sum_cols, sum_rows,
    out_grads, second_pre, gate_at, state_in, end_grad, bc_low,
):
    length = first_pre.shape[0] - EXTRA
    pairs = step_cols.shape[0]
    state_dim, inner = state_in.shape
    shared = bc_low.shape[1]
    wide = inner // pairs
    size = wide // 2
    part = min(SCAN_ROWS, length)

    def body(
        in_ref, rim_ref, tap_ref, bc_ref, bc_rim_ref, bc_tap_ref, step_ref, col_ref, row_ref,
        grad_ref, gate_ref, state_ref, end_ref, bc_low_ref,
        in_grad_ref, tap_grad_ref, step_grad_ref, sum_grad_ref, bc_grad_ref, bc_tap_grad_ref,
        gram_ref, gram_grad_ref, acts_grad_ref, back_ref,
    ):
        b_low = bc_low_ref[:, :state_dim]
        c_low = bc_low_ref[:, state_dim:]

        @pl.when(pl.program_id(0) == 0)
        def _():
            gram_ref[...] = lower_gram(c_low, b_low)
            gram_grad_ref[...] = jnp.zeros_like(gram_grad_ref)
            acts_grad_ref[...] = jnp.zeros_like(acts_grad_ref)

        taps_here = tap_ref[...]
        extended, pre = convolved(rim_ref[...], in_ref[...], taps_here)
        sigmoid = jax.nn.sigmoid(pre)
        acts = pre * sigmoid
        gate = gate_ref[...]
        out_grad = grad_ref[...] * (gate * jax.nn.sigmoid(gate))
        state = state_ref[...]
        end = end_ref[...]
        from_end = low_dot(b_low, end, 1, 0)
        from_start = low_dot(c_low, state, 1, 0)
        state_dot = jnp.sum(
            state.astype(jnp.float32) * end.astype(jnp.float32), axis=0, keepdims=True
        )
        last_row = lax.broadcasted_iota(jnp.int32, (length, 1), 0) == length - 1
        acts_grads, tails, grown_grads = ([], [], [])
        for head in range(2):
            lanes = slice(head * size, (head + 1) * size)
            step = step_ref[0][:, head : head + 1]
            col = col_ref[0][:, head : head + 1]
            row = row_ref[0][head : head + 1, :]
            here = acts[:, lanes]
            stepped = here * step
            stepped_low = stepped.astype(jnp.bfloat16)
            grad = out_grad[:, lanes]
            grad_low = grad.astype(jnp.bfloat16)
            grad_wide = grad_low.astype(jnp.float32)
            back_ref[...] = jnp.zeros_like(back_ref)
            row_terms = []
            for at in range(0, length, part):
                to = at + part
                decay = jnp.exp(jnp.minimum(col[at:to] - row[:, :to], 0.0))
                weights = (decay * gram_ref[at:to, :to]).astype(jnp.bfloat16)
                again = low_dot(weights, stepped_low[:to], 1, 0)
                row_terms.append(jnp.sum(again * grad_wide[at:to], axis=1, keepdims=True))
                back_ref[:to] += low_dot(weights, grad_low[at:to], 0, 0)
                gram_grad_ref[at:to, :to] += decay * low_dot(
                    grad_low[at:to], stepped_low[:to], 1, 1
                )
            back = back_ref[...]
            tail = jnp.exp(col[length - 1 : length] - col)
            growth = jnp.exp(col)
            ended = from_end[:, lanes] * tail
            end_terms = jnp.sum(ended * stepped, axis=1, keepdims=True)
            col_terms = jnp.sum(back * stepped_low.astype(jnp.float32), axis=1, keepdims=True)
            start_terms = growth * jnp.sum(from_start[:, lanes] * grad, axis=1, keepdims=True)
            whole = jnp.sum(end_terms, axis=0, keepdims=True) + growth[
                length - 1 : length
            ] * jnp.sum(state_dot[:, lanes], axis=1, keepdims=True)
            sum_grad_ref[0, :, head : head + 1] = (
                jnp.concatenate(row_terms, axis=0)
                + start_terms
                - col_terms
                - end_terms
                + jnp.where(last_row, whole, 0.0)
            )
            back = back + ended
            step_grad_ref[0, :, head : head + 1] = jnp.sum(back * here, axis=1, keepdims=True)
            acts_grads.append(taps_here[KW + 1 : KW + 2, lanes] * grad + back * step)
            tails.append((stepped * tail).astype(jnp.bfloat16))
            grown_grads.append((grad * growth).astype(jnp.bfloat16))
        acts_grad_ref[:, :state_dim] += low_dot(jnp.concatenate(tails, axis=1), end, 1, 1)
        acts_grad_ref[:, state_dim:] += low_dot(jnp.concatenate(grown_grads, axis=1), state, 1, 1)
        pre_grad = jnp.concatenate(acts_grads, axis=1) * silu_slope(pre, sigmoid)
        total, rows = convolved_back(extended, pre_grad, taps_here)
        gap = jnp.zeros((EXTRA - 8, wide), jnp.float32)
        in_grad_ref[...] = jnp.concatenate([total[8:], gap, total[:8]], axis=0).astype(jnp.bfloat16)
        rows.append(jnp.sum(out_grad * acts, axis=0, keepdims=True))
        rows.append(jnp.zeros((8 - len(rows), wide), jnp.float32))
        tap_grad_ref[...] = jnp.concatenate(rows, axis=0)

        @pl.when(pl.program_id(0) == pairs - 1)
        def _():
            gram_grad = gram_grad_ref[...]
            rows_of = lax.broadcasted_iota(jnp.int32, (length, length), 0)
            cols_of = lax.broadcasted_iota(jnp.int32, (length, length), 1)
            gram_grad = jnp.where(rows_of >= cols_of, gram_grad, 0.0).astype(jnp.bfloat16)
            acts_grad_ref[:, :state_dim] += low_dot(gram_grad, c_low, 0, 0)
            acts_grad_ref[:, state_dim:] += low_dot(gram_grad, b_low, 1, 0)
            bc_taps_here = bc_tap_ref[...]
            bc_extended, bc_pre = convolved(bc_rim_ref[...], bc_ref[...], bc_taps_here)
            bc_pre_grad = acts_grad_ref[...] * silu_slope(bc_pre, jax.nn.sigmoid(bc_pre))
            bc_total, bc_rows = convolved_back(bc_extended, bc_pre_grad, bc_taps_here)
            bc_grad_ref[:length] = bc_total[8:]
            bc_grad_ref[length : length + EXTRA - 8] = jnp.zeros((EXTRA - 8, shared), jnp.float32)
            bc_grad_ref[length + EXTRA - 8 :] = bc_total[:8]
            bc_rows.append(jnp.zeros((8 - len(bc_rows), shared), jnp.float32))
            bc_tap_grad_ref[...] = jnp.concatenate(bc_rows, axis=0)

    block = pl.BlockSpec((length, wide), lambda i: (0, i))
    eight = pl.BlockSpec((8, wide), lambda i: (0, i))
    table = pl.BlockSpec((1, length, 2), lambda i: (i, 0, 0))
    state_block = pl.BlockSpec((state_dim, wide), lambda i: (0, i))
    bc_block = pl.BlockSpec((length, shared), lambda i: (0, 0))
    bc_eight = pl.BlockSpec((8, shared), lambda i: (0, 0))
    wide_low = jax.ShapeDtypeStruct((length + EXTRA, inner), jnp.bfloat16)
    eight_f32 = jax.ShapeDtypeStruct((8, inner), jnp.float32)
    table_f32 = jax.ShapeDtypeStruct(step_cols.shape, jnp.float32)
    bc_f32 = jax.ShapeDtypeStruct((length + EXTRA, shared), jnp.float32)
    bc_eight_f32 = jax.ShapeDtypeStruct((8, shared), jnp.float32)
    return pl.pallas_call(
        body,
        grid=(pairs,),
        out_shape=(
            wide_low, eight_f32, table_f32, table_f32, bc_f32, bc_eight_f32
        ),
        in_specs=scan_blocks(shared, length, wide)
        + [
            block,
            pl.BlockSpec((length, wide), lambda i: (0, gate_at // wide + i)),
            state_block,
            state_block,
            bc_block,
        ],
        out_specs=(
            pl.BlockSpec((length + EXTRA, wide), lambda i: (0, i)),
            eight,
            table,
            table,
            pl.BlockSpec((length + EXTRA, shared), lambda i: (0, 0)),
            bc_eight,
        ),
        scratch_shapes=[
            pltpu.VMEM((length, length), jnp.float32),
            pltpu.VMEM((length, length), jnp.float32),
            pltpu.VMEM((length, shared), jnp.float32),
            pltpu.VMEM((length, size), jnp.float32),
        ],
        compiler_params=pltpu.CompilerParams(vmem_limit_bytes=56 << 20),
        name="scan_back",
    )(
        first_pre, first_pre, taps, mix_pre, mix_pre, bc_taps, step_cols, sum_cols, sum_rows,
        out_grads, second_pre, state_in, end_grad, bc_low,
    )


def turned(values, cos_wide, sin_wide):
    return values * cos_wide + pltpu.roll(values, values.shape[1] // 2, 1) * sin_wide


def own_mask(at, rows, keys, limit):
    query_row = lax.broadcasted_iota(jnp.int32, (rows, keys), 0) + at
    key_row = lax.broadcasted_iota(jnp.int32, (rows, keys), 1)
    return (key_row <= query_row) & (key_row < limit)


def attention_forward(layout, second_pre, query_at, window, cos_wide, sin_wide, heads):
    length = second_pre.shape[0] - EXTRA
    part = min(ATTN_ROWS, length)
    own_at = window.shape[0] - length
    scale = HD ** (-0.5)

    def body(layout_ref, query_ref, window_ref, cos_ref, sin_ref, out_ref, turned_ref, total_ref):
        query = turned(query_ref[...], cos_ref[...], sin_ref[...]).astype(jnp.bfloat16)
        turned_ref[...] = query
        for at in range(0, length, part):
            to = at + part
            here = query[at:to]

            def scores_of(keys):
                return scale * low_dot(here, keys, 1, 1)

            keys = window_ref[own_at : own_at + to, :HD]
            values = window_ref[own_at : own_at + to, HD:]
            scores = jnp.where(
                own_mask(at, part, to, layout_ref[1]), scores_of(keys), masked_score
            )
            top = jnp.max(scores, axis=1, keepdims=True)
            shares = jnp.exp(scores - top)
            total = jnp.sum(shares, axis=1, keepdims=True)
            acc = low_dot(shares, values, 1, 0)

            def earlier(distance, carry):
                top, total, acc = carry
                start = pl.multiple_of(own_at - distance * length, length)
                scores = scores_of(window_ref[pl.ds(start, length), :HD])
                new_top = jnp.maximum(top, jnp.max(scores, axis=1, keepdims=True))
                fade = jnp.exp(top - new_top)
                shares = jnp.exp(scores - new_top)
                total = fade * total + jnp.sum(shares, axis=1, keepdims=True)
                acc = fade * acc + low_dot(shares, window_ref[pl.ds(start, length), HD:], 1, 0)
                return (new_top, total, acc)

            top, total, acc = lax.fori_loop(1, layout_ref[0] + 1, earlier, (top, total, acc))
            out_ref[at:to] = (acc / total).astype(jnp.bfloat16)
            total_ref[0, at:to] = top + jnp.log(total)

    head = pl.BlockSpec((length, HD), lambda i, layout_ref: (0, i))
    whole = pl.BlockSpec((length, HD), lambda i, layout_ref: (0, 0))
    return pl.pallas_call(
        body,
        out_shape=(
            jax.ShapeDtypeStruct((length, heads * HD), jnp.bfloat16),
            jax.ShapeDtypeStruct((length, heads * HD), jnp.bfloat16),
            jax.ShapeDtypeStruct((heads, length, 1), jnp.float32),
        ),
        grid_spec=pltpu.PrefetchScalarGridSpec(
            num_scalar_prefetch=1,
            grid=(heads,),
            in_specs=[
                pl.BlockSpec((length, HD), lambda i, layout_ref: (0, query_at // HD + i)),
                pl.BlockSpec(window.shape, lambda i, layout_ref: (0, 0)),
                whole,
                whole,
            ],
            out_specs=(
                head,
                head,
                pl.BlockSpec((1, length, 1), lambda i, layout_ref: (i, 0, 0)),
            ),
        ),
        compiler_params=pltpu.CompilerParams(vmem_limit_bytes=48 << 20),
        name="attention_forward",
    )(layout, second_pre, window, cos_wide, sin_wide)


def attention_back(layout, query, window, out, totals, mixed_grad, grad_at, cos_wide, sin_wide):
    length = query.shape[0]
    heads = query.shape[1] // HD
    part = min(ATTN_ROWS, length)
    own_at = window.shape[0] - length
    scale = HD ** (-0.5)

    def body(
        layout_ref, query_ref, window_ref, out_in_ref, total_ref, grad_ref, cos_ref, sin_ref,
        query_grad_ref, window_grad_ref, own_grad_ref, sum_ref, acc_ref,
    ):
        @pl.when(pl.program_id(0) == 0)
        def _():
            sum_ref[...] = jnp.zeros_like(sum_ref)

        for at in range(0, length, part):
            to = at + part
            here = query_ref[at:to]
            grad = grad_ref[at:to].astype(jnp.bfloat16)
            dots = jnp.sum(
                grad.astype(jnp.float32) * out_in_ref[at:to].astype(jnp.float32),
                axis=1,
                keepdims=True,
            )
            total = total_ref[0, at:to]

            def step(start, count, mask):
                keys = window_ref[pl.ds(start, count), :HD]
                values = window_ref[pl.ds(start, count), HD:]
                probs = jnp.exp(scale * low_dot(here, keys, 1, 1) - total)
                if mask is not None:
                    probs = jnp.where(mask, probs, 0.0)
                score_grad = (probs * (low_dot(grad, values, 1, 1) - dots)).astype(jnp.bfloat16)
                sum_ref[pl.ds(start, count), :HD] += low_dot(score_grad, here, 0, 0)
                sum_ref[pl.ds(start, count), HD:] += low_dot(probs, grad, 0, 0)
                return low_dot(score_grad, keys, 1, 0)

            acc_ref[...] = step(own_at, to, own_mask(at, part, to, layout_ref[1]))

            def earlier(distance, carry):
                start = pl.multiple_of(own_at - distance * length, length)
                acc_ref[...] += step(start, length, None)
                return carry

            lax.fori_loop(1, layout_ref[0] + 1, earlier, 0)
            query_grad_ref[at:to] = turned(
                acc_ref[...] * scale, cos_ref[at:to], -sin_ref[at:to]
            ).astype(jnp.bfloat16)

        @pl.when(pl.program_id(0) == heads - 1)
        def _():
            own_grad_ref[:, :HD] = sum_ref[own_at:, :HD] * scale
            own_grad_ref[:, HD:] = sum_ref[own_at:, HD:]
            window_grad_ref[:, :HD] = (sum_ref[:own_at, :HD] * scale).astype(jnp.bfloat16)
            window_grad_ref[:, HD:] = sum_ref[:own_at, HD:].astype(jnp.bfloat16)

    head = pl.BlockSpec((length, HD), lambda i, layout_ref: (0, i))
    whole = pl.BlockSpec((length, HD), lambda i, layout_ref: (0, 0))
    return pl.pallas_call(
        body,
        out_shape=(
            jax.ShapeDtypeStruct(query.shape, jnp.bfloat16),
            jax.ShapeDtypeStruct((own_at, 2 * HD), jnp.bfloat16),
            jax.ShapeDtypeStruct((length, 2 * HD), jnp.float32),
        ),
        grid_spec=pltpu.PrefetchScalarGridSpec(
            num_scalar_prefetch=1,
            grid=(heads,),
            in_specs=[
                head,
                pl.BlockSpec(window.shape, lambda i, layout_ref: (0, 0)),
                head,
                pl.BlockSpec((1, length, 1), lambda i, layout_ref: (i, 0, 0)),
                pl.BlockSpec((length, HD), lambda i, layout_ref: (0, grad_at // HD + i)),
                whole,
                whole,
            ],
            out_specs=(
                head,
                pl.BlockSpec((own_at, 2 * HD), lambda i, layout_ref: (0, 0)),
                pl.BlockSpec((length, 2 * HD), lambda i, layout_ref: (0, 0)),
            ),
            scratch_shapes=[
                pltpu.VMEM(window.shape, jnp.float32),
                pltpu.VMEM((part, HD), jnp.float32),
            ],
        ),
        compiler_params=pltpu.CompilerParams(vmem_limit_bytes=56 << 20),
        name="attention_back",
    )(layout, query, window, out, totals, mixed_grad, cos_wide, sin_wide)


def per_device(
    tokens,
    cotangent,
    mix_norm_gain,
    ssm_gate_proj,
    ssm_input_proj,
    ssm_bc_proj,
    ssm_step_proj,
    conv_in_weight,
    conv_in_bias,
    conv_bc_weight,
    conv_bc_bias,
    step_bias,
    decay_log,
    skip_gain,
    ssm_out_proj,
    query_proj,
    key_proj,
    value_proj,
    attn_out_proj,
    ffn_norm_gain,
    ffn_gate_proj,
    ffn_up_proj,
    ffn_down_proj,
    extra_blocks,
    seq_order,
    pad_rows,
):
    block_rows = tokens.shape[0]
    block_index = lax.axis_index("ctx")
    seq_count = seq_order.shape[0]
    slot_ids = jnp.arange(seq_count, dtype=jnp.int32)
    chosen = (seq_order[:, None] == slot_ids[None, :]).astype(jnp.int32)
    counts = jnp.sum(chosen * extra_blocks[None, :], axis=1) + 1
    slot_pads = jnp.sum(chosen * pad_rows[None, :], axis=1)
    slot_ends = jnp.cumsum(counts)
    starts = slot_ends - counts
    inside = (starts <= block_index) & (block_index < slot_ends)
    within = jnp.sum(jnp.where(inside, block_index - starts, 0))
    pad_here = jnp.sum(jnp.where(inside & (slot_ends - 1 == block_index), slot_pads, 0))
    row_ids = jnp.arange(block_rows, dtype=jnp.int32)
    valid_rows = (row_ids < block_rows - pad_here).astype(jnp.float32)
    positions = within * block_rows + row_ids
    keep_state = (within > 0).astype(jnp.float32)
    devices = lax.axis_size("ctx")
    codes = jnp.asarray(slot_devices(devices), jnp.int32)
    from_whole = jnp.bitwise_xor(codes, block_index)
    to_whole = jnp.argsort(from_whole).astype(jnp.int32)
    rows_here = mix_norm_gain.shape[0]
    misc_here = jnp.concatenate(
        [
            ssm_step_proj,
            mix_norm_gain[:, None],
            ffn_norm_gain[:, None],
            conv_bc_weight.reshape(rows_here, 1),
            jnp.pad(conv_bc_bias, (0, rows_here - conv_bc_bias.shape[0]))[:, None],
        ],
        axis=1,
    )
    steps = ssm_step_proj.shape[1]
    misc_here = jnp.pad(misc_here, ((0, 0), (0, 128 - misc_here.shape[1])))
    inner, shared = (ssm_input_proj.shape[1], ssm_bc_proj.shape[1])
    heads_wide, pair_wide = (query_proj.shape[1], key_proj.shape[1])
    across = [4 * k for k in range(1, devices // 4)]
    mix_here = jnp.concatenate([ssm_bc_proj, misc_here, query_proj, key_proj, value_proj], axis=1)
    out_here = jnp.concatenate([ssm_out_proj, attn_out_proj], axis=0)
    first_here = jnp.concatenate([ssm_input_proj, mix_here, ssm_gate_proj], axis=1)
    first_held = spread([([0], first_here)], 0, across)
    gate_from = inner + mix_here.shape[1]
    input_held = spread([(here, piece[:, :inner]) for here, piece in first_held], 0, [1], merge=True)
    mix_held = [(here, piece[:, inner:gate_from]) for here, piece in first_held]
    mix_held = spread(mix_held, 0, [2], merge=True)
    gate_held = [(here, piece[:, gate_from:]) for here, piece in first_held]
    near = (input_held[-1][1], mix_held[-1][1])
    input_held = spread(input_held, 0, [2])
    mix_held = spread(mix_held, 0, [1])
    ffn_here = lax.optimization_barrier((ffn_gate_proj, ffn_up_proj, ffn_down_proj, *near))[:3]
    ffn_gate_weight = lax.all_gather(ffn_here[0], "ctx", axis=0, tiled=True)
    ffn_up_weight = lax.all_gather(ffn_here[1], "ctx", axis=0, tiled=True)
    ffn_down_weight = lax.all_gather(ffn_here[2], "ctx", axis=1, tiled=True)
    out_held = spread([([0], out_here)], 1, across, near)
    input_weight = joined(input_held, 0)
    mix_weights = joined(mix_held, 0)
    misc = mix_weights[:, shared : shared + 128]
    mix_gain = misc[:, steps].astype(jnp.float32)

    def whole_order(column):
        return jnp.take(column.reshape(devices, rows_here), to_whole, axis=0)

    conv_bc_full = whole_order(misc[:, steps + 2]).reshape(shared, KW)
    conv_bc_offset = whole_order(misc[:, steps + 3])[:, : conv_bc_bias.shape[0]].reshape(shared)
    gain_two = whole_order(misc[:, steps + 1]).reshape(-1)
    inputs = tokens.astype(jnp.float32)
    rim_rows = KW - 1
    edge = shifted(tokens[block_rows - EXTRA :], "ctx", 1)
    edge_rows = jnp.arange(EXTRA, dtype=jnp.int32)[:, None] >= EXTRA - rim_rows
    edge = jnp.where(edge_rows & (within > 0), edge, jnp.zeros_like(edge))
    tokens_longer = jnp.concatenate([tokens, edge], axis=0)
    normed_low = rms_scale(
        reordered(tokens_longer, from_whole).astype(jnp.float32), mix_gain
    ).astype(jnp.bfloat16)
    first_pre = plain_product(normed_low, input_weight)
    mix_pre = plain_product(normed_low, mix_weights)
    step_raw = mix_pre[:block_rows, shared : shared + steps]
    query_at = shared + 128
    key_at = query_at + heads_wide
    key_pre = mix_pre[:block_rows, key_at : key_at + pair_wide]
    value_pre = mix_pre[:block_rows, key_at + pair_wide :]
    gate_held = spread(gate_held, 0, [2], (first_pre,), merge=True)
    out_held = spread(out_held, 1, [1], (first_pre,), merge=True)
    head_dim = inner // steps
    skips = jnp.repeat(skip_gain.astype(jnp.float32), head_dim)[None, :]
    taps = jnp.concatenate(
        [conv_in_weight.astype(jnp.float32).T, conv_in_bias.astype(jnp.float32)[None, :], skips]
    )
    taps = jnp.pad(taps, ((0, 8 - taps.shape[0]), (0, 0)))
    bc_taps = jnp.concatenate(
        [conv_bc_full.astype(jnp.float32).T, conv_bc_offset.astype(jnp.float32)[None, :]]
    )
    bc_taps = jnp.pad(bc_taps, ((0, 8 - bc_taps.shape[0]), (0, 0)))
    step_in = step_raw + step_bias.astype(jnp.float32)[None, :]
    step_size = jax.nn.softplus(step_in)
    rate = -jnp.exp(decay_log.astype(jnp.float32))[None, :]
    lower = (row_ids[:, None] >= row_ids[None, :]).astype(jnp.float32)
    log_decay = jnp.dot(lower, rate * step_size, precision=highest)

    def by_pairs(table):
        return table.reshape(block_rows, steps // 2, 2).transpose(1, 0, 2)

    def from_pairs(table):
        return table.transpose(1, 0, 2).reshape(block_rows, steps)

    step_cols = by_pairs(step_size)
    sum_cols = by_pairs(log_decay)
    sum_rows = log_decay.T.reshape(steps // 2, 2, block_rows)
    intra_out, local_states, bc_low = scan_forward(
        first_pre, mix_pre, taps, bc_taps, step_cols, sum_cols, sum_rows, inner, shared
    )
    decay_row = keep_state * jnp.repeat(jnp.exp(log_decay[block_rows - 1]), head_dim)[None, :]
    keep_low = keep_state.astype(jnp.bfloat16)
    reached, returned = carried_states(local_states, decay_row, False)
    state_in = keep_low * reached
    gate_held = spread(gate_held, 0, [1], (returned,))
    out_held = spread(out_held, 1, [2], (returned,))
    cos_table, sin_table = rotary_tables(positions)
    cos_wide = jnp.concatenate([cos_table, cos_table], axis=1)
    sin_wide = jnp.concatenate([-sin_table, sin_table], axis=1)
    key_rot = rotate(key_pre.reshape(block_rows, -1, HD), cos_table, sin_table)
    own_pair = jnp.concatenate(
        [key_rot.reshape(block_rows, HD).astype(jnp.bfloat16), value_pre.astype(jnp.bfloat16)],
        axis=1,
    )
    earlier_pairs = [shifted(own_pair, "ctx", distance) for distance in range(MAXB - 1, 0, -1)]
    window = jnp.concatenate(earlier_pairs + [own_pair], axis=0)
    layout = jnp.stack([within, block_rows - pad_here]).astype(jnp.int32)
    attn_low, query_rot, log_totals = attention_forward(
        layout, mix_pre, query_at, window, cos_wide, sin_wide, heads_wide // HD
    )
    gate_weight = joined(gate_held, 0)
    gate_pre = plain_product(normed_low, gate_weight)
    scan_out, ssm_low = scan_gated(intra_out, state_in, bc_low, sum_cols, gate_pre, 0)
    out_weights = joined(out_held, 1)
    mixed_low = jnp.concatenate([ssm_low, attn_low], axis=1)
    mixed_part = plain_product(mixed_low, out_weights)
    hidden = inputs + reordered(pair_sum(mixed_part), to_whole)
    normed_two, norm_two_back = jax.vjp(rms_scale, hidden, gain_two.astype(jnp.float32))
    normed_two_low = normed_two.astype(jnp.bfloat16)
    ffn_gate = plain_product(normed_two_low, ffn_gate_weight)
    ffn_up = plain_product(normed_two_low, ffn_up_weight)
    ffn_act = (jax.nn.silu(ffn_gate) * ffn_up).astype(jnp.bfloat16)
    ffn_part = plain_product(ffn_act, ffn_down_weight)
    ffn_sum = pair_sum(ffn_part)
    layer_out = ((hidden + ffn_sum) * valid_rows[:, None]).astype(jnp.bfloat16)
    cot_low = (cotangent.astype(jnp.float32) * valid_rows[:, None]).astype(jnp.bfloat16)
    grad_out = cot_low.astype(jnp.float32)

    def in_quarters(value):
        return jnp.split(value, 4, axis=1)

    def rows_grad(left_side, right_side, first, gates=()):
        parts = [product_of_cols(part, right_side) for part in in_quarters(left_side)]
        return Reduction(parts, 0, first, gates)

    def cols_grad(left_side, right_side, first, gates=()):
        parts = [product_of_cols(left_side, part) for part in in_quarters(right_side)]
        return Reduction(parts, 1, first, gates)

    ffn_down_grad = lax.psum_scatter(
        product_of_cols(ffn_act, cot_low).astype(jnp.bfloat16), "ctx", scatter_dimension=1, tiled=True
    )
    act_grad = product_by_rows(cot_low, ffn_down_weight)
    gate_sigmoid = jax.nn.sigmoid(ffn_gate)
    ffn_gate_low = (
        act_grad * ffn_up * gate_sigmoid * (1.0 + ffn_gate * (1.0 - gate_sigmoid))
    ).astype(jnp.bfloat16)
    ffn_up_low = (act_grad * jax.nn.silu(ffn_gate)).astype(jnp.bfloat16)
    norm_two_part = product_by_rows(ffn_gate_low, ffn_gate_weight) + product_by_rows(
        ffn_up_low, ffn_up_weight
    )
    norm_two_grad = pair_sum(norm_two_part)
    hidden_norm_grad, gain_two_grad = norm_two_back(norm_two_grad)
    hidden_grad = grad_out + hidden_norm_grad
    hidden_low = reordered(hidden_grad.astype(jnp.bfloat16), from_whole)
    mixed_grad = product_by_rows(hidden_low, out_weights)
    ssm_gate_low, state_in_grad = scan_gated_back(
        mixed_grad, scan_out, bc_low, sum_cols, gate_pre, 0
    )
    end_grad, returned = carried_states(keep_low * state_in_grad, decay_row, True)
    gate_late, up_late = lax.optimization_barrier((ffn_gate_low, ffn_up_low, ssm_gate_low))[:2]
    ffn_gate_grad = lax.psum_scatter(
        product_of_cols(normed_two_low, gate_late).astype(jnp.bfloat16),
        "ctx",
        scatter_dimension=0,
        tiled=True,
    )
    layout = after(layout, returned)
    query_grad_low, window_grad, own_pair_grad = attention_back(
        layout, query_rot, window, attn_low, log_totals, mixed_grad, inner, cos_wide, sin_wide
    )
    for distance in range(1, MAXB):
        at = (MAXB - 1 - distance) * block_rows
        own_pair_grad = own_pair_grad + shifted(
            window_grad[at : at + block_rows], "ctx", -distance
        ).astype(jnp.float32)
    up_sum = rows_grad(
        reordered(normed_two_low, from_whole), up_late, 1, (end_grad, query_grad_low)
    )
    out_sum = cols_grad(mixed_low, hidden_low, 1, (end_grad, query_grad_low))
    gate_sum = rows_grad(normed_low, ssm_gate_low, 2, (end_grad, query_grad_low))
    key_grad_low = (
        rotate(own_pair_grad[:, :HD].reshape(block_rows, 1, HD), cos_table, -sin_table)
        .reshape(block_rows, HD)
        .astype(jnp.bfloat16)
    )
    value_grad_low = own_pair_grad[:, HD:].astype(jnp.bfloat16)
    input_grad_low, tap_grad, step_part, sum_part, bc_pre_part, bc_tap_grad = scan_back(
        first_pre, mix_pre, taps, bc_taps, step_cols, sum_cols, sum_rows,
        mixed_grad, gate_pre, 0, state_in, end_grad, bc_low,
    )
    up_sum.onward(input_grad_low)
    out_sum.onward(input_grad_low)
    gate_sum.onward(input_grad_low)
    rate_grad = lax.dot_general(
        lower, from_pairs(sum_part), (((0,), (0,)), ((), ())), precision=highest
    )
    step_grad = (from_pairs(step_part) + rate * rate_grad) * jax.nn.sigmoid(step_in)
    step_grad_low = step_grad.astype(jnp.bfloat16)
    tap_sums = [
        tap_grad[:KW].T,
        tap_grad[KW],
        jnp.sum(step_grad, axis=0),
        jnp.sum(rate_grad * rate * step_size, axis=0),
        jnp.sum(tap_grad[KW + 1].reshape(steps, head_dim), axis=1),
    ]
    no_misc = jnp.zeros((block_rows, 128 - steps), jnp.bfloat16)
    mix_grads = jnp.concatenate(
        [step_grad_low, no_misc, query_grad_low, key_grad_low, value_grad_low], axis=1
    )
    mix_grads = jnp.pad(mix_grads, ((0, EXTRA), (0, 0)))
    bc_grad_low = pair_sum(bc_pre_part).astype(jnp.bfloat16)
    input_sum = rows_grad(normed_low, input_grad_low, 1)
    mix_sum = rows_grad(normed_low, jnp.concatenate([bc_grad_low, mix_grads], axis=1), 2)
    mix_grads = jnp.concatenate([bc_pre_part.astype(jnp.bfloat16), mix_grads], axis=1)
    norm_one_part = (
        product_by_rows(input_grad_low, input_weight)
        + product_by_rows(mix_grads, mix_weights)
        + product_by_rows(ssm_gate_low, gate_weight)
    )
    up_sum.last(norm_one_part)
    out_sum.last(norm_one_part)
    gate_sum.last(norm_one_part)
    input_sum.onward(norm_one_part)
    mix_sum.onward(norm_one_part)
    norm_one_grad = reordered(pair_sum(norm_one_part), to_whole)
    conv_bc_grads = jnp.concatenate([bc_tap_grad[:KW].T.reshape(-1), bc_tap_grad[KW]])
    conv_bc_grads = conv_bc_grads + swap(conv_bc_grads)
    longer = tokens_longer.astype(jnp.float32)
    scale_one = lax.rsqrt(jnp.mean(longer * longer, axis=1, keepdims=True) + epsilon)
    gain_one_grad = jnp.sum(norm_one_grad * longer * scale_one, axis=0)
    edge_back = shifted(keep_state * norm_one_grad[block_rows + EXTRA - 8 :], "ctx", -1)
    norm_one_grad = norm_one_grad[:block_rows] + jnp.pad(edge_back, ((block_rows - 8, 0), (0, 0)))
    _, norm_one_back = jax.vjp(lambda v: rms_scale(v, whole_order(mix_gain).reshape(-1)), inputs)
    tokens_grad = hidden_grad + norm_one_back(norm_one_grad)[0]
    small = [
        tap_sums[0].reshape(-1),
        *tap_sums[1:],
        conv_bc_grads,
        gain_one_grad,
        gain_two_grad,
    ]
    packed = jnp.concatenate(small)
    filled = -packed.shape[0] % 1024
    packed = summed(jnp.pad(packed, (0, filled)).reshape(-1, 128)).reshape(-1)
    sums, at = ([], 0)
    for part in small:
        sums.append(packed[at : at + part.shape[0]])
        at += part.shape[0]

    def own(vector, count):
        return lax.dynamic_slice_in_dim(vector, block_index * count, count, 0)

    input_sum.last()
    mix_sum.last()
    mix_grad = mix_sum.total()
    out_grad = out_sum.total()
    conv_bc_sums = sums[5]
    conv_rows = conv_bc_weight.shape[0]
    return (
        layer_out,
        tokens_grad.astype(jnp.bfloat16),
        own(sums[6], rows_here),
        gate_sum.total(),
        input_sum.total(),
        mix_grad[:, :shared],
        mix_grad[:, shared : shared + steps],
        sums[0].reshape(inner, KW),
        sums[1],
        own(conv_bc_sums[: shared * KW], conv_rows * KW).reshape(conv_rows, KW),
        own(conv_bc_sums[shared * KW :], conv_rows),
        sums[2],
        sums[3],
        sums[4],
        out_grad[:inner],
        mix_grad[:, query_at:key_at],
        mix_grad[:, key_at : key_at + pair_wide],
        mix_grad[:, key_at + pair_wide :],
        out_grad[inner:],
        own(sums[7], rows_here),
        ffn_gate_grad.astype(jnp.float32),
        up_sum.total(),
        ffn_down_grad.astype(jnp.float32),
    )


def solution(mesh):
    return jax.shard_map(
        per_device,
        mesh=mesh,
        in_specs=(
            P("ctx", None),
            P("ctx", None),
            P("ctx"),
            P("ctx", "wt"),
            P("ctx", "wt"),
            P("ctx", None),
            P("ctx", "wt"),
            P("wt", None),
            P("wt"),
            P("ctx", None),
            P("ctx"),
            P("wt"),
            P("wt"),
            P("wt"),
            P("wt", "ctx"),
            P("ctx", "wt"),
            P("ctx", "wt"),
            P("ctx", "wt"),
            P("wt", "ctx"),
            P("ctx"),
            P("ctx", "wt"),
            P("ctx", "wt"),
            P("wt", "ctx"),
            P(),
            P(),
            P(),
        ),
        out_specs=(
            P("ctx", None),
            P("ctx", None),
            P("ctx"),
            P("ctx", "wt"),
            P("ctx", "wt"),
            P("ctx", None),
            P("ctx", "wt"),
            P("wt", None),
            P("wt"),
            P("ctx", None),
            P("ctx"),
            P("wt"),
            P("wt"),
            P("wt"),
            P("wt", "ctx"),
            P("ctx", "wt"),
            P("ctx", "wt"),
            P("ctx", "wt"),
            P("wt", "ctx"),
            P("ctx"),
            P("ctx", "wt"),
            P("ctx", "wt"),
            P("wt", "ctx"),
        ),
        check_vma=False,
    )
```

profile of v0, /device:TPU:0, one launch (start us, length us, event | category | flops | bytes accessed | tf_op | source)
XLA Modules:
  0.0 1635.6 jit_solution(6488954477607332672)
XLA Ops:
  25.3 46.5 %collective-permute-done.1 = bf16[128,4480]{1,0:T(8,128)(2,1)S(1)} collective-permute-done((bf16[128,4480]{1,0:T(8,128)(2,1)S(1)}, bf16[128,4480]{1,0:T(8,128)(2,1)S(1)}, u32[]{:S(2)}, u32[]{:S(2)}) %collective-permute-start.1) | collective-permute-done | bytes 1146912 | tf_op jit(solution)/shard_map/ppermute | solution.py:33
  72.8 28.1 %collective-permute-done.2 = bf16[128,4480]{1,0:T(8,128)(2,1)S(1)} collective-permute-done((bf16[128,4480]{1,0:T(8,128)(2,1)S(1)}, bf16[128,4480]{1,0:T(8,128)(2,1)S(1)}, u32[]{:S(2)}, u32[]{:S(2)}) %collective-permute-start.2) | collective-permute-done | bytes 1146912 | tf_op jit(solution)/shard_map/ppermute | solution.py:33
  110.9 28.5 %collective-permute-done.5 = bf16[512,1408]{1,0:T(8,128)(2,1)} collective-permute-done((bf16[512,1408]{1,0:T(8,128)(2,1)}, bf16[512,1408]{1,0:T(8,128)(2,1)}, u32[]{:S(2)}, u32[]{:S(2)}) %collective-permute-start.5) | collective-permute-done | bytes 1441824 | tf_op jit(solution)/shard_map/ppermute | solution.py:33
  166.7 25.0 %collective-permute-start.8 = (bf16[512,1536]{1,0:T(8,128)(2,1)}, bf16[512,1536]{1,0:T(8,128)(2,1)}, u32[]{:S(2)}, u32[]{:S(2)}) collective-permute-start(bf16[512,1536]{1,0:T(8,128)(2,1)} %pad_maximum_fusion.2), channel_id=1, source_target_pairs={{0,4},{2,6},{4,0},{6,2},{8,12},{10,14},{12,8},{14,10},{16,20},{18,... | collective-permute-start | bytes 4718600 | tf_op jit(solution)/shard_map/ppermute | solution.py:33
  200.3 37.0 %collective-permute-start.32 = (bf16[2048,128]{1,0:T(8,128)(2,1)S(1)}, bf16[2048,128]{1,0:T(8,128)(2,1)S(1)}, u32[]{:S(2)}, u32[]{:S(2)}) collective-permute-start(bf16[2048,128]{1,0:T(8,128)(2,1)S(1)} %get-tuple-element.86), channel_id=1, source_target_pairs={{0,8},{2,10},{4,12},{6,14},{8,0},{10,2},{12,4},{14,6},{16,24},{18,... | collective-permute-start | bytes 1572872 | tf_op jit(solution)/shard_map/ppermute | solution.py:33
  247.5 17.0 %collective-permute-done.32 = bf16[2048,128]{1,0:T(8,128)(2,1)S(1)} collective-permute-done((bf16[2048,128]{1,0:T(8,128)(2,1)S(1)}, bf16[2048,128]{1,0:T(8,128)(2,1)S(1)}, u32[]{:S(2)}, u32[]{:S(2)}) %collective-permute-start.32) | collective-permute-done | bytes 524320 | tf_op jit(solution)/shard_map/ppermute | solution.py:33
  265.4 17.8 %collective-permute-done.33 = bf16[2048,128]{1,0:T(8,128)(2,1)S(1)} collective-permute-done((bf16[2048,128]{1,0:T(8,128)(2,1)S(1)}, bf16[2048,128]{1,0:T(8,128)(2,1)S(1)}, u32[]{:S(2)}, u32[]{:S(2)}) %collective-permute-start.33) | collective-permute-done | bytes 524320 | tf_op jit(solution)/shard_map/ppermute | solution.py:33
  284.1 7.5 collective-permute-done.34
  312.0 7.1 collective-permute-start.14
  321.9 31.1 %collective-permute-start.25 = (bf16[512,256]{1,0:T(8,128)(2,1)}, bf16[512,256]{1,0:T(8,128)(2,1)}, u32[]{:S(2)}, u32[]{:S(2)}) collective-permute-start(bf16[512,256]{1,0:T(8,128)(2,1)} %pad_maximum_fusion.7), channel_id=1, source_target_pairs={{0,14},{2,16},{4,18},{6,20},{8,22},{10,24},{12,26},{14,28},{16,30}... | collective-permute-start | bytes 786440 | tf_op jit(solution)/shard_map/ppermute | solution.py:26
  361.2 8.0 fusion.157.in_ref.rim_ref
  369.2 22.1 %scan_forward.1 = (f32[512,1536]{1,0:T(8,128)}, bf16[256,1536]{1,0:T(8,128)(2,1)S(1)}, bf16[512,512]{1,0:T(8,128)(2,1)S(1)}) custom-call(f32[528,1536]{1,0:T(8,128)} %fusion.157.in_ref.rim_ref, f32[528,1536]{1,0:T(8,128)} %fusion.157.in_ref.rim_ref, f32[8,1536]{1,0:T(8,128)S(1)} %copy-done.12, f32[528,1408]{1,0:T(8,128)S(1)} %fusion.158.bc_ref.bc_rim_ref.query_ref, ...), custom_call_target="tpu_custom_call" | custom-call | tf_op jit(solution)/shard_map/scan_forward/pallas_call | solution.py:338
  420.4 6.9 collective-permute-start.30
  428.2 5.9 collective-permute-start.31
  436.6 8.8 collective-permute-start.35
  449.8 9.0 collective-permute-done.30
  469.3 82.2 %collective-permute-done.21 = bf16[256,384]{1,0:T(8,128)(2,1)S(1)} collective-permute-done((bf16[256,384]{1,0:T(8,128)(2,1)S(1)}, bf16[256,384]{1,0:T(8,128)(2,1)S(1)}, u32[]{:S(2)}, u32[]{:S(2)}) %collective-permute-start.21) | collective-permute-done | bytes 196640 | tf_op jit(solution)/shard_map/ppermute | solution.py:33
  553.9 5.9 attention_forward.1
  569.2 10.2 collective-permute-start.37
  582.5 19.5 %collective-permute-done.24 = bf16[512,1536]{1,0:T(8,128)(2,1)S(1)} collective-permute-done((bf16[512,1536]{1,0:T(8,128)(2,1)}, bf16[512,1536]{1,0:T(8,128)(2,1)S(1)}, u32[]{:S(2)}, u32[]{:S(2)}) %collective-permute-start.24) | collective-permute-done | bytes 1572896 | tf_op jit(solution)/shard_map/ppermute | solution.py:33
  603.2 8.1 fusion.159.gate_ref
  611.3 9.4 scan_gated.1
  621.0 9.1 collective-permute-done.37
  633.3 7.0 reduce-precision_convert_fusion.2
  647.1 6.1 reordered.6
  661.9 10.7 fusion.160
  672.5 10.6 fusion.126
  683.1 14.9 multiply_convert_fusion.1
  699.3 6.9 convolution_convert_fusion
  706.3 12.3 copy.131
  718.6 7.8 fusion.161
  726.4 11.4 fusion.154
  738.1 8.2 reduce-precision_convert_fusion.1
  749.8 12.2 collective-permute-done.45
  767.0 6.3 multiply_reduce_fusion
  774.2 7.6 fusion.133
  786.5 10.7 fusion.162.grad_ref
  797.2 10.9 scan_gated_back.1
  829.4 8.1 fusion.163
  837.4 6.9 convolution_convert_fusion.1
  855.5 31.9 %collective-permute-done.44 = bf16[256,384]{1,0:T(8,128)(2,1)S(1)} collective-permute-done((bf16[256,384]{1,0:T(8,128)(2,1)S(1)}, bf16[256,384]{1,0:T(8,128)(2,1)S(1)}, u32[]{:S(2)}, u32[]{:S(2)}) %collective-permute-start.44) | collective-permute-done | bytes 196640 | tf_op jit(solution)/shard_map/ppermute | solution.py:26
  887.4 13.7 collective-permute-done.46
  905.2 10.6 attention_back.1
  930.4 59.4 %scan_back.1 = (bf16[528,1536]{1,0:T(8,128)(2,1)}, f32[8,1536]{1,0:T(8,128)}, f32[12,512,2]{2,1,0:T(8,128)}, f32[12,512,2]{2,1,0:T(8,128)}, f32[528,512]{1,0:T(8,128)}, /*index=5*/f32[8,512]{1,0:T(8,128)}) custom-call(f32[528,1536]{1,0:T(8,128)} %fusion.157.in_ref.rim_ref, f32[528,1536]{1,0:T(8,128)} %fusion.157.in_ref.rim_ref, ...), custom_call_target="tpu_custom_call" | custom-call | tf_op jit(solution)/shard_map/scan_back/pallas_call | solution.py:570
  1020.3 15.6 collective-permute-done.54
  1038.9 8.2 collective-permute-done.55
  1047.1 6.5 collective-permute-start.71
  1053.6 8.8 collective-permute-done.56
  1069.4 8.7 fusion.14
  1081.5 8.4 reduce-precision_convert_fusion
  1092.3 181.4 %collective-permute-done.71 = bf16[512,1536]{1,0:T(8,128)(2,1)} collective-permute-done((bf16[512,1536]{1,0:T(8,128)(2,1)}, bf16[512,1536]{1,0:T(8,128)(2,1)}, u32[]{:S(2)}, u32[]{:S(2)}) %collective-permute-start.71) | collective-permute-done | bytes 1572896 | tf_op jit(solution)/shard_map/ppermute | solution.py:33
  1302.7 6.2 reordered.8
  1313.6 50.2 %collective-permute-done.60 = f32[120,128]{1,0:T(8,128)S(1)} collective-permute-done((f32[120,128]{1,0:T(8,128)S(1)}, f32[120,128]{1,0:T(8,128)S(1)}, u32[]{:S(2)}, u32[]{:S(2)}) %collective-permute-start.60) | collective-permute-done | bytes 61472 | tf_op jit(solution)/shard_map/ppermute | solution.py:33
  1400.3 23.5 %collective-permute-done.66 = bf16[512,1536]{1,0:T(8,128)(2,1)} collective-permute-done((bf16[512,1536]{1,0:T(8,128)(2,1)}, bf16[512,1536]{1,0:T(8,128)(2,1)}, u32[]{:S(2)}, u32[]{:S(2)}) %collective-permute-start.66) | collective-permute-done | bytes 1572896 | tf_op jit(solution)/shard_map/ppermute | solution.py:33
  1432.0 19.0 %collective-permute-done.79 = bf16[512,1408]{1,0:T(8,128)(2,1)S(1)} collective-permute-done((bf16[512,1408]{1,0:T(8,128)(2,1)}, bf16[512,1408]{1,0:T(8,128)(2,1)S(1)}, u32[]{:S(2)}, u32[]{:S(2)}) %collective-permute-start.79) | collective-permute-done | bytes 1441824 | tf_op jit(solution)/shard_map/ppermute | solution.py:33
  1456.1 8.8 collective-permute-done.75
  1472.3 12.7 collective-permute-start.80
  1485.0 9.4 collective-permute-done.68
  1494.5 14.4 collective-permute-start.82
  1511.4 14.7 collective-permute-done.81
  1534.1 5.9 collective-permute-start.86
  1542.7 28.1 %collective-permute-done.91 = bf16[512,2048]{1,0:T(8,128)(2,1)} collective-permute-done((bf16[512,2048]{1,0:T(8,128)(2,1)}, bf16[512,2048]{1,0:T(8,128)(2,1)}, u32[]{:S(2)}, u32[]{:S(2)}) %collective-permute-start.91) | collective-permute-done | bytes 2097184 | tf_op jit(solution)/shard_map/ppermute | solution.py:33
  1580.1 9.1 collective-permute-done.92
  1589.2 33.9 %collective-permute-done.93 = bf16[128,2048]{1,0:T(8,128)(2,1)S(1)} collective-permute-done((bf16[128,2048]{1,0:T(8,128)(2,1)S(1)}, bf16[128,2048]{1,0:T(8,128)(2,1)S(1)}, u32[]{:S(2)}, u32[]{:S(2)}) %collective-permute-start.93) | collective-permute-done | bytes 524320 | tf_op jit(solution)/shard_map/ppermute | solution.py:33
  (624 shorter events, 419.3 us)
Async XLA Ops:
  7.2 654.7 %all-gather.6.cloned.1.call-start = ((), (), s32[]{:S(2)}) async-start(), calls=%async_computation.3 | async-start | bytes 8912896 | tf_op jit(solution)/shard_map/all_gather | solution.py:856
  19.6 52.2 %collective-permute-start.1 = (bf16[128,4480]{1,0:T(8,128)(2,1)S(1)}, bf16[128,4480]{1,0:T(8,128)(2,1)S(1)}, u32[]{:S(2)}, u32[]{:S(2)}) collective-permute-start(bf16[128,4480]{1,0:T(8,128)(2,1)S(1)} %get-tuple-element.373), channel_id=1, source_target_pairs={{0,8},{2,10},{4,12},{6,14},{8,0},{10,2},{12,4},{14,6},{16,24},{18,... | collective-permute-start | bytes 3440648 | tf_op jit(solution)/shard_map/ppermute | solution.py:33
  22.7 78.2 %collective-permute-start.2 = (bf16[128,4480]{1,0:T(8,128)(2,1)S(1)}, bf16[128,4480]{1,0:T(8,128)(2,1)S(1)}, u32[]{:S(2)}, u32[]{:S(2)}) collective-permute-start(bf16[128,4480]{1,0:T(8,128)(2,1)S(1)} %get-tuple-element.373), channel_id=1, source_target_pairs={{0,16},{2,18},{4,20},{6,22},{8,24},{10,26},{12,28},{14,30},{16,0},... | collective-permute-start | bytes 3440648 | tf_op jit(solution)/shard_map/ppermute | solution.py:33
  25.3 76.6 %collective-permute-start.3 = (bf16[128,4480]{1,0:T(8,128)(2,1)S(1)}, bf16[128,4480]{1,0:T(8,128)(2,1)S(1)}, u32[]{:S(2)}, u32[]{:S(2)}) collective-permute-start(bf16[128,4480]{1,0:T(8,128)(2,1)S(1)} %get-tuple-element.373), channel_id=1, source_target_pairs={{0,24},{2,26},{4,28},{6,30},{8,16},{10,18},{12,20},{14,22},{16,8},... | collective-permute-start | bytes 3440648 | tf_op jit(solution)/shard_map/ppermute | solution.py:33
  104.2 35.2 %collective-permute-start.7 = (bf16[512,1536]{1,0:T(8,128)(2,1)}, bf16[512,1536]{1,0:T(8,128)(2,1)}, u32[]{:S(2)}, u32[]{:S(2)}) collective-permute-start(bf16[512,1536]{1,0:T(8,128)(2,1)} %pad_maximum_fusion.2), channel_id=1, source_target_pairs={{0,2},{2,0},{4,6},{6,4},{8,10},{10,8},{12,14},{14,12},{16,18},{18,... | collective-permute-start | bytes 4718600 | tf_op jit(solution)/shard_map/ppermute | solution.py:33
  139.4 533.2 %all-gather.8.cloned.1.call-start = ((), (), s32[]{:S(2)}) async-start(), calls=%async_computation.4 | async-start | bytes 8912896 | tf_op jit(solution)/shard_map/all_gather | solution.py:857
  140.1 543.0 %all-gather.4.cloned.1.call-start = ((), (), s32[]{:S(2)}) async-start(), calls=%async_computation.2 | async-start | bytes 8912896 | tf_op jit(solution)/shard_map/all_gather | solution.py:855
  157.4 37.7 %collective-permute-start.4 = (bf16[512,1408]{1,0:T(8,128)(2,1)}, bf16[512,1408]{1,0:T(8,128)(2,1)}, u32[]{:S(2)}, u32[]{:S(2)}) collective-permute-start(bf16[512,1408]{1,0:T(8,128)(2,1)} %pad_maximum_fusion.5), channel_id=1, source_target_pairs={{0,2},{2,0},{4,6},{6,4},{8,10},{10,8},{12,14},{14,12},{16,18},{18,... | collective-permute-start | bytes 4325384 | tf_op jit(solution)/shard_map/ppermute | solution.py:33
  166.7 76.4 %collective-permute-start.8 = (bf16[512,1536]{1,0:T(8,128)(2,1)}, bf16[512,1536]{1,0:T(8,128)(2,1)}, u32[]{:S(2)}, u32[]{:S(2)}) collective-permute-start(bf16[512,1536]{1,0:T(8,128)(2,1)} %pad_maximum_fusion.2), channel_id=1, source_target_pairs={{0,4},{2,6},{4,0},{6,2},{8,12},{10,14},{12,8},{14,10},{16,20},{18,... | collective-permute-start | bytes 4718600 | tf_op jit(solution)/shard_map/ppermute | solution.py:33
  195.0 98.2 %collective-permute-start.6 = (bf16[512,1408]{1,0:T(8,128)(2,1)}, bf16[512,1408]{1,0:T(8,128)(2,1)}, u32[]{:S(2)}, u32[]{:S(2)}) collective-permute-start(bf16[512,1408]{1,0:T(8,128)(2,1)} %collective-permute-done.5), channel_id=1, source_target_pairs={{0,2},{2,0},{4,6},{6,4},{8,10},{10,8},{12,14},{14,12},{16,18},{18,... | collective-permute-start | bytes 4325384 | tf_op jit(solution)/shard_map/ppermute | solution.py:33
  200.3 64.2 %collective-permute-start.32 = (bf16[2048,128]{1,0:T(8,128)(2,1)S(1)}, bf16[2048,128]{1,0:T(8,128)(2,1)S(1)}, u32[]{:S(2)}, u32[]{:S(2)}) collective-permute-start(bf16[2048,128]{1,0:T(8,128)(2,1)S(1)} %get-tuple-element.86), channel_id=1, source_target_pairs={{0,8},{2,10},{4,12},{6,14},{8,0},{10,2},{12,4},{14,6},{16,24},{18,... | collective-permute-start | bytes 1572872 | tf_op jit(solution)/shard_map/ppermute | solution.py:33
  237.3 46.0 %collective-permute-start.33 = (bf16[2048,128]{1,0:T(8,128)(2,1)S(1)}, bf16[2048,128]{1,0:T(8,128)(2,1)S(1)}, u32[]{:S(2)}, u32[]{:S(2)}) collective-permute-start(bf16[2048,128]{1,0:T(8,128)(2,1)S(1)} %get-tuple-element.86), channel_id=1, source_target_pairs={{0,16},{2,18},{4,20},{6,22},{8,24},{10,26},{12,28},{14,30},{16,0},... | collective-permute-start | bytes 1572872 | tf_op jit(solution)/shard_map/ppermute | solution.py:33
  238.3 53.4 %collective-permute-start.34 = (bf16[2048,128]{1,0:T(8,128)(2,1)S(1)}, bf16[2048,128]{1,0:T(8,128)(2,1)S(1)}, u32[]{:S(2)}, u32[]{:S(2)}) collective-permute-start(bf16[2048,128]{1,0:T(8,128)(2,1)S(1)} %get-tuple-element.86), channel_id=1, source_target_pairs={{0,24},{2,26},{4,28},{6,30},{8,16},{10,18},{12,20},{14,22},{16,8},... | collective-permute-start | bytes 1572872 | tf_op jit(solution)/shard_map/ppermute | solution.py:33
  239.8 1384.7 %reduce-scatter.7.cloned.1.call-start = ((), (), s32[]{:S(2)}) async-start(), calls=%async_computation.6 | async-start | bytes 8912896
  243.0 115.5 %collective-permute-start.9 = (bf16[512,1536]{1,0:T(8,128)(2,1)}, bf16[512,1536]{1,0:T(8,128)(2,1)}, u32[]{:S(2)}, u32[]{:S(2)}) collective-permute-start(bf16[512,1536]{1,0:T(8,128)(2,1)} %collective-permute-done.7), channel_id=1, source_target_pairs={{0,4},{2,6},{4,0},{6,2},{8,12},{10,14},{12,8},{14,10},{16,20},{18,... | collective-permute-start | bytes 4718600 | tf_op jit(solution)/shard_map/ppermute | solution.py:33
  311.6 46.0 %collective-permute-start.13 = (f32[1,384]{1,0:T(1,128)}, f32[1,384]{1,0:T(1,128)}, u32[]{:S(2)}, u32[]{:S(2)}) collective-permute-start(f32[1,384]{1,0:T(1,128)} %get-tuple-element.409), channel_id=1, source_target_pairs={{0,2},{2,0},{4,6},{6,4},{8,10},{10,8},{12,14},{14,12},{16,18},{18,... | collective-permute-start | bytes 4616 | tf_op jit(solution)/shard_map/ppermute | solution.py:33
  312.0 45.6 %collective-permute-start.14 = (f32[1,384]{1,0:T(1,128)}, f32[1,384]{1,0:T(1,128)}, u32[]{:S(2)}, u32[]{:S(2)}) collective-permute-start(f32[1,384]{1,0:T(1,128)} %get-tuple-element.407), channel_id=1, source_target_pairs={{0,4},{2,6},{4,0},{6,2},{8,12},{10,14},{12,8},{14,10},{16,20},{18,... | collective-permute-start | bytes 4616 | tf_op jit(solution)/shard_map/ppermute | solution.py:33
  319.1 38.5 %collective-permute-start.15 = (f32[1,384]{1,0:T(1,128)}, f32[1,384]{1,0:T(1,128)}, u32[]{:S(2)}, u32[]{:S(2)}) collective-permute-start(f32[1,384]{1,0:T(1,128)} %get-tuple-element.408), channel_id=1, source_target_pairs={{0,6},{2,4},{4,2},{6,0},{8,14},{10,12},{12,10},{14,8},{16,22},{18,... | collective-permute-start | bytes 4616 | tf_op jit(solution)/shard_map/ppermute | solution.py:33
  321.9 90.9 %collective-permute-start.25 = (bf16[512,256]{1,0:T(8,128)(2,1)}, bf16[512,256]{1,0:T(8,128)(2,1)}, u32[]{:S(2)}, u32[]{:S(2)}) collective-permute-start(bf16[512,256]{1,0:T(8,128)(2,1)} %pad_maximum_fusion.7), channel_id=1, source_target_pairs={{0,14},{2,16},{4,18},{6,20},{8,22},{10,24},{12,26},{14,28},{16,30}... | collective-permute-start | bytes 786440 | tf_op jit(solution)/shard_map/ppermute | solution.py:26
  418.0 143.1 %collective-permute-start.23 = (bf16[512,1536]{1,0:T(8,128)(2,1)}, bf16[512,1536]{1,0:T(8,128)(2,1)}, u32[]{:S(2)}, u32[]{:S(2)}) collective-permute-start(bf16[512,1536]{1,0:T(8,128)(2,1)} %pad_maximum_fusion.3), channel_id=1, source_target_pairs={{0,4},{2,6},{4,0},{6,2},{8,12},{10,14},{12,8},{14,10},{16,20},{18,... | collective-permute-start | bytes 4718600 | tf_op jit(solution)/shard_map/ppermute | solution.py:33
  420.4 38.4 %collective-permute-start.30 = (bf16[512,256]{1,0:T(8,128)(2,1)}, bf16[512,256]{1,0:T(8,128)(2,1)S(1)}, u32[]{:S(2)}, u32[]{:S(2)}) collective-permute-start(bf16[512,256]{1,0:T(8,128)(2,1)} %pad_maximum_fusion.7), channel_id=1, source_target_pairs={{0,4},{2,6},{4,8},{6,10},{8,12},{10,14},{12,16},{14,18},{16,20},{1... | collective-permute-start | bytes 786440 | tf_op jit(solution)/shard_map/ppermute | solution.py:26
  428.2 34.0 %collective-permute-start.31 = (bf16[512,256]{1,0:T(8,128)(2,1)}, bf16[512,256]{1,0:T(8,128)(2,1)S(1)}, u32[]{:S(2)}, u32[]{:S(2)}) collective-permute-start(bf16[512,256]{1,0:T(8,128)(2,1)} %pad_maximum_fusion.7), channel_id=1, source_target_pairs={{0,2},{2,4},{4,6},{6,8},{8,10},{10,12},{12,14},{14,16},{16,18},{18... | collective-permute-start | bytes 786440 | tf_op jit(solution)/shard_map/ppermute | solution.py:26
  436.6 132.6 %collective-permute-start.35 = (bf16[2048,512]{1,0:T(8,128)(2,1)S(1)}, bf16[2048,512]{1,0:T(8,128)(2,1)S(1)}, u32[]{:S(2)}, u32[]{:S(2)}) collective-permute-start(bf16[2048,512]{1,0:T(8,128)(2,1)S(1)} %copy-done.38), channel_id=1, source_target_pairs={{0,2},{2,0},{4,6},{6,4},{8,10},{10,8},{12,14},{14,12},{16,18},{18,... | collective-permute-start | bytes 6291464 | tf_op jit(solution)/shard_map/ppermute | solution.py:33
  445.5 119.7 %collective-permute-start.22 = (bf16[512,1536]{1,0:T(8,128)(2,1)S(1)}, bf16[512,1536]{1,0:T(8,128)(2,1)S(1)}, u32[]{:S(2)}, u32[]{:S(2)}) collective-permute-start(bf16[512,1536]{1,0:T(8,128)(2,1)S(1)} %copy-done.46), channel_id=1, source_target_pairs={{0,2},{2,0},{4,6},{6,4},{8,10},{10,8},{12,14},{14,12},{16,18},{18,... | collective-permute-start | bytes 4718600 | tf_op jit(solution)/shard_map/ppermute | solution.py:33
  462.2 118.8 %collective-permute-start.36 = (bf16[2048,512]{1,0:T(8,128)(2,1)S(1)}, bf16[2048,512]{1,0:T(8,128)(2,1)S(1)}, u32[]{:S(2)}, u32[]{:S(2)}) collective-permute-start(bf16[2048,512]{1,0:T(8,128)(2,1)S(1)} %copy-done.38), channel_id=1, source_target_pairs={{0,4},{2,6},{4,0},{6,2},{8,12},{10,14},{12,8},{14,10},{16,20},{18,... | collective-permute-start | bytes 6291464 | tf_op jit(solution)/shard_map/ppermute | solution.py:33
  466.5 85.1 %collective-permute-start.21 = (bf16[256,384]{1,0:T(8,128)(2,1)S(1)}, bf16[256,384]{1,0:T(8,128)(2,1)S(1)}, u32[]{:S(2)}, u32[]{:S(2)}) collective-permute-start(bf16[256,384]{1,0:T(8,128)(2,1)S(1)} %get-tuple-element.376), channel_id=1, source_target_pairs={{0,2},{2,0},{4,6},{6,4},{8,10},{10,8},{12,14},{14,12},{16,18},{18,... | collective-permute-start | bytes 589832 | tf_op jit(solution)/shard_map/ppermute | solution.py:33
  561.1 40.8 %collective-permute-start.24 = (bf16[512,1536]{1,0:T(8,128)(2,1)}, bf16[512,1536]{1,0:T(8,128)(2,1)S(1)}, u32[]{:S(2)}, u32[]{:S(2)}) collective-permute-start(bf16[512,1536]{1,0:T(8,128)(2,1)} %collective-permute-done.23), channel_id=1, source_target_pairs={{0,2},{2,0},{4,6},{6,4},{8,10},{10,8},{12,14},{14,12},{16,18},{18,... | collective-permute-start | bytes 4718600 | tf_op jit(solution)/shard_map/ppermute | solution.py:33
  569.2 60.9 %collective-permute-start.37 = (bf16[2048,512]{1,0:T(8,128)(2,1)S(1)}, bf16[2048,512]{1,0:T(8,128)(2,1)}, u32[]{:S(2)}, u32[]{:S(2)}) collective-permute-start(bf16[2048,512]{1,0:T(8,128)(2,1)S(1)} %collective-permute-done.35), channel_id=1, source_target_pairs={{0,4},{2,6},{4,0},{6,2},{8,12},{10,14},{12,8},{14,10},{16,20},{18,... | collective-permute-start | bytes 6291464 | tf_op jit(solution)/shard_map/ppermute | solution.py:33
  718.6 908.2 %reduce-scatter.5.cloned.1.call-start = ((), (), s32[]{:S(2)}) async-start(), calls=%async_computation.5 | async-start | bytes 8912896 | tf_op jit(solution)/shard_map/reduce_scatter | solution.py:987
  808.3 39.9 %collective-permute-start.41 = (bf16[256,384]{1,0:T(8,128)(2,1)S(1)}, bf16[256,384]{1,0:T(8,128)(2,1)S(1)}, u32[]{:S(2)}, u32[]{:S(2)}) collective-permute-start(bf16[256,384]{1,0:T(8,128)(2,1)S(1)} %get-tuple-element.359), channel_id=1, source_target_pairs={{0,4},{2,6},{4,0},{6,2},{8,12},{10,14},{12,8},{14,10},{16,20},{18,... | collective-permute-start | bytes 589832 | tf_op jit(solution)/shard_map/ppermute | solution.py:33
  809.8 38.4 %collective-permute-start.42 = (bf16[256,384]{1,0:T(8,128)(2,1)S(1)}, bf16[256,384]{1,0:T(8,128)(2,1)S(1)}, u32[]{:S(2)}, u32[]{:S(2)}) collective-permute-start(bf16[256,384]{1,0:T(8,128)(2,1)S(1)} %get-tuple-element.357), channel_id=1, source_target_pairs={{0,6},{2,4},{4,2},{6,0},{8,14},{10,12},{12,10},{14,8},{16,22},{18,... | collective-permute-start | bytes 589832 | tf_op jit(solution)/shard_map/ppermute | solution.py:33
  811.8 37.1 %collective-permute-start.43 = (bf16[256,384]{1,0:T(8,128)(2,1)S(1)}, bf16[256,384]{1,0:T(8,128)(2,1)}, u32[]{:S(2)}, u32[]{:S(2)}) collective-permute-start(bf16[256,384]{1,0:T(8,128)(2,1)S(1)} %get-tuple-element.358), channel_id=1, source_target_pairs={{0,2},{2,0},{4,6},{6,4},{8,10},{10,8},{12,14},{14,12},{16,18},{18,... | collective-permute-start | bytes 589832 | tf_op jit(solution)/shard_map/ppermute | solution.py:33
  850.3 37.2 %collective-permute-start.44 = (bf16[256,384]{1,0:T(8,128)(2,1)S(1)}, bf16[256,384]{1,0:T(8,128)(2,1)S(1)}, u32[]{:S(2)}, u32[]{:S(2)}) collective-permute-start(bf16[256,384]{1,0:T(8,128)(2,1)S(1)} %get-tuple-element.282), channel_id=1, source_target_pairs={{8,0},{10,2},{12,4},{14,6},{16,8},{18,10},{20,12},{22,14},{24,16},... | collective-permute-start | bytes 589832 | tf_op jit(solution)/shard_map/ppermute | solution.py:26
  851.6 49.6 %collective-permute-start.46 = (bf16[256,384]{1,0:T(8,128)(2,1)S(1)}, bf16[256,384]{1,0:T(8,128)(2,1)S(1)}, u32[]{:S(2)}, u32[]{:S(2)}) collective-permute-start(bf16[256,384]{1,0:T(8,128)(2,1)S(1)} %get-tuple-element.282), channel_id=1, source_target_pairs={{16,0},{18,2},{20,4},{22,6},{24,8},{26,10},{28,12},{30,14},{17,1},... | collective-permute-start | bytes 589832 | tf_op jit(solution)/shard_map/ppermute | solution.py:26
  918.2 93.5 %collective-permute-start.50 = (bf16[512,256]{1,0:T(8,128)(2,1)S(1)}, bf16[512,256]{1,0:T(8,128)(2,1)}, u32[]{:S(2)}, u32[]{:S(2)}) collective-permute-start(bf16[512,256]{1,0:T(8,128)(2,1)S(1)} %get-tuple-element.317), channel_id=1, source_target_pairs={{2,0},{4,2},{6,4},{8,6},{10,8},{12,10},{14,12},{16,14},{18,16},{20... | collective-permute-start | bytes 786440 | tf_op jit(solution)/shard_map/ppermute | solution.py:26
  919.5 93.6 %collective-permute-start.51 = (bf16[512,256]{1,0:T(8,128)(2,1)S(1)}, bf16[512,256]{1,0:T(8,128)(2,1)}, u32[]{:S(2)}, u32[]{:S(2)}) collective-permute-start(bf16[512,256]{1,0:T(8,128)(2,1)S(1)} %get-tuple-element.323), channel_id=1, source_target_pairs={{4,0},{6,2},{8,4},{10,6},{12,8},{14,10},{16,12},{18,14},{20,16},{2... | collective-permute-start | bytes 786440 | tf_op jit(solution)/shard_map/ppermute | solution.py:26
  920.8 98.8 %collective-permute-start.52 = (bf16[512,256]{1,0:T(8,128)(2,1)}, bf16[512,256]{1,0:T(8,128)(2,1)}, u32[]{:S(2)}, u32[]{:S(2)}) collective-permute-start(bf16[512,256]{1,0:T(8,128)(2,1)} %get-tuple-element.322), channel_id=1, source_target_pairs={{6,0},{8,2},{10,4},{12,6},{14,8},{16,10},{18,12},{20,14},{22,16},{... | collective-permute-start | bytes 786440 | tf_op jit(solution)/shard_map/ppermute | solution.py:26
  922.2 97.9 %collective-permute-start.53 = (bf16[512,256]{1,0:T(8,128)(2,1)}, bf16[512,256]{1,0:T(8,128)(2,1)}, u32[]{:S(2)}, u32[]{:S(2)}) collective-permute-start(bf16[512,256]{1,0:T(8,128)(2,1)} %get-tuple-element.321), channel_id=1, source_target_pairs={{8,0},{10,2},{12,4},{14,6},{16,8},{18,10},{20,12},{22,14},{24,16},... | collective-permute-start | bytes 786440 | tf_op jit(solution)/shard_map/ppermute | solution.py:26
  1011.8 35.3 %collective-permute-start.55 = (bf16[512,256]{1,0:T(8,128)(2,1)}, bf16[512,256]{1,0:T(8,128)(2,1)}, u32[]{:S(2)}, u32[]{:S(2)}) collective-permute-start(bf16[512,256]{1,0:T(8,128)(2,1)} %get-tuple-element.319), channel_id=1, source_target_pairs={{12,0},{14,2},{16,4},{18,6},{20,8},{22,10},{24,12},{26,14},{28,16}... | collective-permute-start | bytes 786440 | tf_op jit(solution)/shard_map/ppermute | solution.py:26
  1013.1 49.3 %collective-permute-start.56 = (bf16[512,256]{1,0:T(8,128)(2,1)}, bf16[512,256]{1,0:T(8,128)(2,1)}, u32[]{:S(2)}, u32[]{:S(2)}) collective-permute-start(bf16[512,256]{1,0:T(8,128)(2,1)} %get-tuple-element.318), channel_id=1, source_target_pairs={{14,0},{16,2},{18,4},{20,6},{22,8},{24,10},{26,12},{28,14},{30,16}... | collective-permute-start | bytes 786440 | tf_op jit(solution)/shard_map/ppermute | solution.py:26
  1019.6 269.4 %collective-permute-start.90 = (bf16[512,2048]{1,0:T(8,128)(2,1)}, bf16[512,2048]{1,0:T(8,128)(2,1)}, u32[]{:S(2)}, u32[]{:S(2)}) collective-permute-start(bf16[512,2048]{1,0:T(8,128)(2,1)} %convolution_convert_fusion.6), channel_id=1, source_target_pairs={{0,2},{2,0},{4,6},{6,4},{8,10},{10,8},{12,14},{14,12},{16,18},{18,... | collective-permute-start | bytes 6291464 | tf_op jit(solution)/shard_map/ppermute | solution.py:33
  1020.1 49.1 %collective-permute-start.76 = (bf16[528,512]{1,0:T(8,128)(2,1)}, bf16[528,512]{1,0:T(8,128)(2,1)S(1)}, u32[]{:S(2)}, u32[]{:S(2)}) collective-permute-start(bf16[528,512]{1,0:T(8,128)(2,1)} %reduce-precision_convert_fusion.3), channel_id=1, source_target_pairs={{0,1},{1,0},{2,3},{3,2},{4,5},{5,4},{6,7},{7,6},{8,9},{9,8},{10,11... | collective-permute-start | bytes 1622024 | tf_op jit(solution)/shard_map/ppermute | solution.py:37
  1035.8 257.7 %collective-permute-start.84 = (bf16[2048,512]{1,0:T(8,128)(2,1)}, bf16[2048,512]{1,0:T(8,128)(2,1)}, u32[]{:S(2)}, u32[]{:S(2)}) collective-permute-start(bf16[2048,512]{1,0:T(8,128)(2,1)} %convolution_convert_fusion.8), channel_id=1, source_target_pairs={{0,2},{2,0},{4,6},{6,4},{8,10},{10,8},{12,14},{14,12},{16,18},{18,... | collective-permute-start | bytes 6291464 | tf_op jit(solution)/shard_map/ppermute | solution.py:33
  1047.1 226.5 %collective-permute-start.71 = (bf16[512,1536]{1,0:T(8,128)(2,1)}, bf16[512,1536]{1,0:T(8,128)(2,1)}, u32[]{:S(2)}, u32[]{:S(2)}) collective-permute-start(bf16[512,1536]{1,0:T(8,128)(2,1)} %convolution_convert_fusion.2), channel_id=1, source_target_pairs={{0,2},{2,0},{4,6},{6,4},{8,10},{10,8},{12,14},{14,12},{16,18},{18,... | collective-permute-start | bytes 4718600 | tf_op jit(solution)/shard_map/ppermute | solution.py:33
  1062.5 218.1 %collective-permute-start.65 = (bf16[512,1536]{1,0:T(8,128)(2,1)}, bf16[512,1536]{1,0:T(8,128)(2,1)}, u32[]{:S(2)}, u32[]{:S(2)}) collective-permute-start(bf16[512,1536]{1,0:T(8,128)(2,1)} %convolution_convert_fusion.4), channel_id=1, source_target_pairs={{0,4},{2,6},{4,0},{6,2},{8,12},{10,14},{12,8},{14,10},{16,20},{18,... | collective-permute-start | bytes 4718600 | tf_op jit(solution)/shard_map/ppermute | solution.py:33
  1079.4 205.1 %collective-permute-start.78 = (bf16[512,1408]{1,0:T(8,128)(2,1)S(1)}, bf16[512,1408]{1,0:T(8,128)(2,1)S(1)}, u32[]{:S(2)}, u32[]{:S(2)}) collective-permute-start(bf16[512,1408]{1,0:T(8,128)(2,1)S(1)} %convolution_convert_fusion.10), channel_id=1, source_target_pairs={{0,4},{2,6},{4,0},{6,2},{8,12},{10,14},{12,8},{14,10},{16,20},{18,... | collective-permute-start | bytes 4325384 | tf_op jit(solution)/shard_map/ppermute | solution.py:33
  1280.5 248.7 %collective-permute-start.83 = (bf16[2048,512]{1,0:T(8,128)(2,1)}, bf16[2048,512]{1,0:T(8,128)(2,1)}, u32[]{:S(2)}, u32[]{:S(2)}) collective-permute-start(bf16[2048,512]{1,0:T(8,128)(2,1)} %convolution_convert_fusion.9), channel_id=1, source_target_pairs={{0,2},{2,0},{4,6},{6,4},{8,10},{10,8},{12,14},{14,12},{16,18},{18,... | collective-permute-start | bytes 6291464 | tf_op jit(solution)/shard_map/ppermute | solution.py:33
  1284.5 109.4 %collective-permute-start.70 = (bf16[512,1536]{1,0:T(8,128)(2,1)}, bf16[512,1536]{1,0:T(8,128)(2,1)}, u32[]{:S(2)}, u32[]{:S(2)}) collective-permute-start(bf16[512,1536]{1,0:T(8,128)(2,1)} %convolution_convert_fusion.3), channel_id=1, source_target_pairs={{0,2},{2,0},{4,6},{6,4},{8,10},{10,8},{12,14},{14,12},{16,18},{18,... | collective-permute-start | bytes 4718600 | tf_op jit(solution)/shard_map/ppermute | solution.py:33
  1289.0 110.7 %collective-permute-start.64 = (bf16[512,1536]{1,0:T(8,128)(2,1)}, bf16[512,1536]{1,0:T(8,128)(2,1)}, u32[]{:S(2)}, u32[]{:S(2)}) collective-permute-start(bf16[512,1536]{1,0:T(8,128)(2,1)} %convolution_convert_fusion.5), channel_id=1, source_target_pairs={{0,4},{2,6},{4,0},{6,2},{8,12},{10,14},{12,8},{14,10},{16,20},{18,... | collective-permute-start | bytes 4718600 | tf_op jit(solution)/shard_map/ppermute | solution.py:33
  1293.6 100.8 %collective-permute-start.72 = (bf16[512,1536]{1,0:T(8,128)(2,1)}, bf16[512,1536]{1,0:T(8,128)(2,1)}, u32[]{:S(2)}, u32[]{:S(2)}) collective-permute-start(bf16[512,1536]{1,0:T(8,128)(2,1)} %add_convert_fusion.2), channel_id=1, source_target_pairs={{0,4},{2,6},{4,0},{6,2},{8,12},{10,14},{12,8},{14,10},{16,20},{18,... | collective-permute-start | bytes 4718600 | tf_op jit(solution)/shard_map/ppermute | solution.py:33
  1312.7 51.1 %collective-permute-start.60 = (f32[120,128]{1,0:T(8,128)S(1)}, f32[120,128]{1,0:T(8,128)S(1)}, u32[]{:S(2)}, u32[]{:S(2)}) collective-permute-start(f32[120,128]{1,0:T(8,128)S(1)} %pad_bitcast_fusion), channel_id=1, source_target_pairs={{0,2},{2,0},{4,6},{6,4},{8,10},{10,8},{12,14},{14,12},{16,18},{18,... | collective-permute-start | bytes 184328 | tf_op jit(solution)/shard_map/ppermute | solution.py:33
  1386.2 37.6 %collective-permute-start.66 = (bf16[512,1536]{1,0:T(8,128)(2,1)}, bf16[512,1536]{1,0:T(8,128)(2,1)}, u32[]{:S(2)}, u32[]{:S(2)}) collective-permute-start(bf16[512,1536]{1,0:T(8,128)(2,1)} %add_convert_fusion.3), channel_id=1, source_target_pairs={{0,2},{2,0},{4,6},{6,4},{8,10},{10,8},{12,14},{14,12},{16,18},{18,... | collective-permute-start | bytes 4718600 | tf_op jit(solution)/shard_map/ppermute | solution.py:33
  1393.9 35.9 %collective-permute-start.77 = (bf16[512,1408]{1,0:T(8,128)(2,1)}, bf16[512,1408]{1,0:T(8,128)(2,1)S(1)}, u32[]{:S(2)}, u32[]{:S(2)}) collective-permute-start(bf16[512,1408]{1,0:T(8,128)(2,1)} %convolution_convert_fusion.11), channel_id=1, source_target_pairs={{0,4},{2,6},{4,0},{6,2},{8,12},{10,14},{12,8},{14,10},{16,20},{18,... | collective-permute-start | bytes 4325384 | tf_op jit(solution)/shard_map/ppermute | solution.py:33
  1394.3 56.7 %collective-permute-start.79 = (bf16[512,1408]{1,0:T(8,128)(2,1)}, bf16[512,1408]{1,0:T(8,128)(2,1)S(1)}, u32[]{:S(2)}, u32[]{:S(2)}) collective-permute-start(bf16[512,1408]{1,0:T(8,128)(2,1)} %add_convert_fusion.4), channel_id=1, source_target_pairs={{0,2},{2,0},{4,6},{6,4},{8,10},{10,8},{12,14},{14,12},{16,18},{18,... | collective-permute-start | bytes 4325384 | tf_op jit(solution)/shard_map/ppermute | solution.py:33
  1399.7 129.5 %collective-permute-start.85 = (bf16[2048,512]{1,0:T(8,128)(2,1)}, bf16[2048,512]{1,0:T(8,128)(2,1)}, u32[]{:S(2)}, u32[]{:S(2)}) collective-permute-start(bf16[2048,512]{1,0:T(8,128)(2,1)} %add_convert_fusion.1), channel_id=1, source_target_pairs={{0,4},{2,6},{4,0},{6,2},{8,12},{10,14},{12,8},{14,10},{16,20},{18,... | collective-permute-start | bytes 6291464 | tf_op jit(solution)/shard_map/ppermute | solution.py:33
  1455.0 39.5 %collective-permute-start.68 = (bf16[128,1536]{1,0:T(8,128)(2,1)S(1)}, bf16[128,1536]{1,0:T(8,128)(2,1)S(1)}, u32[]{:S(2)}, u32[]{:S(2)}) collective-permute-start(bf16[128,1536]{1,0:T(8,128)(2,1)S(1)} %get-tuple-element.112), channel_id=1, source_target_pairs={{0,16},{2,18},{4,20},{6,22},{8,24},{10,26},{12,28},{14,30},{16,0},... | collective-permute-start | bytes 1179656 | tf_op jit(solution)/shard_map/ppermute | solution.py:33
  1472.3 37.6 %collective-permute-start.80 = (bf16[128,1408]{1,0:T(8,128)(2,1)S(1)}, bf16[128,1408]{1,0:T(8,128)(2,1)S(1)}, u32[]{:S(2)}, u32[]{:S(2)}) collective-permute-start(bf16[128,1408]{1,0:T(8,128)(2,1)S(1)} %get-tuple-element.330), channel_id=1, source_target_pairs={{0,8},{2,10},{4,12},{6,14},{8,0},{10,2},{12,4},{14,6},{16,24},{18,... | collective-permute-start | bytes 1081352 | tf_op jit(solution)/shard_map/ppermute | solution.py:33
  1509.9 32.7 %collective-permute-start.89 = (bf16[512,2048]{1,0:T(8,128)(2,1)}, bf16[512,2048]{1,0:T(8,128)(2,1)S(1)}, u32[]{:S(2)}, u32[]{:S(2)}) collective-permute-start(bf16[512,2048]{1,0:T(8,128)(2,1)} %convolution_convert_fusion.7), channel_id=1, source_target_pairs={{0,2},{2,0},{4,6},{6,4},{8,10},{10,8},{12,14},{14,12},{16,18},{18,... | collective-permute-start | bytes 6291464 | tf_op jit(solution)/shard_map/ppermute | solution.py:33
  1526.1 44.6 %collective-permute-start.91 = (bf16[512,2048]{1,0:T(8,128)(2,1)}, bf16[512,2048]{1,0:T(8,128)(2,1)}, u32[]{:S(2)}, u32[]{:S(2)}) collective-permute-start(bf16[512,2048]{1,0:T(8,128)(2,1)} %add_convert_fusion), channel_id=1, source_target_pairs={{0,4},{2,6},{4,0},{6,2},{8,12},{10,14},{12,8},{14,10},{16,20},{18,... | collective-permute-start | bytes 6291464 | tf_op jit(solution)/shard_map/ppermute | solution.py:33
  1534.1 42.6 %collective-permute-start.86 = (bf16[2048,128]{1,0:T(8,128)(2,1)S(1)}, bf16[2048,128]{1,0:T(8,128)(2,1)S(1)}, u32[]{:S(2)}, u32[]{:S(2)}) collective-permute-start(bf16[2048,128]{1,0:T(8,128)(2,1)S(1)} %get-tuple-element.119), channel_id=1, source_target_pairs={{0,8},{2,10},{4,12},{6,14},{8,0},{10,2},{12,4},{14,6},{16,24},{18,... | collective-permute-start | bytes 1572872 | tf_op jit(solution)/shard_map/ppermute | solution.py:33
  1540.1 38.2 %collective-permute-start.87 = (bf16[2048,128]{1,0:T(8,128)(2,1)S(1)}, bf16[2048,128]{1,0:T(8,128)(2,1)S(1)}, u32[]{:S(2)}, u32[]{:S(2)}) collective-permute-start(bf16[2048,128]{1,0:T(8,128)(2,1)S(1)} %get-tuple-element.120), channel_id=1, source_target_pairs={{0,16},{2,18},{4,20},{6,22},{8,24},{10,26},{12,28},{14,30},{16,0},... | collective-permute-start | bytes 1572872 | tf_op jit(solution)/shard_map/ppermute | solution.py:33
  1541.3 37.0 %collective-permute-start.88 = (bf16[2048,128]{1,0:T(8,128)(2,1)S(1)}, bf16[2048,128]{1,0:T(8,128)(2,1)S(1)}, u32[]{:S(2)}, u32[]{:S(2)}) collective-permute-start(bf16[2048,128]{1,0:T(8,128)(2,1)S(1)} %get-tuple-element.121), channel_id=1, source_target_pairs={{0,24},{2,26},{4,28},{6,30},{8,16},{10,18},{12,20},{14,22},{16,8},... | collective-permute-start | bytes 1572872 | tf_op jit(solution)/shard_map/ppermute | solution.py:33
  1573.8 49.4 %collective-permute-start.93 = (bf16[128,2048]{1,0:T(8,128)(2,1)S(1)}, bf16[128,2048]{1,0:T(8,128)(2,1)S(1)}, u32[]{:S(2)}, u32[]{:S(2)}) collective-permute-start(bf16[128,2048]{1,0:T(8,128)(2,1)S(1)} %get-tuple-element.128), channel_id=1, source_target_pairs={{0,16},{2,18},{4,20},{6,22},{8,24},{10,26},{12,28},{14,30},{16,0},... | collective-permute-start | bytes 1572872 | tf_op jit(solution)/shard_map/ppermute | solution.py:33
  1576.7 46.5 %collective-permute-start.94 = (bf16[128,2048]{1,0:T(8,128)(2,1)S(1)}, bf16[128,2048]{1,0:T(8,128)(2,1)S(1)}, u32[]{:S(2)}, u32[]{:S(2)}) collective-permute-start(bf16[128,2048]{1,0:T(8,128)(2,1)S(1)} %get-tuple-element.129), channel_id=1, source_target_pairs={{0,24},{2,26},{4,28},{6,30},{8,16},{10,18},{12,20},{14,22},{16,8},... | collective-permute-start | bytes 1572872 | tf_op jit(solution)/shard_map/ppermute | solution.py:33
  (147 other events, 3955.8 us)
Sparse Core Ops, SparseCore 0:
  139.5 188.6 all-gather.5
  330.9 183.5 all-gather.7
  517.3 154.8 all-gather.3
  718.7 242.3 reduce-scatter.6
  963.3 302.0 reduce-scatter.4
where the time goes:
time: 1650 us; the launch traced here: 1640 us
  waiting for transfers between devices  765 us (46%)
  starting transfers between devices  288 us (17%)
  matrix products  207 us (13%)
  Pallas kernels  145 us (9%)
  local copies, waits for them, and re-layouts  113 us (7%)
  other arithmetic  99.4 us (6%)
  between operations  17.9 us (1%)
    ppermute x67, waiting for transfers between devices, hop(): lax.ppermute(value, 'ctx', [(source, source ^ code) for source in range(c...  654 us
    ppermute x67, starting transfers between devices, hop(): lax.ppermute(value, 'ctx', [(source, source ^ code) for source in range(c...  209 us
    ppermute x22, waiting for transfers between devices, shifted(): lax.ppermute(value, axis, [(source, source + steps) for source in range(l...  106 us
    dot_general x22, matrix products, product_of_cols(): lax.dot_general(left_side, right_side, (((0,), (0,)), ((), ())), preferre...  78.1 us
    ppermute x22, starting transfers between devices, shifted(): lax.ppermute(value, axis, [(source, source + steps) for source in range(l...  77.8 us
    dot_general x7, matrix products, product_by_rows(): lax.dot_general(left_side, right_side, (((1,), (1,)), ((), ())), preferre...  65.6 us
    dot_general x7, matrix products, plain_product(): return jnp.dot(left_side, right_side, preferred_element_type=jnp.float32)  60.3 us
    pallas_call x1, Pallas kernels, scan_back(): pl.pallas_call(body, grid=(pairs,), out_shape=(wide_low, eight_f32, table...  59.4 us
  transfers between devices with their start and end apart: 100, of which 37 were waited for; matrix products, arithmetic and copies ran while one was open for 22% of the time, Pallas kernels for 9%

commit v1 on v0

--- a/solution.py
+++ b/solution.py
@@ -89,22 +89,19 @@
         self.got = [hop(part, first) for part in low]
 
     def onward(self, *gates):
-        far = self.far + self.got[1].astype(jnp.float32)
-        self.far_low = far.astype(jnp.bfloat16)
-        operand = after(self.far_low, *gates) if gates else self.far_low
-        self.near = self.near + self.got[0].astype(jnp.float32)
-        self.got = [hop(operand, self.second)]
+        got = lax.optimization_barrier((*self.got, *gates))[:2] if gates else self.got
+        self.far_low = (self.far + got[1].astype(jnp.float32)).astype(jnp.bfloat16)
+        self.near = self.near + got[0].astype(jnp.float32)
+        self.got = [hop(self.far_low, self.second)]
 
     def last(self, *gates):
         high = lax.axis_size("ctx") // 4
-        quarter = self.near + self.got[0].astype(jnp.float32)
+        got = after(self.got[0], *gates) if gates else self.got[0]
+        quarter = self.near + got.astype(jnp.float32)
         blocks = jnp.split(quarter, high, axis=self.axis)
         self.block = blocks[0]
         self.blocks_low = [block.astype(jnp.bfloat16) for block in blocks[1:]]
-        operands = self.blocks_low
-        if gates:
-            operands = lax.optimization_barrier((*operands, *gates))[: len(operands)]
-        self.got = [hop(block, 4 * (k + 1)) for k, block in enumerate(operands)]
+        self.got = [hop(block, 4 * (k + 1)) for k, block in enumerate(self.blocks_low)]
 
     def total(self):
         total = self.block
@@ -851,10 +848,8 @@
     near = (input_held[-1][1], mix_held[-1][1])
     input_held = spread(input_held, 0, [2])
     mix_held = spread(mix_held, 0, [1])
-    ffn_here = lax.optimization_barrier((ffn_gate_proj, ffn_up_proj, ffn_down_proj, *near))[:3]
-    ffn_gate_weight = lax.all_gather(ffn_here[0], "ctx", axis=0, tiled=True)
-    ffn_up_weight = lax.all_gather(ffn_here[1], "ctx", axis=0, tiled=True)
-    ffn_down_weight = lax.all_gather(ffn_here[2], "ctx", axis=1, tiled=True)
+    ffn_gate_weight = lax.all_gather(ffn_gate_proj, "ctx", axis=0, tiled=True)
+    ffn_up_weight = lax.all_gather(after(ffn_up_proj, *near), "ctx", axis=0, tiled=True)
     out_held = spread([([0], out_here)], 1, across, near)
     input_weight = joined(input_held, 0)
     mix_weights = joined(mix_held, 0)
@@ -878,6 +873,7 @@
     ).astype(jnp.bfloat16)
     first_pre = plain_product(normed_low, input_weight)
     mix_pre = plain_product(normed_low, mix_weights)
+    ffn_down_weight = lax.all_gather(after(ffn_down_proj, mix_pre), "ctx", axis=1, tiled=True)
     step_raw = mix_pre[:block_rows, shared : shared + steps]
     query_at = shared + 128
     key_at = query_at + heads_wide
@@ -962,9 +958,7 @@
         parts = [product_of_cols(left_side, part) for part in in_quarters(right_side)]
         return Reduction(parts, 1, first, gates)
 
-    ffn_down_grad = lax.psum_scatter(
-        product_of_cols(ffn_act, cot_low).astype(jnp.bfloat16), "ctx", scatter_dimension=1, tiled=True
-    )
+    down_sum = cols_grad(ffn_act, reordered(cot_low, from_whole), 1)
     act_grad = product_by_rows(cot_low, ffn_down_weight)
     gate_sigmoid = jax.nn.sigmoid(ffn_gate)
     ffn_gate_low = (
@@ -974,6 +968,12 @@
     norm_two_part = product_by_rows(ffn_gate_low, ffn_gate_weight) + product_by_rows(
         ffn_up_low, ffn_up_weight
     )
+    ffn_up_grad = lax.psum_scatter(
+        product_of_cols(normed_two_low, ffn_up_low).astype(jnp.bfloat16),
+        "ctx",
+        scatter_dimension=0,
+        tiled=True,
+    )
     norm_two_grad = pair_sum(norm_two_part)
     hidden_norm_grad, gain_two_grad = norm_two_back(norm_two_grad)
     hidden_grad = grad_out + hidden_norm_grad
@@ -983,7 +983,7 @@
         mixed_grad, scan_out, bc_low, sum_cols, gate_pre, 0
     )
     end_grad, returned = carried_states(keep_low * state_in_grad, decay_row, True)
-    gate_late, up_late = lax.optimization_barrier((ffn_gate_low, ffn_up_low, ssm_gate_low))[:2]
+    gate_late = after(ffn_gate_low, ssm_gate_low)
     ffn_gate_grad = lax.psum_scatter(
         product_of_cols(normed_two_low, gate_late).astype(jnp.bfloat16),
         "ctx",
@@ -999,9 +999,7 @@
         own_pair_grad = own_pair_grad + shifted(
             window_grad[at : at + block_rows], "ctx", -distance
         ).astype(jnp.float32)
-    up_sum = rows_grad(
-        reordered(normed_two_low, from_whole), up_late, 1, (end_grad, query_grad_low)
-    )
+    down_sum.onward(end_grad, query_grad_low)
     out_sum = cols_grad(mixed_low, hidden_low, 1, (end_grad, query_grad_low))
     gate_sum = rows_grad(normed_low, ssm_gate_low, 2, (end_grad, query_grad_low))
     key_grad_low = (
@@ -1014,9 +1012,6 @@
         first_pre, mix_pre, taps, bc_taps, step_cols, sum_cols, sum_rows,
         mixed_grad, gate_pre, 0, state_in, end_grad, bc_low,
     )
-    up_sum.onward(input_grad_low)
-    out_sum.onward(input_grad_low)
-    gate_sum.onward(input_grad_low)
     rate_grad = lax.dot_general(
         lower, from_pairs(sum_part), (((0,), (0,)), ((), ())), precision=highest
     )
@@ -1043,11 +1038,15 @@
         + product_by_rows(mix_grads, mix_weights)
         + product_by_rows(ssm_gate_low, gate_weight)
     )
-    up_sum.last(norm_one_part)
-    out_sum.last(norm_one_part)
-    gate_sum.last(norm_one_part)
-    input_sum.onward(norm_one_part)
-    mix_sum.onward(norm_one_part)
+    gate_sum.onward(norm_one_part)
+    out_sum.onward(gate_sum.far_low)
+    down_sum.last(out_sum.far_low)
+    mix_sum.onward(*down_sum.blocks_low)
+    input_sum.onward(mix_sum.far_low)
+    gate_sum.last(input_sum.far_low)
+    out_sum.last(*gate_sum.blocks_low)
+    mix_sum.last(*out_sum.blocks_low)
+    input_sum.last(*mix_sum.blocks_low)
     norm_one_grad = reordered(pair_sum(norm_one_part), to_whole)
     conv_bc_grads = jnp.concatenate([bc_tap_grad[:KW].T.reshape(-1), bc_tap_grad[KW]])
     conv_bc_grads = conv_bc_grads + swap(conv_bc_grads)
@@ -1076,8 +1075,6 @@
     def own(vector, count):
         return lax.dynamic_slice_in_dim(vector, block_index * count, count, 0)
 
-    input_sum.last()
-    mix_sum.last()
     mix_grad = mix_sum.total()
     out_grad = out_sum.total()
     conv_bc_sums = sums[5]
@@ -1104,8 +1101,8 @@
         out_grad[inner:],
         own(sums[7], rows_here),
         ffn_gate_grad.astype(jnp.float32),
-        up_sum.total(),
-        ffn_down_grad.astype(jnp.float32),
+        ffn_up_grad.astype(jnp.float32),
+        down_sum.total(),
     )
 
 

time: 1650 us -> 1710 us (1.036)
  waiting for transfers between devices: 765 us -> 835 us
    ppermute x67, waiting for transfers between devices: 654 us -> 757 us  [hop(): lax.ppermute(value, 'ctx', [(source, source ^ code) for source in range(c...]
    ppermute x22, waiting for transfers between devices: 106 us -> 74.2 us  [shifted(): lax.ppermute(value, axis, [(source, source + steps) for source in range(l...]
    unnamed x255 -> x273, local copies, waits for them, and re-layouts: 55.6 us -> 48.4 us
  transfers between devices with their start and end apart: 100 -> 100, of which waited for: 37 -> 44; matrix products, arithmetic and copies ran while one was open for 22% -> 23% of each run, Pallas kernels for 9% -> 9%
where the time goes in v1:
time: 1710 us; the launch traced here: 1690 us
  waiting for transfers between devices  835 us (49%)
  starting transfers between devices  272 us (16%)
  matrix products  201 us (12%)
  Pallas kernels  144 us (8%)
  local copies, waits for them, and re-layouts  110 us (6%)
  other arithmetic  106 us (6%)
  between operations  18.2 us (1%)
    ppermute x67, waiting for transfers between devices, hop(): lax.ppermute(value, 'ctx', [(source, source ^ code) for source in range(c...  757 us
    ppermute x67, starting transfers between devices, hop(): lax.ppermute(value, 'ctx', [(source, source ^ code) for source in range(c...  193 us
    dot_general x22, matrix products, product_of_cols(): lax.dot_general(left_side, right_side, (((0,), (0,)), ((), ())), preferre...  78.5 us
    ppermute x22, starting transfers between devices, shifted(): lax.ppermute(value, axis, [(source, source + steps) for source in range(l...  77.2 us
    ppermute x22, waiting for transfers between devices, shifted(): lax.ppermute(value, axis, [(source, source + steps) for source in range(l...  74.2 us
    dot_general x7, matrix products, product_by_rows(): lax.dot_general(left_side, right_side, (((1,), (1,)), ((), ())), preferre...  59.6 us
    pallas_call x1, Pallas kernels, scan_back(): pl.pallas_call(body, grid=(pairs,), out_shape=(wide_low, eight_f32, table...  59.6 us
    dot_general x7, matrix products, plain_product(): return jnp.dot(left_side, right_side, preferred_element_type=jnp.float32)  58.8 us
  transfers between devices with their start and end apart: 100, of which 44 were waited for; matrix products, arithmetic and copies ran while one was open for 23% of the time, Pallas kernels for 9%

profile of v1, /device:TPU:0, one launch (start us, length us, event | category | flops | bytes accessed | tf_op | source)
XLA Modules:
  0.0 1685.6 jit_solution(3247589741956050171)
XLA Ops:
  24.5 66.7 %collective-permute-done.1 = bf16[128,4480]{1,0:T(8,128)(2,1)S(1)} collective-permute-done((bf16[128,4480]{1,0:T(8,128)(2,1)S(1)}, bf16[128,4480]{1,0:T(8,128)(2,1)S(1)}, u32[]{:S(2)}, u32[]{:S(2)}) %collective-permute-start.1) | collective-permute-done | bytes 1146912 | tf_op jit(solution)/shard_map/ppermute | solution.py:33
  94.1 27.9 %collective-permute-done.3 = bf16[128,4480]{1,0:T(8,128)(2,1)S(1)} collective-permute-done((bf16[128,4480]{1,0:T(8,128)(2,1)S(1)}, bf16[128,4480]{1,0:T(8,128)(2,1)S(1)}, u32[]{:S(2)}, u32[]{:S(2)}) %collective-permute-start.3) | collective-permute-done | bytes 1146912 | tf_op jit(solution)/shard_map/ppermute | solution.py:33
  134.8 35.2 %collective-permute-done.5 = bf16[512,1408]{1,0:T(8,128)(2,1)S(1)} collective-permute-done((bf16[512,1408]{1,0:T(8,128)(2,1)}, bf16[512,1408]{1,0:T(8,128)(2,1)S(1)}, u32[]{:S(2)}, u32[]{:S(2)}) %collective-permute-start.5) | collective-permute-done | bytes 1441824 | tf_op jit(solution)/shard_map/ppermute | solution.py:33
  179.9 6.3 collective-permute-done.4
  190.0 36.8 %collective-permute-done.6 = bf16[512,1408]{1,0:T(8,128)(2,1)} collective-permute-done((bf16[512,1408]{1,0:T(8,128)(2,1)S(1)}, bf16[512,1408]{1,0:T(8,128)(2,1)}, u32[]{:S(2)}, u32[]{:S(2)}) %collective-permute-start.6) | collective-permute-done | bytes 1441824 | tf_op jit(solution)/shard_map/ppermute | solution.py:33
  232.7 5.9 fusion.155.bc_ref.bc_rim_ref.query_ref
  252.4 23.5 %collective-permute-start.8 = (bf16[512,1536]{1,0:T(8,128)(2,1)}, bf16[512,1536]{1,0:T(8,128)(2,1)}, u32[]{:S(2)}, u32[]{:S(2)}) collective-permute-start(bf16[512,1536]{1,0:T(8,128)(2,1)} %pad_maximum_fusion.2), channel_id=1, source_target_pairs={{0,4},{2,6},{4,0},{6,2},{8,12},{10,14},{12,8},{14,10},{16,20},{18,... | collective-permute-start | bytes 4718600 | tf_op jit(solution)/shard_map/ppermute | solution.py:33
  279.7 9.1 collective-permute-done.7
  288.8 22.8 %collective-permute-start.32 = (bf16[2048,128]{1,0:T(8,128)(2,1)}, bf16[2048,128]{1,0:T(8,128)(2,1)}, u32[]{:S(2)}, u32[]{:S(2)}) collective-permute-start(bf16[2048,128]{1,0:T(8,128)(2,1)} %get-tuple-element.83), channel_id=1, source_target_pairs={{0,8},{2,10},{4,12},{6,14},{8,0},{10,2},{12,4},{14,6},{16,24},{18,... | collective-permute-start | bytes 1572872 | tf_op jit(solution)/shard_map/ppermute | solution.py:33
  326.4 34.3 %collective-permute-done.32 = bf16[2048,128]{1,0:T(8,128)(2,1)} collective-permute-done((bf16[2048,128]{1,0:T(8,128)(2,1)}, bf16[2048,128]{1,0:T(8,128)(2,1)}, u32[]{:S(2)}, u32[]{:S(2)}) %collective-permute-start.32) | collective-permute-done | bytes 524320 | tf_op jit(solution)/shard_map/ppermute | solution.py:33
  391.2 29.0 %collective-permute-start.25 = (bf16[512,256]{1,0:T(8,128)(2,1)}, bf16[512,256]{1,0:T(8,128)(2,1)}, u32[]{:S(2)}, u32[]{:S(2)}) collective-permute-start(bf16[512,256]{1,0:T(8,128)(2,1)} %pad_maximum_fusion.7), channel_id=1, source_target_pairs={{0,14},{2,16},{4,18},{6,20},{8,22},{10,24},{12,26},{14,28},{16,30}... | collective-permute-start | bytes 786440 | tf_op jit(solution)/shard_map/ppermute | solution.py:26
  428.4 8.1 fusion.154.in_ref.rim_ref
  436.5 22.1 %scan_forward.1 = (f32[512,1536]{1,0:T(8,128)}, bf16[256,1536]{1,0:T(8,128)(2,1)S(1)}, bf16[512,512]{1,0:T(8,128)(2,1)S(1)}) custom-call(f32[528,1536]{1,0:T(8,128)} %fusion.154.in_ref.rim_ref, f32[528,1536]{1,0:T(8,128)} %fusion.154.in_ref.rim_ref, f32[8,1536]{1,0:T(8,128)S(1)} %copy-done.12, f32[528,1408]{1,0:T(8,128)S(1)} %fusion.155.bc_ref.bc_rim_ref.query_ref, ...), custom_call_target="tpu_custom_call" | custom-call | tf_op jit(solution)/shard_map/scan_forward/pallas_call | solution.py:335
  492.1 6.7 collective-permute-start.30
  504.3 6.0 collective-permute-start.35
  511.4 26.7 %collective-permute-done.30 = bf16[512,256]{1,0:T(8,128)(2,1)S(1)} collective-permute-done((bf16[512,256]{1,0:T(8,128)(2,1)}, bf16[512,256]{1,0:T(8,128)(2,1)S(1)}, u32[]{:S(2)}, u32[]{:S(2)}) %collective-permute-start.30) | collective-permute-done | bytes 262176 | tf_op jit(solution)/shard_map/ppermute | solution.py:26
  547.3 91.8 %collective-permute-done.21 = bf16[256,384]{1,0:T(8,128)(2,1)S(1)} collective-permute-done((bf16[256,384]{1,0:T(8,128)(2,1)S(1)}, bf16[256,384]{1,0:T(8,128)(2,1)S(1)}, u32[]{:S(2)}, u32[]{:S(2)}) %collective-permute-start.21) | collective-permute-done | bytes 196640 | tf_op jit(solution)/shard_map/ppermute | solution.py:33
  639.8 5.9 attention_forward.1
  655.5 11.5 collective-permute-start.37
  677.3 9.4 scan_gated.1
  694.2 7.1 reduce-precision_convert_fusion.2
  708.1 5.8 reordered.6
  720.5 10.5 fusion.157
  731.0 10.5 fusion.158
  741.5 14.8 multiply_convert_fusion
  757.7 6.8 convolution_convert_fusion
  773.0 9.8 collective-permute-done.45
  782.9 7.8 fusion.159
  790.7 7.3 fusion.151
  798.1 7.2 reduce-precision_convert_fusion.1
  821.7 5.8 fusion.130
  832.2 10.7 fusion.160.grad_ref
  842.9 10.5 scan_gated_back.1
  853.6 7.2 collective-permute-start.41
  876.6 7.0 convolution_convert_fusion.1
  887.5 141.2 %collective-permute-done.42 = bf16[256,384]{1,0:T(8,128)(2,1)S(1)} collective-permute-done((bf16[256,384]{1,0:T(8,128)(2,1)S(1)}, bf16[256,384]{1,0:T(8,128)(2,1)S(1)}, u32[]{:S(2)}, u32[]{:S(2)}) %collective-permute-start.42) | collective-permute-done | bytes 196640 | tf_op jit(solution)/shard_map/ppermute | solution.py:33
  1041.0 12.3 collective-permute-done.44
  1053.4 8.3 collective-permute-done.46
  1062.2 7.3 collective-permute-start.48
  1069.6 10.6 attention_back.1
  1085.1 10.2 collective-permute-done.47
  1097.7 59.6 %scan_back.1 = (bf16[528,1536]{1,0:T(8,128)(2,1)}, f32[8,1536]{1,0:T(8,128)}, f32[12,512,2]{2,1,0:T(8,128)}, f32[12,512,2]{2,1,0:T(8,128)}, f32[528,512]{1,0:T(8,128)}, /*index=5*/f32[8,512]{1,0:T(8,128)}) custom-call(f32[528,1536]{1,0:T(8,128)} %fusion.154.in_ref.rim_ref, f32[528,1536]{1,0:T(8,128)} %fusion.154.in_ref.rim_ref, ...), custom_call_target="tpu_custom_call" | custom-call | tf_op jit(solution)/shard_map/scan_back/pallas_call | solution.py:567
  1194.1 13.1 collective-permute-done.54
  1207.2 5.6 collective-permute-start.64
  1215.2 11.3 collective-permute-start.65
  1236.9 8.8 fusion.14
  1253.4 9.2 reduce-precision_convert_fusion
  1262.7 7.2 collective-permute-done.64
  1269.8 5.9 collective-permute-start.68
  1275.7 39.0 %collective-permute-done.65 = bf16[512,1536]{1,0:T(8,128)(2,1)} collective-permute-done((bf16[512,1536]{1,0:T(8,128)(2,1)}, bf16[512,1536]{1,0:T(8,128)(2,1)}, u32[]{:S(2)}, u32[]{:S(2)}) %collective-permute-start.65) | collective-permute-done | bytes 1572896 | tf_op jit(solution)/shard_map/ppermute | solution.py:33
  1321.3 39.6 %collective-permute-done.76 = bf16[2048,512]{1,0:T(8,128)(2,1)} collective-permute-done((bf16[2048,512]{1,0:T(8,128)(2,1)}, bf16[2048,512]{1,0:T(8,128)(2,1)}, u32[]{:S(2)}, u32[]{:S(2)}) %collective-permute-start.76) | collective-permute-done | bytes 2097184 | tf_op jit(solution)/shard_map/ppermute | solution.py:33
  1369.7 25.0 %collective-permute-done.71 = bf16[512,1408]{1,0:T(8,128)(2,1)} collective-permute-done((bf16[512,1408]{1,0:T(8,128)(2,1)}, bf16[512,1408]{1,0:T(8,128)(2,1)}, u32[]{:S(2)}, u32[]{:S(2)}) %collective-permute-start.71) | collective-permute-done | bytes 1441824 | tf_op jit(solution)/shard_map/ppermute | solution.py:33
  1394.7 10.2 collective-permute-start.92
  1404.9 20.6 %collective-permute-done.70 = bf16[512,1408]{1,0:T(8,128)(2,1)} collective-permute-done((bf16[512,1408]{1,0:T(8,128)(2,1)}, bf16[512,1408]{1,0:T(8,128)(2,1)}, u32[]{:S(2)}, u32[]{:S(2)}) %collective-permute-start.70) | collective-permute-done | bytes 1441824 | tf_op jit(solution)/shard_map/ppermute | solution.py:33
  1429.2 7.9 collective-permute-start.94
  1447.9 16.5 collective-permute-done.93
  1470.4 6.2 reordered.8
  1482.7 26.2 %collective-permute-done.60 = f32[120,128]{1,0:T(8,128)S(1)} collective-permute-done((f32[120,128]{1,0:T(8,128)S(1)}, f32[120,128]{1,0:T(8,128)S(1)}, u32[]{:S(2)}, u32[]{:S(2)}) %collective-permute-start.60) | collective-permute-done | bytes 61472 | tf_op jit(solution)/shard_map/ppermute | solution.py:33
  1539.4 8.2 collective-permute-done.77
  1548.1 13.7 collective-permute-done.78
  1586.6 20.7 %collective-permute-done.86 = bf16[128,1408]{1,0:T(8,128)(2,1)S(1)} collective-permute-done((bf16[128,1408]{1,0:T(8,128)(2,1)S(1)}, bf16[128,1408]{1,0:T(8,128)(2,1)S(1)}, u32[]{:S(2)}, u32[]{:S(2)}) %collective-permute-start.86) | collective-permute-done | bytes 360480 | tf_op jit(solution)/shard_map/ppermute | solution.py:33
  1608.0 15.9 collective-permute-done.87
  1624.7 5.6 collective-permute-start.85
  1636.8 31.8 %collective-permute-done.84 = bf16[128,1536]{1,0:T(8,128)(2,1)} collective-permute-done((bf16[128,1536]{1,0:T(8,128)(2,1)}, bf16[128,1536]{1,0:T(8,128)(2,1)}, u32[]{:S(2)}, u32[]{:S(2)}) %collective-permute-start.84) | collective-permute-done | bytes 393248 | tf_op jit(solution)/shard_map/ppermute | solution.py:33
  (644 shorter events, 455.1 us)
Async XLA Ops:
  7.2 713.3 %all-gather.4.cloned.1.call-start = ((), (), s32[]{:S(2)}) async-start(), calls=%async_computation.2 | async-start | bytes 8912896 | tf_op jit(solution)/shard_map/all_gather | solution.py:851
  8.0 723.1 %all-gather.8.cloned.1.call-start = ((), (), s32[]{:S(2)}) async-start(), calls=%async_computation.4 | async-start | bytes 8912896 | tf_op jit(solution)/shard_map/all_gather | solution.py:876
  18.9 72.4 %collective-permute-start.1 = (bf16[128,4480]{1,0:T(8,128)(2,1)S(1)}, bf16[128,4480]{1,0:T(8,128)(2,1)S(1)}, u32[]{:S(2)}, u32[]{:S(2)}) collective-permute-start(bf16[128,4480]{1,0:T(8,128)(2,1)S(1)} %get-tuple-element.367), channel_id=1, source_target_pairs={{0,8},{2,10},{4,12},{6,14},{8,0},{10,2},{12,4},{14,6},{16,24},{18,... | collective-permute-start | bytes 3440648 | tf_op jit(solution)/shard_map/ppermute | solution.py:33
  21.9 71.3 %collective-permute-start.2 = (bf16[128,4480]{1,0:T(8,128)(2,1)S(1)}, bf16[128,4480]{1,0:T(8,128)(2,1)S(1)}, u32[]{:S(2)}, u32[]{:S(2)}) collective-permute-start(bf16[128,4480]{1,0:T(8,128)(2,1)S(1)} %get-tuple-element.367), channel_id=1, source_target_pairs={{0,16},{2,18},{4,20},{6,22},{8,24},{10,26},{12,28},{14,30},{16,0},... | collective-permute-start | bytes 3440648 | tf_op jit(solution)/shard_map/ppermute | solution.py:33
  24.5 97.5 %collective-permute-start.3 = (bf16[128,4480]{1,0:T(8,128)(2,1)S(1)}, bf16[128,4480]{1,0:T(8,128)(2,1)S(1)}, u32[]{:S(2)}, u32[]{:S(2)}) collective-permute-start(bf16[128,4480]{1,0:T(8,128)(2,1)S(1)} %get-tuple-element.367), channel_id=1, source_target_pairs={{0,24},{2,26},{4,28},{6,30},{8,16},{10,18},{12,20},{14,22},{16,8},... | collective-permute-start | bytes 3440648 | tf_op jit(solution)/shard_map/ppermute | solution.py:33
  125.0 45.0 %collective-permute-start.5 = (bf16[512,1408]{1,0:T(8,128)(2,1)}, bf16[512,1408]{1,0:T(8,128)(2,1)S(1)}, u32[]{:S(2)}, u32[]{:S(2)}) collective-permute-start(bf16[512,1408]{1,0:T(8,128)(2,1)} %pad_maximum_fusion.5), channel_id=1, source_target_pairs={{0,4},{2,6},{4,0},{6,2},{8,12},{10,14},{12,8},{14,10},{16,20},{18,... | collective-permute-start | bytes 4325384 | tf_op jit(solution)/shard_map/ppermute | solution.py:33
  127.2 42.9 %collective-permute-start = (bf16[16,2048]{1,0:T(8,128)(2,1)}, bf16[16,2048]{1,0:T(8,128)(2,1)}, u32[]{:S(2)}, u32[]{:S(2)}) collective-permute-start(bf16[16,2048]{1,0:T(8,128)(2,1)} %slice.179), channel_id=1, source_target_pairs={{0,2},{2,4},{4,6},{6,8},{8,10},{10,12},{12,14},{14,16},{16,18},{18... | collective-permute-start | bytes 196616 | tf_op jit(solution)/shard_map/ppermute | solution.py:26
  133.5 52.6 %collective-permute-start.4 = (bf16[512,1408]{1,0:T(8,128)(2,1)}, bf16[512,1408]{1,0:T(8,128)(2,1)}, u32[]{:S(2)}, u32[]{:S(2)}) collective-permute-start(bf16[512,1408]{1,0:T(8,128)(2,1)} %pad_maximum_fusion.5), channel_id=1, source_target_pairs={{0,2},{2,0},{4,6},{6,4},{8,10},{10,8},{12,14},{14,12},{16,18},{18,... | collective-permute-start | bytes 4325384 | tf_op jit(solution)/shard_map/ppermute | solution.py:33
  170.0 56.7 %collective-permute-start.6 = (bf16[512,1408]{1,0:T(8,128)(2,1)S(1)}, bf16[512,1408]{1,0:T(8,128)(2,1)}, u32[]{:S(2)}, u32[]{:S(2)}) collective-permute-start(bf16[512,1408]{1,0:T(8,128)(2,1)S(1)} %collective-permute-done.5), channel_id=1, source_target_pairs={{0,2},{2,0},{4,6},{6,4},{8,10},{10,8},{12,14},{14,12},{16,18},{18,... | collective-permute-start | bytes 4325384 | tf_op jit(solution)/shard_map/ppermute | solution.py:33
  238.6 502.9 %all-gather.6.cloned.1.call-start = ((), (), s32[]{:S(2)}) async-start(), calls=%async_computation.3 | async-start | bytes 8912896 | tf_op jit(solution)/shard_map/all_gather | solution.py:852
  249.0 39.8 %collective-permute-start.7 = (bf16[512,1536]{1,0:T(8,128)(2,1)}, bf16[512,1536]{1,0:T(8,128)(2,1)}, u32[]{:S(2)}, u32[]{:S(2)}) collective-permute-start(bf16[512,1536]{1,0:T(8,128)(2,1)} %pad_maximum_fusion.2), channel_id=1, source_target_pairs={{0,2},{2,0},{4,6},{6,4},{8,10},{10,8},{12,14},{14,12},{16,18},{18,... | collective-permute-start | bytes 4718600 | tf_op jit(solution)/shard_map/ppermute | solution.py:33
  252.4 71.3 %collective-permute-start.8 = (bf16[512,1536]{1,0:T(8,128)(2,1)}, bf16[512,1536]{1,0:T(8,128)(2,1)}, u32[]{:S(2)}, u32[]{:S(2)}) collective-permute-start(bf16[512,1536]{1,0:T(8,128)(2,1)} %pad_maximum_fusion.2), channel_id=1, source_target_pairs={{0,4},{2,6},{4,0},{6,2},{8,12},{10,14},{12,8},{14,10},{16,20},{18,... | collective-permute-start | bytes 4718600 | tf_op jit(solution)/shard_map/ppermute | solution.py:33
  288.8 71.8 %collective-permute-start.32 = (bf16[2048,128]{1,0:T(8,128)(2,1)}, bf16[2048,128]{1,0:T(8,128)(2,1)}, u32[]{:S(2)}, u32[]{:S(2)}) collective-permute-start(bf16[2048,128]{1,0:T(8,128)(2,1)} %get-tuple-element.83), channel_id=1, source_target_pairs={{0,8},{2,10},{4,12},{6,14},{8,0},{10,2},{12,4},{14,6},{16,24},{18,... | collective-permute-start | bytes 1572872 | tf_op jit(solution)/shard_map/ppermute | solution.py:33
  311.6 51.3 %collective-permute-start.33 = (bf16[2048,128]{1,0:T(8,128)(2,1)}, bf16[2048,128]{1,0:T(8,128)(2,1)}, u32[]{:S(2)}, u32[]{:S(2)}) collective-permute-start(bf16[2048,128]{1,0:T(8,128)(2,1)} %get-tuple-element.83), channel_id=1, source_target_pairs={{0,16},{2,18},{4,20},{6,22},{8,24},{10,26},{12,28},{14,30},{16,0},... | collective-permute-start | bytes 1572872 | tf_op jit(solution)/shard_map/ppermute | solution.py:33
  313.2 53.6 %collective-permute-start.34 = (bf16[2048,128]{1,0:T(8,128)(2,1)}, bf16[2048,128]{1,0:T(8,128)(2,1)S(1)}, u32[]{:S(2)}, u32[]{:S(2)}) collective-permute-start(bf16[2048,128]{1,0:T(8,128)(2,1)} %get-tuple-element.83), channel_id=1, source_target_pairs={{0,24},{2,26},{4,28},{6,30},{8,16},{10,18},{12,20},{14,22},{16,8},... | collective-permute-start | bytes 1572872 | tf_op jit(solution)/shard_map/ppermute | solution.py:33
  314.7 1359.6 %reduce-scatter.5.cloned.1.call-start = ((), (), s32[]{:S(2)}) async-start(), calls=%async_computation.6 | async-start | bytes 8912896 | tf_op jit(solution)/shard_map/reduce_scatter | solution.py:971
  315.0 110.8 %collective-permute-start.9 = (bf16[512,1536]{1,0:T(8,128)(2,1)}, bf16[512,1536]{1,0:T(8,128)(2,1)}, u32[]{:S(2)}, u32[]{:S(2)}) collective-permute-start(bf16[512,1536]{1,0:T(8,128)(2,1)} %collective-permute-done.7), channel_id=1, source_target_pairs={{0,4},{2,6},{4,0},{6,2},{8,12},{10,14},{12,8},{14,10},{16,20},{18,... | collective-permute-start | bytes 4718600 | tf_op jit(solution)/shard_map/ppermute | solution.py:33
  384.2 40.7 %collective-permute-start.13 = (f32[1,384]{1,0:T(1,128)}, f32[1,384]{1,0:T(1,128)}, u32[]{:S(2)}, u32[]{:S(2)}) collective-permute-start(f32[1,384]{1,0:T(1,128)} %get-tuple-element.403), channel_id=1, source_target_pairs={{0,2},{2,0},{4,6},{6,4},{8,10},{10,8},{12,14},{14,12},{16,18},{18,... | collective-permute-start | bytes 4616 | tf_op jit(solution)/shard_map/ppermute | solution.py:33
  384.9 39.9 %collective-permute-start.14 = (f32[1,384]{1,0:T(1,128)}, f32[1,384]{1,0:T(1,128)}, u32[]{:S(2)}, u32[]{:S(2)}) collective-permute-start(f32[1,384]{1,0:T(1,128)} %get-tuple-element.401), channel_id=1, source_target_pairs={{0,4},{2,6},{4,0},{6,2},{8,12},{10,14},{12,8},{14,10},{16,20},{18,... | collective-permute-start | bytes 4616 | tf_op jit(solution)/shard_map/ppermute | solution.py:33
  387.2 37.7 %collective-permute-start.15 = (f32[1,384]{1,0:T(1,128)}, f32[1,384]{1,0:T(1,128)}, u32[]{:S(2)}, u32[]{:S(2)}) collective-permute-start(f32[1,384]{1,0:T(1,128)} %get-tuple-element.402), channel_id=1, source_target_pairs={{0,6},{2,4},{4,2},{6,0},{8,14},{10,12},{12,10},{14,8},{16,22},{18,... | collective-permute-start | bytes 4616 | tf_op jit(solution)/shard_map/ppermute | solution.py:33
  391.2 93.9 %collective-permute-start.25 = (bf16[512,256]{1,0:T(8,128)(2,1)}, bf16[512,256]{1,0:T(8,128)(2,1)}, u32[]{:S(2)}, u32[]{:S(2)}) collective-permute-start(bf16[512,256]{1,0:T(8,128)(2,1)} %pad_maximum_fusion.7), channel_id=1, source_target_pairs={{0,14},{2,16},{4,18},{6,20},{8,22},{10,24},{12,26},{14,28},{16,30}... | collective-permute-start | bytes 786440 | tf_op jit(solution)/shard_map/ppermute | solution.py:26
  489.8 157.8 %collective-permute-start.23 = (bf16[512,1536]{1,0:T(8,128)(2,1)}, bf16[512,1536]{1,0:T(8,128)(2,1)}, u32[]{:S(2)}, u32[]{:S(2)}) collective-permute-start(bf16[512,1536]{1,0:T(8,128)(2,1)} %pad_maximum_fusion.3), channel_id=1, source_target_pairs={{0,4},{2,6},{4,0},{6,2},{8,12},{10,14},{12,8},{14,10},{16,20},{18,... | collective-permute-start | bytes 4718600 | tf_op jit(solution)/shard_map/ppermute | solution.py:33
  492.1 46.0 %collective-permute-start.30 = (bf16[512,256]{1,0:T(8,128)(2,1)}, bf16[512,256]{1,0:T(8,128)(2,1)S(1)}, u32[]{:S(2)}, u32[]{:S(2)}) collective-permute-start(bf16[512,256]{1,0:T(8,128)(2,1)} %pad_maximum_fusion.7), channel_id=1, source_target_pairs={{0,4},{2,6},{4,8},{6,10},{8,12},{10,14},{12,16},{14,18},{16,20},{1... | collective-permute-start | bytes 786440 | tf_op jit(solution)/shard_map/ppermute | solution.py:26
  499.8 41.6 %collective-permute-start.31 = (bf16[512,256]{1,0:T(8,128)(2,1)}, bf16[512,256]{1,0:T(8,128)(2,1)S(1)}, u32[]{:S(2)}, u32[]{:S(2)}) collective-permute-start(bf16[512,256]{1,0:T(8,128)(2,1)} %pad_maximum_fusion.7), channel_id=1, source_target_pairs={{0,2},{2,4},{4,6},{6,8},{8,10},{10,12},{12,14},{14,16},{16,18},{18... | collective-permute-start | bytes 786440 | tf_op jit(solution)/shard_map/ppermute | solution.py:26
  504.3 151.2 %collective-permute-start.35 = (bf16[2048,512]{1,0:T(8,128)(2,1)S(1)}, bf16[2048,512]{1,0:T(8,128)(2,1)S(1)}, u32[]{:S(2)}, u32[]{:S(2)}) collective-permute-start(bf16[2048,512]{1,0:T(8,128)(2,1)S(1)} %copy-done.42), channel_id=1, source_target_pairs={{0,2},{2,0},{4,6},{6,4},{8,10},{10,8},{12,14},{14,12},{16,18},{18,... | collective-permute-start | bytes 6291464 | tf_op jit(solution)/shard_map/ppermute | solution.py:33
  510.3 141.1 %collective-permute-start.22 = (bf16[512,1536]{1,0:T(8,128)(2,1)S(1)}, bf16[512,1536]{1,0:T(8,128)(2,1)S(1)}, u32[]{:S(2)}, u32[]{:S(2)}) collective-permute-start(bf16[512,1536]{1,0:T(8,128)(2,1)S(1)} %copy-done.50), channel_id=1, source_target_pairs={{0,2},{2,0},{4,6},{6,4},{8,10},{10,8},{12,14},{14,12},{16,18},{18,... | collective-permute-start | bytes 4718600 | tf_op jit(solution)/shard_map/ppermute | solution.py:33
  541.5 127.0 %collective-permute-start.36 = (bf16[2048,512]{1,0:T(8,128)(2,1)S(1)}, bf16[2048,512]{1,0:T(8,128)(2,1)S(1)}, u32[]{:S(2)}, u32[]{:S(2)}) collective-permute-start(bf16[2048,512]{1,0:T(8,128)(2,1)S(1)} %copy-done.42), channel_id=1, source_target_pairs={{0,4},{2,6},{4,0},{6,2},{8,12},{10,14},{12,8},{14,10},{16,20},{18,... | collective-permute-start | bytes 6291464 | tf_op jit(solution)/shard_map/ppermute | solution.py:33
  545.8 93.3 %collective-permute-start.21 = (bf16[256,384]{1,0:T(8,128)(2,1)S(1)}, bf16[256,384]{1,0:T(8,128)(2,1)S(1)}, u32[]{:S(2)}, u32[]{:S(2)}) collective-permute-start(bf16[256,384]{1,0:T(8,128)(2,1)S(1)} %get-tuple-element.370), channel_id=1, source_target_pairs={{0,2},{2,0},{4,6},{6,4},{8,10},{10,8},{12,14},{14,12},{16,18},{18,... | collective-permute-start | bytes 589832 | tf_op jit(solution)/shard_map/ppermute | solution.py:33
  655.5 35.6 %collective-permute-start.37 = (bf16[2048,512]{1,0:T(8,128)(2,1)S(1)}, bf16[2048,512]{1,0:T(8,128)(2,1)}, u32[]{:S(2)}, u32[]{:S(2)}) collective-permute-start(bf16[2048,512]{1,0:T(8,128)(2,1)S(1)} %collective-permute-done.35), channel_id=1, source_target_pairs={{0,4},{2,6},{4,0},{6,2},{8,12},{10,14},{12,8},{14,10},{16,20},{18,... | collective-permute-start | bytes 6291464 | tf_op jit(solution)/shard_map/ppermute | solution.py:33
  764.5 911.9 %reduce-scatter.3.cloned.1.call-start = ((), (), s32[]{:S(2)}) async-start(), calls=%async_computation.5 | async-start | bytes 8912896 | tf_op jit(solution)/shard_map/reduce_scatter | solution.py:987
  808.4 358.4 %collective-permute-start.72 = (bf16[2048,512]{1,0:T(8,128)(2,1)}, bf16[2048,512]{1,0:T(8,128)(2,1)}, u32[]{:S(2)}, u32[]{:S(2)}) collective-permute-start(bf16[2048,512]{1,0:T(8,128)(2,1)} %convolution_convert_fusion.9), channel_id=1, source_target_pairs={{0,2},{2,0},{4,6},{6,4},{8,10},{10,8},{12,14},{14,12},{16,18},{18,... | collective-permute-start | bytes 6291464 | tf_op jit(solution)/shard_map/ppermute | solution.py:33
  811.3 356.9 %collective-permute-start.73 = (bf16[2048,512]{1,0:T(8,128)(2,1)}, bf16[2048,512]{1,0:T(8,128)(2,1)}, u32[]{:S(2)}, u32[]{:S(2)}) collective-permute-start(bf16[2048,512]{1,0:T(8,128)(2,1)} %convolution_convert_fusion.8), channel_id=1, source_target_pairs={{0,2},{2,0},{4,6},{6,4},{8,10},{10,8},{12,14},{14,12},{16,18},{18,... | collective-permute-start | bytes 6291464 | tf_op jit(solution)/shard_map/ppermute | solution.py:33
  853.6 33.9 %collective-permute-start.41 = (bf16[256,384]{1,0:T(8,128)(2,1)S(1)}, bf16[256,384]{1,0:T(8,128)(2,1)S(1)}, u32[]{:S(2)}, u32[]{:S(2)}) collective-permute-start(bf16[256,384]{1,0:T(8,128)(2,1)S(1)} %get-tuple-element.353), channel_id=1, source_target_pairs={{0,4},{2,6},{4,0},{6,2},{8,12},{10,14},{12,8},{14,10},{16,20},{18,... | collective-permute-start | bytes 589832 | tf_op jit(solution)/shard_map/ppermute | solution.py:33
  860.7 167.9 %collective-permute-start.42 = (bf16[256,384]{1,0:T(8,128)(2,1)S(1)}, bf16[256,384]{1,0:T(8,128)(2,1)S(1)}, u32[]{:S(2)}, u32[]{:S(2)}) collective-permute-start(bf16[256,384]{1,0:T(8,128)(2,1)S(1)} %get-tuple-element.351), channel_id=1, source_target_pairs={{0,6},{2,4},{4,2},{6,0},{8,14},{10,12},{12,10},{14,8},{16,22},{18,... | collective-permute-start | bytes 589832 | tf_op jit(solution)/shard_map/ppermute | solution.py:33
  862.3 172.2 %collective-permute-start.43 = (bf16[256,384]{1,0:T(8,128)(2,1)S(1)}, bf16[256,384]{1,0:T(8,128)(2,1)}, u32[]{:S(2)}, u32[]{:S(2)}) collective-permute-start(bf16[256,384]{1,0:T(8,128)(2,1)S(1)} %get-tuple-element.352), channel_id=1, source_target_pairs={{0,2},{2,0},{4,6},{6,4},{8,10},{10,8},{12,14},{14,12},{16,18},{18,... | collective-permute-start | bytes 589832 | tf_op jit(solution)/shard_map/ppermute | solution.py:33
  1082.5 103.6 %collective-permute-start.50 = (bf16[512,256]{1,0:T(8,128)(2,1)S(1)}, bf16[512,256]{1,0:T(8,128)(2,1)}, u32[]{:S(2)}, u32[]{:S(2)}) collective-permute-start(bf16[512,256]{1,0:T(8,128)(2,1)S(1)} %get-tuple-element.311), channel_id=1, source_target_pairs={{2,0},{4,2},{6,4},{8,6},{10,8},{12,10},{14,12},{16,14},{18,16},{20... | collective-permute-start | bytes 786440 | tf_op jit(solution)/shard_map/ppermute | solution.py:26
  1083.8 103.6 %collective-permute-start.51 = (bf16[512,256]{1,0:T(8,128)(2,1)S(1)}, bf16[512,256]{1,0:T(8,128)(2,1)}, u32[]{:S(2)}, u32[]{:S(2)}) collective-permute-start(bf16[512,256]{1,0:T(8,128)(2,1)S(1)} %get-tuple-element.317), channel_id=1, source_target_pairs={{4,0},{6,2},{8,4},{10,6},{12,8},{14,10},{16,12},{18,14},{20,16},{2... | collective-permute-start | bytes 786440 | tf_op jit(solution)/shard_map/ppermute | solution.py:26
  1095.3 96.6 %collective-permute-start.52 = (bf16[512,256]{1,0:T(8,128)(2,1)}, bf16[512,256]{1,0:T(8,128)(2,1)}, u32[]{:S(2)}, u32[]{:S(2)}) collective-permute-start(bf16[512,256]{1,0:T(8,128)(2,1)} %get-tuple-element.316), channel_id=1, source_target_pairs={{6,0},{8,2},{10,4},{12,6},{14,8},{16,10},{18,12},{20,14},{22,16},{... | collective-permute-start | bytes 786440 | tf_op jit(solution)/shard_map/ppermute | solution.py:26
  1187.4 39.5 %collective-permute-start.56 = (bf16[512,256]{1,0:T(8,128)(2,1)S(1)}, bf16[512,256]{1,0:T(8,128)(2,1)}, u32[]{:S(2)}, u32[]{:S(2)}) collective-permute-start(bf16[512,256]{1,0:T(8,128)(2,1)S(1)} %get-tuple-element.312), channel_id=1, source_target_pairs={{14,0},{16,2},{18,4},{20,6},{22,8},{24,10},{26,12},{28,14},{30,16}... | collective-permute-start | bytes 786440 | tf_op jit(solution)/shard_map/ppermute | solution.py:26
  1192.0 127.0 %collective-permute-start.75 = (bf16[2048,512]{1,0:T(8,128)(2,1)}, bf16[2048,512]{1,0:T(8,128)(2,1)}, u32[]{:S(2)}, u32[]{:S(2)}) collective-permute-start(bf16[2048,512]{1,0:T(8,128)(2,1)} %convolution_convert_fusion.7), channel_id=1, source_target_pairs={{0,2},{2,0},{4,6},{6,4},{8,10},{10,8},{12,14},{14,12},{16,18},{18,... | collective-permute-start | bytes 6291464 | tf_op jit(solution)/shard_map/ppermute | solution.py:33
  1192.1 168.8 %collective-permute-start.76 = (bf16[2048,512]{1,0:T(8,128)(2,1)}, bf16[2048,512]{1,0:T(8,128)(2,1)}, u32[]{:S(2)}, u32[]{:S(2)}) collective-permute-start(bf16[2048,512]{1,0:T(8,128)(2,1)} %convolution_convert_fusion.6), channel_id=1, source_target_pairs={{0,2},{2,0},{4,6},{6,4},{8,10},{10,8},{12,14},{14,12},{16,18},{18,... | collective-permute-start | bytes 6291464 | tf_op jit(solution)/shard_map/ppermute | solution.py:33
  1207.2 62.6 %collective-permute-start.64 = (bf16[512,1536]{1,0:T(8,128)(2,1)}, bf16[512,1536]{1,0:T(8,128)(2,1)}, u32[]{:S(2)}, u32[]{:S(2)}) collective-permute-start(bf16[512,1536]{1,0:T(8,128)(2,1)} %convolution_convert_fusion.5), channel_id=1, source_target_pairs={{0,4},{2,6},{4,0},{6,2},{8,12},{10,14},{12,8},{14,10},{16,20},{18,... | collective-permute-start | bytes 4718600 | tf_op jit(solution)/shard_map/ppermute | solution.py:33
  1215.2 99.5 %collective-permute-start.65 = (bf16[512,1536]{1,0:T(8,128)(2,1)}, bf16[512,1536]{1,0:T(8,128)(2,1)}, u32[]{:S(2)}, u32[]{:S(2)}) collective-permute-start(bf16[512,1536]{1,0:T(8,128)(2,1)} %convolution_convert_fusion.4), channel_id=1, source_target_pairs={{0,4},{2,6},{4,0},{6,2},{8,12},{10,14},{12,8},{14,10},{16,20},{18,... | collective-permute-start | bytes 4718600 | tf_op jit(solution)/shard_map/ppermute | solution.py:33
  1233.7 133.1 %collective-permute-start.74 = (bf16[2048,512]{1,0:T(8,128)(2,1)}, bf16[2048,512]{1,0:T(8,128)(2,1)S(1)}, u32[]{:S(2)}, u32[]{:S(2)}) collective-permute-start(bf16[2048,512]{1,0:T(8,128)(2,1)} %add_convert_fusion.1), channel_id=1, source_target_pairs={{0,4},{2,6},{4,0},{6,2},{8,12},{10,14},{12,8},{14,10},{16,20},{18,... | collective-permute-start | bytes 6291464 | tf_op jit(solution)/shard_map/ppermute | solution.py:33
  1269.8 159.4 %collective-permute-start.68 = (bf16[512,1536]{1,0:T(8,128)(2,1)}, bf16[512,1536]{1,0:T(8,128)(2,1)}, u32[]{:S(2)}, u32[]{:S(2)}) collective-permute-start(bf16[512,1536]{1,0:T(8,128)(2,1)} %convolution_convert_fusion.2), channel_id=1, source_target_pairs={{0,2},{2,0},{4,6},{6,4},{8,10},{10,8},{12,14},{14,12},{16,18},{18,... | collective-permute-start | bytes 4718600 | tf_op jit(solution)/shard_map/ppermute | solution.py:33
  1314.8 126.2 %collective-permute-start.67 = (bf16[512,1536]{1,0:T(8,128)(2,1)}, bf16[512,1536]{1,0:T(8,128)(2,1)S(1)}, u32[]{:S(2)}, u32[]{:S(2)}) collective-permute-start(bf16[512,1536]{1,0:T(8,128)(2,1)} %convolution_convert_fusion.3), channel_id=1, source_target_pairs={{0,2},{2,0},{4,6},{6,4},{8,10},{10,8},{12,14},{14,12},{16,18},{18,... | collective-permute-start | bytes 4718600 | tf_op jit(solution)/shard_map/ppermute | solution.py:33
  1318.9 75.7 %collective-permute-start.71 = (bf16[512,1408]{1,0:T(8,128)(2,1)}, bf16[512,1408]{1,0:T(8,128)(2,1)}, u32[]{:S(2)}, u32[]{:S(2)}) collective-permute-start(bf16[512,1408]{1,0:T(8,128)(2,1)} %convolution_convert_fusion.10), channel_id=1, source_target_pairs={{0,4},{2,6},{4,0},{6,2},{8,12},{10,14},{12,8},{14,10},{16,20},{18,... | collective-permute-start | bytes 4325384 | tf_op jit(solution)/shard_map/ppermute | solution.py:33
  1360.8 64.6 %collective-permute-start.70 = (bf16[512,1408]{1,0:T(8,128)(2,1)}, bf16[512,1408]{1,0:T(8,128)(2,1)}, u32[]{:S(2)}, u32[]{:S(2)}) collective-permute-start(bf16[512,1408]{1,0:T(8,128)(2,1)} %convolution_convert_fusion.11), channel_id=1, source_target_pairs={{0,4},{2,6},{4,0},{6,2},{8,12},{10,14},{12,8},{14,10},{16,20},{18,... | collective-permute-start | bytes 4325384 | tf_op jit(solution)/shard_map/ppermute | solution.py:33
  1366.8 100.6 %collective-permute-start.57 = (bf16[528,2048]{1,0:T(8,128)(2,1)}, bf16[528,2048]{1,0:T(8,128)(2,1)S(1)}, u32[]{:S(2)}, u32[]{:S(2)}) collective-permute-start(bf16[528,2048]{1,0:T(8,128)(2,1)} %get-tuple-element.422), channel_id=1, source_target_pairs={{0,1},{1,0},{2,3},{3,2},{4,5},{5,4},{6,7},{7,6},{8,9},{9,8},{10,11... | collective-permute-start | bytes 6488072 | tf_op jit(solution)/shard_map/ppermute | solution.py:37
  1394.7 50.8 %collective-permute-start.92 = (bf16[2048,128]{1,0:T(8,128)(2,1)S(1)}, bf16[2048,128]{1,0:T(8,128)(2,1)S(1)}, u32[]{:S(2)}, u32[]{:S(2)}) collective-permute-start(bf16[2048,128]{1,0:T(8,128)(2,1)S(1)} %get-tuple-element.310), channel_id=1, source_target_pairs={{0,8},{2,10},{4,12},{6,14},{8,0},{10,2},{12,4},{14,6},{16,24},{18,... | collective-permute-start | bytes 1572872 | tf_op jit(solution)/shard_map/ppermute | solution.py:33
  1425.5 39.0 %collective-permute-start.93 = (bf16[2048,128]{1,0:T(8,128)(2,1)S(1)}, bf16[2048,128]{1,0:T(8,128)(2,1)S(1)}, u32[]{:S(2)}, u32[]{:S(2)}) collective-permute-start(bf16[2048,128]{1,0:T(8,128)(2,1)S(1)} %get-tuple-element.309), channel_id=1, source_target_pairs={{0,16},{2,18},{4,20},{6,22},{8,24},{10,26},{12,28},{14,30},{16,0},... | collective-permute-start | bytes 1572872 | tf_op jit(solution)/shard_map/ppermute | solution.py:33
  1429.2 37.0 %collective-permute-start.94 = (bf16[2048,128]{1,0:T(8,128)(2,1)S(1)}, bf16[2048,128]{1,0:T(8,128)(2,1)S(1)}, u32[]{:S(2)}, u32[]{:S(2)}) collective-permute-start(bf16[2048,128]{1,0:T(8,128)(2,1)S(1)} %get-tuple-element.308), channel_id=1, source_target_pairs={{0,24},{2,26},{4,28},{6,30},{8,16},{10,18},{12,20},{14,22},{16,8},... | collective-permute-start | bytes 1572872 | tf_op jit(solution)/shard_map/ppermute | solution.py:33
  1440.9 88.9 %collective-permute-start.66 = (bf16[512,1536]{1,0:T(8,128)(2,1)}, bf16[512,1536]{1,0:T(8,128)(2,1)}, u32[]{:S(2)}, u32[]{:S(2)}) collective-permute-start(bf16[512,1536]{1,0:T(8,128)(2,1)} %add_convert_fusion.3), channel_id=1, source_target_pairs={{0,2},{2,0},{4,6},{6,4},{8,10},{10,8},{12,14},{14,12},{16,18},{18,... | collective-permute-start | bytes 4718600 | tf_op jit(solution)/shard_map/ppermute | solution.py:33
  1445.5 117.4 %collective-permute-start.82 = (bf16[2048,512]{1,0:T(8,128)(2,1)}, bf16[2048,512]{1,0:T(8,128)(2,1)}, u32[]{:S(2)}, u32[]{:S(2)}) collective-permute-start(bf16[2048,512]{1,0:T(8,128)(2,1)} %add_convert_fusion), channel_id=1, source_target_pairs={{0,4},{2,6},{4,0},{6,2},{8,12},{10,14},{12,8},{14,10},{16,20},{18,... | collective-permute-start | bytes 6291464 | tf_op jit(solution)/shard_map/ppermute | solution.py:33
  1464.4 111.3 %collective-permute-start.81 = (bf16[512,1408]{1,0:T(8,128)(2,1)}, bf16[512,1408]{1,0:T(8,128)(2,1)}, u32[]{:S(2)}, u32[]{:S(2)}) collective-permute-start(bf16[512,1408]{1,0:T(8,128)(2,1)} %add_convert_fusion.4), channel_id=1, source_target_pairs={{0,2},{2,0},{4,6},{6,4},{8,10},{10,8},{12,14},{14,12},{16,18},{18,... | collective-permute-start | bytes 4325384 | tf_op jit(solution)/shard_map/ppermute | solution.py:33
  1481.4 30.0 %collective-permute-start.58 = (f32[8,2048]{1,0:T(8,128)S(1)}, f32[8,2048]{1,0:T(8,128)S(1)}, u32[]{:S(2)}, u32[]{:S(2)}) collective-permute-start(f32[8,2048]{1,0:T(8,128)S(1)} %slice_multiply_fusion), channel_id=1, source_target_pairs={{2,0},{4,2},{6,4},{8,6},{10,8},{12,10},{14,12},{16,14},{18,16},{20... | collective-permute-start | bytes 196616 | tf_op jit(solution)/shard_map/ppermute | solution.py:26
  1547.5 33.0 %collective-permute-start.80 = (bf16[512,1536]{1,0:T(8,128)(2,1)S(1)}, bf16[512,1536]{1,0:T(8,128)(2,1)S(1)}, u32[]{:S(2)}, u32[]{:S(2)}) collective-permute-start(bf16[512,1536]{1,0:T(8,128)(2,1)S(1)} %copy-done.112), channel_id=1, source_target_pairs={{0,4},{2,6},{4,0},{6,2},{8,12},{10,14},{12,8},{14,10},{16,20},{18,... | collective-permute-start | bytes 4718600 | tf_op jit(solution)/shard_map/ppermute | solution.py:33
  1569.2 101.7 %collective-permute-start.89 = (bf16[2048,128]{1,0:T(8,128)(2,1)}, bf16[2048,128]{1,0:T(8,128)(2,1)}, u32[]{:S(2)}, u32[]{:S(2)}) collective-permute-start(bf16[2048,128]{1,0:T(8,128)(2,1)} %get-tuple-element.307), channel_id=1, source_target_pairs={{0,8},{2,10},{4,12},{6,14},{8,0},{10,2},{12,4},{14,6},{16,24},{18,... | collective-permute-start | bytes 1572872 | tf_op jit(solution)/shard_map/ppermute | solution.py:33
  1574.0 96.9 %collective-permute-start.90 = (bf16[2048,128]{1,0:T(8,128)(2,1)}, bf16[2048,128]{1,0:T(8,128)(2,1)}, u32[]{:S(2)}, u32[]{:S(2)}) collective-permute-start(bf16[2048,128]{1,0:T(8,128)(2,1)} %get-tuple-element.306), channel_id=1, source_target_pairs={{0,16},{2,18},{4,20},{6,22},{8,24},{10,26},{12,28},{14,30},{16,0},... | collective-permute-start | bytes 1572872 | tf_op jit(solution)/shard_map/ppermute | solution.py:33
  1580.5 43.4 %collective-permute-start.87 = (bf16[128,1408]{1,0:T(8,128)(2,1)S(1)}, bf16[128,1408]{1,0:T(8,128)(2,1)S(1)}, u32[]{:S(2)}, u32[]{:S(2)}) collective-permute-start(bf16[128,1408]{1,0:T(8,128)(2,1)S(1)} %get-tuple-element.325), channel_id=1, source_target_pairs={{0,16},{2,18},{4,20},{6,22},{8,24},{10,26},{12,28},{14,30},{16,0},... | collective-permute-start | bytes 1081352 | tf_op jit(solution)/shard_map/ppermute | solution.py:33
  1580.5 44.2 %collective-permute-start.88 = (bf16[128,1408]{1,0:T(8,128)(2,1)S(1)}, bf16[128,1408]{1,0:T(8,128)(2,1)S(1)}, u32[]{:S(2)}, u32[]{:S(2)}) collective-permute-start(bf16[128,1408]{1,0:T(8,128)(2,1)S(1)} %get-tuple-element.324), channel_id=1, source_target_pairs={{0,24},{2,26},{4,28},{6,30},{8,16},{10,18},{12,20},{14,22},{16,8},... | collective-permute-start | bytes 1081352 | tf_op jit(solution)/shard_map/ppermute | solution.py:33
  1623.9 44.7 %collective-permute-start.84 = (bf16[128,1536]{1,0:T(8,128)(2,1)}, bf16[128,1536]{1,0:T(8,128)(2,1)}, u32[]{:S(2)}, u32[]{:S(2)}) collective-permute-start(bf16[128,1536]{1,0:T(8,128)(2,1)} %get-tuple-element.320), channel_id=1, source_target_pairs={{0,16},{2,18},{4,20},{6,22},{8,24},{10,26},{12,28},{14,30},{16,0},... | collective-permute-start | bytes 1179656 | tf_op jit(solution)/shard_map/ppermute | solution.py:33
  1624.7 44.0 %collective-permute-start.85 = (bf16[128,1536]{1,0:T(8,128)(2,1)S(1)}, bf16[128,1536]{1,0:T(8,128)(2,1)}, u32[]{:S(2)}, u32[]{:S(2)}) collective-permute-start(bf16[128,1536]{1,0:T(8,128)(2,1)S(1)} %get-tuple-element.319), channel_id=1, source_target_pairs={{0,24},{2,26},{4,28},{6,30},{8,16},{10,18},{12,20},{14,22},{16,8},... | collective-permute-start | bytes 1179656 | tf_op jit(solution)/shard_map/ppermute | solution.py:33
  1636.8 34.1 %collective-permute-start.91 = (bf16[2048,128]{1,0:T(8,128)(2,1)}, bf16[2048,128]{1,0:T(8,128)(2,1)S(1)}, u32[]{:S(2)}, u32[]{:S(2)}) collective-permute-start(bf16[2048,128]{1,0:T(8,128)(2,1)} %get-tuple-element.305), channel_id=1, source_target_pairs={{0,24},{2,26},{4,28},{6,30},{8,16},{10,18},{12,20},{14,22},{16,8},... | collective-permute-start | bytes 1572872 | tf_op jit(solution)/shard_map/ppermute | solution.py:33
  (157 other events, 4737.6 us)
Sparse Core Ops, SparseCore 0:
  10.8 215.6 all-gather.3
  238.8 220.3 all-gather.7
  461.9 177.7 all-gather.5
  764.6 296.6 reduce-scatter.4
  1063.5 270.8 reduce-scatter.2

commit v2 on v1

--- a/solution.py
+++ b/solution.py
@@ -80,13 +80,16 @@
 
 
 class Reduction:
-    def __init__(self, parts, axis, first, gates=()):
+    def __init__(self, parts, axis, first, gates=(), later=()):
         self.axis, self.second = (axis, 3 - first)
         self.near, self.far = (parts[0], parts[3 - first])
         low = [parts[k].astype(jnp.bfloat16) for k in (first, 3)]
         if gates:
-            low = lax.optimization_barrier((*low, *gates))[:2]
-        self.got = [hop(part, first) for part in low]
+            low = list(lax.optimization_barrier((*low, *gates))[:2])
+        if later:
+            low[1] = after(low[1], *later)
+        one = hop(low[0], first)
+        self.got = [one, hop(low[1], first)]
 
     def onward(self, *gates):
         got = lax.optimization_barrier((*self.got, *gates))[:2] if gates else self.got
@@ -848,8 +851,7 @@
     near = (input_held[-1][1], mix_held[-1][1])
     input_held = spread(input_held, 0, [2])
     mix_held = spread(mix_held, 0, [1])
-    ffn_gate_weight = lax.all_gather(ffn_gate_proj, "ctx", axis=0, tiled=True)
-    ffn_up_weight = lax.all_gather(after(ffn_up_proj, *near), "ctx", axis=0, tiled=True)
+    ffn_gate_weight = lax.all_gather(after(ffn_gate_proj, *near), "ctx", axis=0, tiled=True)
     out_held = spread([([0], out_here)], 1, across, near)
     input_weight = joined(input_held, 0)
     mix_weights = joined(mix_held, 0)
@@ -873,7 +875,7 @@
     ).astype(jnp.bfloat16)
     first_pre = plain_product(normed_low, input_weight)
     mix_pre = plain_product(normed_low, mix_weights)
-    ffn_down_weight = lax.all_gather(after(ffn_down_proj, mix_pre), "ctx", axis=1, tiled=True)
+    ffn_up_weight = lax.all_gather(after(ffn_up_proj, mix_pre), "ctx", axis=0, tiled=True)
     step_raw = mix_pre[:block_rows, shared : shared + steps]
     query_at = shared + 128
     key_at = query_at + heads_wide
@@ -909,6 +911,7 @@
     intra_out, local_states, bc_low = scan_forward(
         first_pre, mix_pre, taps, bc_taps, step_cols, sum_cols, sum_rows, inner, shared
     )
+    ffn_down_weight = lax.all_gather(after(ffn_down_proj, local_states), "ctx", axis=1, tiled=True)
     decay_row = keep_state * jnp.repeat(jnp.exp(log_decay[block_rows - 1]), head_dim)[None, :]
     keep_low = keep_state.astype(jnp.bfloat16)
     reached, returned = carried_states(local_states, decay_row, False)
@@ -950,9 +953,9 @@
     def in_quarters(value):
         return jnp.split(value, 4, axis=1)
 
-    def rows_grad(left_side, right_side, first, gates=()):
+    def rows_grad(left_side, right_side, first, gates=(), later=()):
         parts = [product_of_cols(part, right_side) for part in in_quarters(left_side)]
-        return Reduction(parts, 0, first, gates)
+        return Reduction(parts, 0, first, gates, later)
 
     def cols_grad(left_side, right_side, first, gates=()):
         parts = [product_of_cols(left_side, part) for part in in_quarters(right_side)]
@@ -968,12 +971,6 @@
     norm_two_part = product_by_rows(ffn_gate_low, ffn_gate_weight) + product_by_rows(
         ffn_up_low, ffn_up_weight
     )
-    ffn_up_grad = lax.psum_scatter(
-        product_of_cols(normed_two_low, ffn_up_low).astype(jnp.bfloat16),
-        "ctx",
-        scatter_dimension=0,
-        tiled=True,
-    )
     norm_two_grad = pair_sum(norm_two_part)
     hidden_norm_grad, gain_two_grad = norm_two_back(norm_two_grad)
     hidden_grad = grad_out + hidden_norm_grad
@@ -983,13 +980,6 @@
         mixed_grad, scan_out, bc_low, sum_cols, gate_pre, 0
     )
     end_grad, returned = carried_states(keep_low * state_in_grad, decay_row, True)
-    gate_late = after(ffn_gate_low, ssm_gate_low)
-    ffn_gate_grad = lax.psum_scatter(
-        product_of_cols(normed_two_low, gate_late).astype(jnp.bfloat16),
-        "ctx",
-        scatter_dimension=0,
-        tiled=True,
-    )
     layout = after(layout, returned)
     query_grad_low, window_grad, own_pair_grad = attention_back(
         layout, query_rot, window, attn_low, log_totals, mixed_grad, inner, cos_wide, sin_wide
@@ -1000,8 +990,12 @@
             window_grad[at : at + block_rows], "ctx", -distance
         ).astype(jnp.float32)
     down_sum.onward(end_grad, query_grad_low)
-    out_sum = cols_grad(mixed_low, hidden_low, 1, (end_grad, query_grad_low))
-    gate_sum = rows_grad(normed_low, ssm_gate_low, 2, (end_grad, query_grad_low))
+    free = (end_grad, query_grad_low)
+    normed_two_slots = reordered(normed_two_low, from_whole)
+    swish_sum = rows_grad(normed_two_slots, ffn_gate_low, 2, (ssm_gate_low,), free)
+    up_sum = rows_grad(normed_two_slots, ffn_up_low, 1, (ssm_gate_low,), free)
+    out_sum = cols_grad(mixed_low, hidden_low, 1, free)
+    gate_sum = rows_grad(normed_low, ssm_gate_low, 2, free)
     key_grad_low = (
         rotate(own_pair_grad[:, :HD].reshape(block_rows, 1, HD), cos_table, -sin_table)
         .reshape(block_rows, HD)
@@ -1038,10 +1032,14 @@
         + product_by_rows(mix_grads, mix_weights)
         + product_by_rows(ssm_gate_low, gate_weight)
     )
-    gate_sum.onward(norm_one_part)
-    out_sum.onward(gate_sum.far_low)
-    down_sum.last(out_sum.far_low)
-    mix_sum.onward(*down_sum.blocks_low)
+    up_sum.onward(norm_one_part)
+    swish_sum.onward(up_sum.far_low)
+    down_sum.last(swish_sum.far_low)
+    out_sum.onward(*down_sum.blocks_low)
+    gate_sum.onward(out_sum.far_low)
+    up_sum.last(gate_sum.far_low)
+    swish_sum.last(*up_sum.blocks_low)
+    mix_sum.onward(*swish_sum.blocks_low)
     input_sum.onward(mix_sum.far_low)
     gate_sum.last(input_sum.far_low)
     out_sum.last(*gate_sum.blocks_low)
@@ -1100,8 +1098,8 @@
         mix_grad[:, key_at + pair_wide :],
         out_grad[inner:],
         own(sums[7], rows_here),
-        ffn_gate_grad.astype(jnp.float32),
-        ffn_up_grad.astype(jnp.float32),
+        swish_sum.total(),
+        up_sum.total(),
         down_sum.total(),
     )
 

time: 1710 us -> 1810 us (1.058)
  starting transfers between devices: 272 us -> 375 us
    ppermute x67 -> x79, starting transfers between devices: 193 us -> 308 us  [hop(): lax.ppermute(value, 'ctx', [(source, source ^ code) for source in range(c...]
    dot_general x22 -> x28, matrix products: 78.5 us -> 90.2 us  [product_of_cols(): lax.dot_general(left_side, right_side, (((0,), (0,)), ((), ())), preferre...]
    ppermute x67 -> x79, waiting for transfers between devices: 757 us -> 750 us  [hop(): lax.ppermute(value, 'ctx', [(source, source ^ code) for source in range(c...]
    unnamed x273 -> x295, local copies, waits for them, and re-layouts: 48.4 us -> 49.5 us
  transfers between devices with their start and end apart: 100 -> 110, of which waited for: 44 -> 39; matrix products, arithmetic and copies ran while one was open for 23% -> 20% of each run, Pallas kernels for 9% -> 8%
where the time goes in v2:
time: 1810 us; the launch traced here: 1800 us
  waiting for transfers between devices  824 us (46%)
  starting transfers between devices  375 us (21%)
  matrix products  210 us (12%)
  Pallas kernels  149 us (8%)
  other arithmetic  118 us (7%)
  local copies, waits for them, and re-layouts  108 us (6%)
  between operations  18.3 us (1%)
    ppermute x79, waiting for transfers between devices, hop(): lax.ppermute(value, 'ctx', [(source, source ^ code) for source in range(c...  750 us
    ppermute x79, starting transfers between devices, hop(): lax.ppermute(value, 'ctx', [(source, source ^ code) for source in range(c...  308 us
    dot_general x28, matrix products, product_of_cols(): lax.dot_general(left_side, right_side, (((0,), (0,)), ((), ())), preferre...  90.2 us
    ppermute x22, waiting for transfers between devices, shifted(): lax.ppermute(value, axis, [(source, source + steps) for source in range(l...  74.4 us
    ppermute x22, starting transfers between devices, shifted(): lax.ppermute(value, axis, [(source, source + steps) for source in range(l...  66 us
    pallas_call x1, Pallas kernels, scan_back(): pl.pallas_call(body, grid=(pairs,), out_shape=(wide_low, eight_f32, table...  59.6 us
    dot_general x7, matrix products, plain_product(): return jnp.dot(left_side, right_side, preferred_element_type=jnp.float32)  58.9 us
    dot_general x7, matrix products, product_by_rows(): lax.dot_general(left_side, right_side, (((1,), (1,)), ((), ())), preferre...  57.4 us
  transfers between devices with their start and end apart: 110, of which 39 were waited for; matrix products, arithmetic and copies ran while one was open for 20% of the time, Pallas kernels for 8%

profile of v2, /device:TPU:0, one launch (start us, length us, event | category | flops | bytes accessed | tf_op | source)
XLA Modules:
  0.0 1802.7 jit_solution(10241035795990632940)
XLA Ops:
  23.7 46.5 %collective-permute-done.1 = bf16[128,4480]{1,0:T(8,128)(2,1)S(1)} collective-permute-done((bf16[128,4480]{1,0:T(8,128)(2,1)S(1)}, bf16[128,4480]{1,0:T(8,128)(2,1)S(1)}, u32[]{:S(2)}, u32[]{:S(2)}) %collective-permute-start.1) | collective-permute-done | bytes 1146912 | tf_op jit(solution)/shard_map/ppermute | solution.py:33
  71.1 28.2 %collective-permute-done.2 = bf16[128,4480]{1,0:T(8,128)(2,1)S(1)} collective-permute-done((bf16[128,4480]{1,0:T(8,128)(2,1)S(1)}, bf16[128,4480]{1,0:T(8,128)(2,1)S(1)}, u32[]{:S(2)}, u32[]{:S(2)}) %collective-permute-start.2) | collective-permute-done | bytes 1146912 | tf_op jit(solution)/shard_map/ppermute | solution.py:33
  113.1 21.0 %collective-permute-done.5 = bf16[512,1408]{1,0:T(8,128)(2,1)S(1)} collective-permute-done((bf16[512,1408]{1,0:T(8,128)(2,1)}, bf16[512,1408]{1,0:T(8,128)(2,1)S(1)}, u32[]{:S(2)}, u32[]{:S(2)}) %collective-permute-start.5) | collective-permute-done | bytes 1441824 | tf_op jit(solution)/shard_map/ppermute | solution.py:33
  150.5 22.8 %collective-permute-done.6 = bf16[512,1408]{1,0:T(8,128)(2,1)} collective-permute-done((bf16[512,1408]{1,0:T(8,128)(2,1)S(1)}, bf16[512,1408]{1,0:T(8,128)(2,1)}, u32[]{:S(2)}, u32[]{:S(2)}) %collective-permute-start.6) | collective-permute-done | bytes 1441824 | tf_op jit(solution)/shard_map/ppermute | solution.py:33
  179.2 5.8 fusion.175.bc_ref.bc_rim_ref.query_ref
  193.2 24.9 %collective-permute-start.8 = (bf16[512,1536]{1,0:T(8,128)(2,1)}, bf16[512,1536]{1,0:T(8,128)(2,1)}, u32[]{:S(2)}, u32[]{:S(2)}) collective-permute-start(bf16[512,1536]{1,0:T(8,128)(2,1)} %pad_maximum_fusion.2), channel_id=1, source_target_pairs={{0,4},{2,6},{4,0},{6,2},{8,12},{10,14},{12,8},{14,10},{16,20},{18,... | collective-permute-start | bytes 4718600 | tf_op jit(solution)/shard_map/ppermute | solution.py:33
  219.2 8.7 collective-permute-done.7
  227.9 39.3 %collective-permute-start.9 = (bf16[512,1536]{1,0:T(8,128)(2,1)}, bf16[512,1536]{1,0:T(8,128)(2,1)}, u32[]{:S(2)}, u32[]{:S(2)}) collective-permute-start(bf16[512,1536]{1,0:T(8,128)(2,1)} %collective-permute-done.7), channel_id=1, source_target_pairs={{0,4},{2,6},{4,0},{6,2},{8,12},{10,14},{12,8},{14,10},{16,20},{18,... | collective-permute-start | bytes 4718600 | tf_op jit(solution)/shard_map/ppermute | solution.py:33
  284.0 30.0 %collective-permute-done.9 = bf16[512,1536]{1,0:T(8,128)(2,1)} collective-permute-done((bf16[512,1536]{1,0:T(8,128)(2,1)}, bf16[512,1536]{1,0:T(8,128)(2,1)}, u32[]{:S(2)}, u32[]{:S(2)}) %collective-permute-start.9) | collective-permute-done | bytes 1572896 | tf_op jit(solution)/shard_map/ppermute | solution.py:33
  316.7 8.0 fusion.174.in_ref.rim_ref
  324.7 22.0 %scan_forward.1 = (f32[512,1536]{1,0:T(8,128)}, bf16[256,1536]{1,0:T(8,128)(2,1)S(1)}, bf16[512,512]{1,0:T(8,128)(2,1)S(1)}) custom-call(f32[528,1536]{1,0:T(8,128)} %fusion.174.in_ref.rim_ref, f32[528,1536]{1,0:T(8,128)} %fusion.174.in_ref.rim_ref, f32[8,1536]{1,0:T(8,128)S(1)} %copy-done.14, f32[528,1408]{1,0:T(8,128)S(1)} %fusion.175.bc_ref.bc_rim_ref.query_ref, ...), custom_call_target="tpu_custom_call" | custom-call | tf_op jit(solution)/shard_map/scan_forward/pallas_call | solution.py:338
  369.1 13.3 collective-permute-done.33
  396.2 15.0 collective-permute-start.25
  442.0 6.9 collective-permute-start.29
  459.9 7.3 collective-permute-start.35
  468.3 14.2 collective-permute-done.30
  482.5 8.2 collective-permute-start.19
  491.7 98.5 %collective-permute-done.19 = bf16[256,384]{1,0:T(8,128)(2,1)S(1)} collective-permute-done((bf16[256,384]{1,0:T(8,128)(2,1)S(1)}, bf16[256,384]{1,0:T(8,128)(2,1)S(1)}, u32[]{:S(2)}, u32[]{:S(2)}) %collective-permute-start.19) | collective-permute-done | bytes 196640 | tf_op jit(solution)/shard_map/ppermute | solution.py:33
  600.6 5.9 attention_forward.1
  617.0 7.9 collective-permute-start.37
  628.0 29.4 %collective-permute-done.24 = bf16[512,1536]{1,0:T(8,128)(2,1)S(1)} collective-permute-done((bf16[512,1536]{1,0:T(8,128)(2,1)S(1)}, bf16[512,1536]{1,0:T(8,128)(2,1)S(1)}, u32[]{:S(2)}, u32[]{:S(2)}) %collective-permute-start.24) | collective-permute-done | bytes 1572896 | tf_op jit(solution)/shard_map/ppermute | solution.py:33
  662.8 9.7 scan_gated.1
  672.8 7.4 collective-permute-done.37
  681.8 9.7 reduce-precision_convert_fusion.2
  703.6 6.3 collective-permute-done.45
  710.0 5.8 convert_add_fusion.7.in_ref
  732.6 9.4 fusion.177
  742.1 10.6 fusion.178
  752.6 11.4 multiply_convert_fusion.1
  781.3 6.1 fusion.179
  787.4 10.4 fusion.171
  797.9 9.2 reduce-precision_convert_fusion.1
  831.0 5.7 fusion.148
  841.4 10.6 fusion.180.grad_ref
  860.8 10.5 scan_gated_back.1
  884.0 30.3 %collective-permute-done.43 = bf16[256,384]{1,0:T(8,128)(2,1)S(1)} collective-permute-done((bf16[256,384]{1,0:T(8,128)(2,1)S(1)}, bf16[256,384]{1,0:T(8,128)(2,1)S(1)}, u32[]{:S(2)}, u32[]{:S(2)}) %collective-permute-start.43) | collective-permute-done | bytes 196640 | tf_op jit(solution)/shard_map/ppermute | solution.py:33
  914.3 5.6 collective-permute-done.42
  925.4 47.7 %collective-permute-done.46 = bf16[256,384]{1,0:T(8,128)(2,1)S(1)} collective-permute-done((bf16[256,384]{1,0:T(8,128)(2,1)S(1)}, bf16[256,384]{1,0:T(8,128)(2,1)S(1)}, u32[]{:S(2)}, u32[]{:S(2)}) %collective-permute-start.46) | collective-permute-done | bytes 196640 | tf_op jit(solution)/shard_map/ppermute | solution.py:26
  977.1 10.6 attention_back.1
  995.1 59.6 %scan_back.1 = (bf16[528,1536]{1,0:T(8,128)(2,1)}, f32[8,1536]{1,0:T(8,128)}, f32[12,512,2]{2,1,0:T(8,128)}, f32[12,512,2]{2,1,0:T(8,128)}, f32[528,512]{1,0:T(8,128)}, /*index=5*/f32[8,512]{1,0:T(8,128)}) custom-call(f32[528,1536]{1,0:T(8,128)} %fusion.174.in_ref.rim_ref, f32[528,1536]{1,0:T(8,128)} %fusion.174.in_ref.rim_ref, ...), custom_call_target="tpu_custom_call" | custom-call | tf_op jit(solution)/shard_map/scan_back/pallas_call | solution.py:570
  1088.0 12.5 collective-permute-start.71
  1100.5 6.5 collective-permute-start.73
  1119.4 6.3 collective-permute-start.74
  1141.4 9.2 reduce-precision_convert_fusion
  1150.6 7.8 collective-permute-done.73
  1160.9 42.5 %collective-permute-done.74 = bf16[512,2048]{1,0:T(8,128)(2,1)S(1)} collective-permute-done((bf16[512,2048]{1,0:T(8,128)(2,1)}, bf16[512,2048]{1,0:T(8,128)(2,1)S(1)}, u32[]{:S(2)}, u32[]{:S(2)}) %collective-permute-start.74) | collective-permute-done | bytes 2097184 | tf_op jit(solution)/shard_map/ppermute | solution.py:33
  1207.8 35.4 %collective-permute-done.72 = bf16[512,2048]{1,0:T(8,128)(2,1)} collective-permute-done((bf16[512,2048]{1,0:T(8,128)(2,1)}, bf16[512,2048]{1,0:T(8,128)(2,1)}, u32[]{:S(2)}, u32[]{:S(2)}) %collective-permute-start.72) | collective-permute-done | bytes 2097184 | tf_op jit(solution)/shard_map/ppermute | solution.py:33
  1252.6 30.2 %collective-permute-start.106 = (bf16[2048,128]{1,0:T(8,128)(2,1)S(1)}, bf16[2048,128]{1,0:T(8,128)(2,1)S(1)}, u32[]{:S(2)}, u32[]{:S(2)}) collective-permute-start(bf16[2048,128]{1,0:T(8,128)(2,1)S(1)} %get-tuple-element.342), channel_id=1, source_target_pairs={{0,24},{2,26},{4,28},{6,30},{8,16},{10,18},{12,20},{14,22},{16,8},... | collective-permute-start | bytes 1572872 | tf_op jit(solution)/shard_map/ppermute | solution.py:33
  1282.8 10.0 collective-permute-done.67
  1292.8 27.1 %collective-permute-start.105 = (bf16[2048,128]{1,0:T(8,128)(2,1)S(1)}, bf16[2048,128]{1,0:T(8,128)(2,1)S(1)}, u32[]{:S(2)}, u32[]{:S(2)}) collective-permute-start(bf16[2048,128]{1,0:T(8,128)(2,1)S(1)} %get-tuple-element.343), channel_id=1, source_target_pairs={{0,16},{2,18},{4,20},{6,22},{8,24},{10,26},{12,28},{14,30},{16,0},... | collective-permute-start | bytes 1572872 | tf_op jit(solution)/shard_map/ppermute | solution.py:33
  1331.5 9.3 collective-permute-done.105
  1348.3 6.2 reordered.9
  1361.6 80.1 %collective-permute-done.60 = f32[120,128]{1,0:T(8,128)S(1)} collective-permute-done((f32[120,128]{1,0:T(8,128)S(1)}, f32[120,128]{1,0:T(8,128)S(1)}, u32[]{:S(2)}, u32[]{:S(2)}) %collective-permute-start.60) | collective-permute-done | bytes 61472 | tf_op jit(solution)/shard_map/ppermute | solution.py:33
  1456.8 20.4 %collective-permute-start.63 = (f32[120,128]{1,0:T(8,128)S(1)}, f32[120,128]{1,0:T(8,128)S(1)}, u32[]{:S(2)}, u32[]{:S(2)}) collective-permute-start(f32[120,128]{1,0:T(8,128)S(1)} %add.464), channel_id=1, source_target_pairs={{0,16},{2,18},{4,20},{6,22},{8,24},{10,26},{12,28},{14,30},{16,0},... | collective-permute-start | bytes 184328 | tf_op jit(solution)/shard_map/ppermute | solution.py:33
  1502.9 13.8 collective-permute-done.79
  1518.0 29.5 %collective-permute-done.80 = bf16[512,1408]{1,0:T(8,128)(2,1)S(1)} collective-permute-done((bf16[512,1408]{1,0:T(8,128)(2,1)}, bf16[512,1408]{1,0:T(8,128)(2,1)S(1)}, u32[]{:S(2)}, u32[]{:S(2)}) %collective-permute-start.80) | collective-permute-done | bytes 1441824 | tf_op jit(solution)/shard_map/ppermute | solution.py:33
  1562.3 30.2 %collective-permute-done.88 = bf16[2048,512]{1,0:T(8,128)(2,1)S(1)} collective-permute-done((bf16[2048,512]{1,0:T(8,128)(2,1)}, bf16[2048,512]{1,0:T(8,128)(2,1)S(1)}, u32[]{:S(2)}, u32[]{:S(2)}) %collective-permute-start.88) | collective-permute-done | bytes 2097184 | tf_op jit(solution)/shard_map/ppermute | solution.py:33
  1600.2 10.0 collective-permute-done.83
  1619.1 50.0 %collective-permute-done.96 = bf16[2048,128]{1,0:T(8,128)(2,1)S(1)} collective-permute-done((bf16[2048,128]{1,0:T(8,128)(2,1)S(1)}, bf16[2048,128]{1,0:T(8,128)(2,1)S(1)}, u32[]{:S(2)}, u32[]{:S(2)}) %collective-permute-start.96) | collective-permute-done | bytes 524320 | tf_op jit(solution)/shard_map/ppermute | solution.py:33
  1673.8 32.3 %collective-permute-done.99 = bf16[128,2048]{1,0:T(8,128)(2,1)S(1)} collective-permute-done((bf16[128,2048]{1,0:T(8,128)(2,1)S(1)}, bf16[128,2048]{1,0:T(8,128)(2,1)S(1)}, u32[]{:S(2)}, u32[]{:S(2)}) %collective-permute-start.99) | collective-permute-done | bytes 524320 | tf_op jit(solution)/shard_map/ppermute | solution.py:33
  1707.4 19.1 %collective-permute-done.102 = bf16[128,2048]{1,0:T(8,128)(2,1)S(1)} collective-permute-done((bf16[128,2048]{1,0:T(8,128)(2,1)S(1)}, bf16[128,2048]{1,0:T(8,128)(2,1)S(1)}, u32[]{:S(2)}, u32[]{:S(2)}) %collective-permute-start.102) | collective-permute-done | bytes 524320 | tf_op jit(solution)/shard_map/ppermute | solution.py:33
  1745.1 22.3 %collective-permute-start.89 = (bf16[128,1536]{1,0:T(8,128)(2,1)S(1)}, bf16[128,1536]{1,0:T(8,128)(2,1)}, u32[]{:S(2)}, u32[]{:S(2)}) collective-permute-start(bf16[128,1536]{1,0:T(8,128)(2,1)S(1)} %get-tuple-element.352), channel_id=1, source_target_pairs={{0,8},{2,10},{4,12},{6,14},{8,0},{10,2},{12,4},{14,6},{16,24},{18,... | collective-permute-start | bytes 1179656 | tf_op jit(solution)/shard_map/ppermute | solution.py:33
  1767.4 12.4 collective-permute-done.93
  1786.4 7.1 collective-permute-done.90
  (699 shorter events, 513.6 us)
Async XLA Ops:
  7.2 725.4 %all-gather.6.cloned.1.call-start = ((), (), s32[]{:S(2)}) async-start(), calls=%async_computation.1 | async-start | bytes 8912896 | tf_op jit(solution)/shard_map/all_gather | solution.py:878
  18.1 52.2 %collective-permute-start.1 = (bf16[128,4480]{1,0:T(8,128)(2,1)S(1)}, bf16[128,4480]{1,0:T(8,128)(2,1)S(1)}, u32[]{:S(2)}, u32[]{:S(2)}) collective-permute-start(bf16[128,4480]{1,0:T(8,128)(2,1)S(1)} %get-tuple-element.401), channel_id=1, source_target_pairs={{0,8},{2,10},{4,12},{6,14},{8,0},{10,2},{12,4},{14,6},{16,24},{18,... | collective-permute-start | bytes 3440648 | tf_op jit(solution)/shard_map/ppermute | solution.py:33
  21.1 78.2 %collective-permute-start.2 = (bf16[128,4480]{1,0:T(8,128)(2,1)S(1)}, bf16[128,4480]{1,0:T(8,128)(2,1)S(1)}, u32[]{:S(2)}, u32[]{:S(2)}) collective-permute-start(bf16[128,4480]{1,0:T(8,128)(2,1)S(1)} %get-tuple-element.401), channel_id=1, source_target_pairs={{0,16},{2,18},{4,20},{6,22},{8,24},{10,26},{12,28},{14,30},{16,0},... | collective-permute-start | bytes 3440648 | tf_op jit(solution)/shard_map/ppermute | solution.py:33
  23.7 76.5 %collective-permute-start.3 = (bf16[128,4480]{1,0:T(8,128)(2,1)S(1)}, bf16[128,4480]{1,0:T(8,128)(2,1)S(1)}, u32[]{:S(2)}, u32[]{:S(2)}) collective-permute-start(bf16[128,4480]{1,0:T(8,128)(2,1)S(1)} %get-tuple-element.401), channel_id=1, source_target_pairs={{0,24},{2,26},{4,28},{6,30},{8,16},{10,18},{12,20},{14,22},{16,8},... | collective-permute-start | bytes 3440648 | tf_op jit(solution)/shard_map/ppermute | solution.py:33
  134.0 39.2 %collective-permute-start.6 = (bf16[512,1408]{1,0:T(8,128)(2,1)S(1)}, bf16[512,1408]{1,0:T(8,128)(2,1)}, u32[]{:S(2)}, u32[]{:S(2)}) collective-permute-start(bf16[512,1408]{1,0:T(8,128)(2,1)S(1)} %collective-permute-done.5), channel_id=1, source_target_pairs={{0,2},{2,0},{4,6},{6,4},{8,10},{10,8},{12,14},{14,12},{16,18},{18,... | collective-permute-start | bytes 4325384 | tf_op jit(solution)/shard_map/ppermute | solution.py:33
  185.1 557.0 %all-gather.8.cloned.1.call-start = ((), (), s32[]{:S(2)}) async-start(), calls=%async_computation.2 | async-start | bytes 8912896 | tf_op jit(solution)/shard_map/all_gather | solution.py:914
  191.7 36.2 %collective-permute-start.7 = (bf16[512,1536]{1,0:T(8,128)(2,1)}, bf16[512,1536]{1,0:T(8,128)(2,1)}, u32[]{:S(2)}, u32[]{:S(2)}) collective-permute-start(bf16[512,1536]{1,0:T(8,128)(2,1)} %pad_maximum_fusion.2), channel_id=1, source_target_pairs={{0,2},{2,0},{4,6},{6,4},{8,10},{10,8},{12,14},{14,12},{16,18},{18,... | collective-permute-start | bytes 4718600 | tf_op jit(solution)/shard_map/ppermute | solution.py:33
  193.2 76.7 %collective-permute-start.8 = (bf16[512,1536]{1,0:T(8,128)(2,1)}, bf16[512,1536]{1,0:T(8,128)(2,1)}, u32[]{:S(2)}, u32[]{:S(2)}) collective-permute-start(bf16[512,1536]{1,0:T(8,128)(2,1)} %pad_maximum_fusion.2), channel_id=1, source_target_pairs={{0,4},{2,6},{4,0},{6,2},{8,12},{10,14},{12,8},{14,10},{16,20},{18,... | collective-permute-start | bytes 4718600 | tf_op jit(solution)/shard_map/ppermute | solution.py:33
  227.9 86.1 %collective-permute-start.9 = (bf16[512,1536]{1,0:T(8,128)(2,1)}, bf16[512,1536]{1,0:T(8,128)(2,1)}, u32[]{:S(2)}, u32[]{:S(2)}) collective-permute-start(bf16[512,1536]{1,0:T(8,128)(2,1)} %collective-permute-done.7), channel_id=1, source_target_pairs={{0,4},{2,6},{4,0},{6,2},{8,12},{10,14},{12,8},{14,10},{16,20},{18,... | collective-permute-start | bytes 4718600 | tf_op jit(solution)/shard_map/ppermute | solution.py:33
  347.7 405.0 %all-gather.4.cloned.1.call-start = ((), (), s32[]{:S(2)}) async-start(), calls=%async_computation | async-start | bytes 8912896 | tf_op jit(solution)/shard_map/all_gather | solution.py:854
  396.2 39.0 %collective-permute-start.25 = (bf16[512,256]{1,0:T(8,128)(2,1)}, bf16[512,256]{1,0:T(8,128)(2,1)S(1)}, u32[]{:S(2)}, u32[]{:S(2)}) collective-permute-start(bf16[512,256]{1,0:T(8,128)(2,1)} %pad_maximum_fusion.7), channel_id=1, source_target_pairs={{0,14},{2,16},{4,18},{6,20},{8,22},{10,24},{12,26},{14,28},{16,30}... | collective-permute-start | bytes 786440 | tf_op jit(solution)/shard_map/ppermute | solution.py:26
  449.0 159.3 %collective-permute-start.23 = (bf16[512,1536]{1,0:T(8,128)(2,1)}, bf16[512,1536]{1,0:T(8,128)(2,1)S(1)}, u32[]{:S(2)}, u32[]{:S(2)}) collective-permute-start(bf16[512,1536]{1,0:T(8,128)(2,1)} %pad_maximum_fusion.3), channel_id=1, source_target_pairs={{0,4},{2,6},{4,0},{6,2},{8,12},{10,14},{12,8},{14,10},{16,20},{18,... | collective-permute-start | bytes 4718600 | tf_op jit(solution)/shard_map/ppermute | solution.py:33
  455.1 36.5 %collective-permute-start.31 = (bf16[512,256]{1,0:T(8,128)(2,1)}, bf16[512,256]{1,0:T(8,128)(2,1)S(1)}, u32[]{:S(2)}, u32[]{:S(2)}) collective-permute-start(bf16[512,256]{1,0:T(8,128)(2,1)} %pad_maximum_fusion.7), channel_id=1, source_target_pairs={{0,2},{2,4},{4,6},{6,8},{8,10},{10,12},{12,14},{14,16},{16,18},{18... | collective-permute-start | bytes 786440 | tf_op jit(solution)/shard_map/ppermute | solution.py:26
  459.9 157.1 %collective-permute-start.35 = (bf16[2048,512]{1,0:T(8,128)(2,1)S(1)}, bf16[2048,512]{1,0:T(8,128)(2,1)S(1)}, u32[]{:S(2)}, u32[]{:S(2)}) collective-permute-start(bf16[2048,512]{1,0:T(8,128)(2,1)S(1)} %copy-done.50), channel_id=1, source_target_pairs={{0,2},{2,0},{4,6},{6,4},{8,10},{10,8},{12,14},{14,12},{16,18},{18,... | collective-permute-start | bytes 6291464 | tf_op jit(solution)/shard_map/ppermute | solution.py:33
  467.2 145.6 %collective-permute-start.22 = (bf16[512,1536]{1,0:T(8,128)(2,1)S(1)}, bf16[512,1536]{1,0:T(8,128)(2,1)}, u32[]{:S(2)}, u32[]{:S(2)}) collective-permute-start(bf16[512,1536]{1,0:T(8,128)(2,1)S(1)} %copy-done.57), channel_id=1, source_target_pairs={{0,2},{2,0},{4,6},{6,4},{8,10},{10,8},{12,14},{14,12},{16,18},{18,... | collective-permute-start | bytes 4718600 | tf_op jit(solution)/shard_map/ppermute | solution.py:33
  482.5 107.8 %collective-permute-start.19 = (bf16[256,384]{1,0:T(8,128)(2,1)S(1)}, bf16[256,384]{1,0:T(8,128)(2,1)S(1)}, u32[]{:S(2)}, u32[]{:S(2)}) collective-permute-start(bf16[256,384]{1,0:T(8,128)(2,1)S(1)} %get-tuple-element.317), channel_id=1, source_target_pairs={{0,6},{2,4},{4,2},{6,0},{8,14},{10,12},{12,10},{14,8},{16,22},{18,... | collective-permute-start | bytes 589832 | tf_op jit(solution)/shard_map/ppermute | solution.py:33
  491.6 134.8 %collective-permute-start.36 = (bf16[2048,512]{1,0:T(8,128)(2,1)S(1)}, bf16[2048,512]{1,0:T(8,128)(2,1)S(1)}, u32[]{:S(2)}, u32[]{:S(2)}) collective-permute-start(bf16[2048,512]{1,0:T(8,128)(2,1)S(1)} %copy-done.50), channel_id=1, source_target_pairs={{0,4},{2,6},{4,0},{6,2},{8,12},{10,14},{12,8},{14,10},{16,20},{18,... | collective-permute-start | bytes 6291464 | tf_op jit(solution)/shard_map/ppermute | solution.py:33
  608.3 49.1 %collective-permute-start.24 = (bf16[512,1536]{1,0:T(8,128)(2,1)S(1)}, bf16[512,1536]{1,0:T(8,128)(2,1)S(1)}, u32[]{:S(2)}, u32[]{:S(2)}) collective-permute-start(bf16[512,1536]{1,0:T(8,128)(2,1)S(1)} %collective-permute-done.23), channel_id=1, source_target_pairs={{0,2},{2,0},{4,6},{6,4},{8,10},{10,8},{12,14},{14,12},{16,18},{18,... | collective-permute-start | bytes 4718600 | tf_op jit(solution)/shard_map/ppermute | solution.py:33
  617.0 63.2 %collective-permute-start.37 = (bf16[2048,512]{1,0:T(8,128)(2,1)S(1)}, bf16[2048,512]{1,0:T(8,128)(2,1)S(1)}, u32[]{:S(2)}, u32[]{:S(2)}) collective-permute-start(bf16[2048,512]{1,0:T(8,128)(2,1)S(1)} %collective-permute-done.35), channel_id=1, source_target_pairs={{0,4},{2,6},{4,0},{6,2},{8,12},{10,14},{12,8},{14,10},{16,20},{18,... | collective-permute-start | bytes 6291464 | tf_op jit(solution)/shard_map/ppermute | solution.py:33
  816.4 250.8 %collective-permute-start.68 = (bf16[2048,512]{1,0:T(8,128)(2,1)}, bf16[2048,512]{1,0:T(8,128)(2,1)}, u32[]{:S(2)}, u32[]{:S(2)}) collective-permute-start(bf16[2048,512]{1,0:T(8,128)(2,1)} %convolution_convert_fusion.9), channel_id=1, source_target_pairs={{0,2},{2,0},{4,6},{6,4},{8,10},{10,8},{12,14},{14,12},{16,18},{18,... | collective-permute-start | bytes 6291464 | tf_op jit(solution)/shard_map/ppermute | solution.py:33
  817.1 251.4 %collective-permute-start.69 = (bf16[2048,512]{1,0:T(8,128)(2,1)}, bf16[2048,512]{1,0:T(8,128)(2,1)}, u32[]{:S(2)}, u32[]{:S(2)}) collective-permute-start(bf16[2048,512]{1,0:T(8,128)(2,1)} %convolution_convert_fusion.8), channel_id=1, source_target_pairs={{0,2},{2,0},{4,6},{6,4},{8,10},{10,8},{12,14},{14,12},{16,18},{18,... | collective-permute-start | bytes 6291464 | tf_op jit(solution)/shard_map/ppermute | solution.py:33
  876.8 37.5 %collective-permute-start.43 = (bf16[256,384]{1,0:T(8,128)(2,1)S(1)}, bf16[256,384]{1,0:T(8,128)(2,1)S(1)}, u32[]{:S(2)}, u32[]{:S(2)}) collective-permute-start(bf16[256,384]{1,0:T(8,128)(2,1)S(1)} %get-tuple-element.386), channel_id=1, source_target_pairs={{0,2},{2,0},{4,6},{6,4},{8,10},{10,8},{12,14},{14,12},{16,18},{18,... | collective-permute-start | bytes 589832 | tf_op jit(solution)/shard_map/ppermute | solution.py:33
  877.5 36.8 %collective-permute-start.41 = (bf16[256,384]{1,0:T(8,128)(2,1)S(1)}, bf16[256,384]{1,0:T(8,128)(2,1)S(1)}, u32[]{:S(2)}, u32[]{:S(2)}) collective-permute-start(bf16[256,384]{1,0:T(8,128)(2,1)S(1)} %get-tuple-element.387), channel_id=1, source_target_pairs={{0,4},{2,6},{4,0},{6,2},{8,12},{10,14},{12,8},{14,10},{16,20},{18,... | collective-permute-start | bytes 589832 | tf_op jit(solution)/shard_map/ppermute | solution.py:33
  881.4 38.5 %collective-permute-start.42 = (bf16[256,384]{1,0:T(8,128)(2,1)S(1)}, bf16[256,384]{1,0:T(8,128)(2,1)S(1)}, u32[]{:S(2)}, u32[]{:S(2)}) collective-permute-start(bf16[256,384]{1,0:T(8,128)(2,1)S(1)} %get-tuple-element.385), channel_id=1, source_target_pairs={{0,6},{2,4},{4,2},{6,0},{8,14},{10,12},{12,10},{14,8},{16,22},{18,... | collective-permute-start | bytes 589832 | tf_op jit(solution)/shard_map/ppermute | solution.py:33
  920.2 52.9 %collective-permute-start.46 = (bf16[256,384]{1,0:T(8,128)(2,1)S(1)}, bf16[256,384]{1,0:T(8,128)(2,1)S(1)}, u32[]{:S(2)}, u32[]{:S(2)}) collective-permute-start(bf16[256,384]{1,0:T(8,128)(2,1)S(1)} %get-tuple-element.304), channel_id=1, source_target_pairs={{16,0},{18,2},{20,4},{22,6},{24,8},{26,10},{28,12},{30,14},{17,1},... | collective-permute-start | bytes 589832 | tf_op jit(solution)/shard_map/ppermute | solution.py:26
  921.5 51.6 %collective-permute-start.44 = (bf16[256,384]{1,0:T(8,128)(2,1)S(1)}, bf16[256,384]{1,0:T(8,128)(2,1)S(1)}, u32[]{:S(2)}, u32[]{:S(2)}) collective-permute-start(bf16[256,384]{1,0:T(8,128)(2,1)S(1)} %get-tuple-element.304), channel_id=1, source_target_pairs={{8,0},{10,2},{12,4},{14,6},{16,8},{18,10},{20,12},{22,14},{24,16},... | collective-permute-start | bytes 589832 | tf_op jit(solution)/shard_map/ppermute | solution.py:26
  990.1 92.1 %collective-permute-start.56 = (bf16[512,256]{1,0:T(8,128)(2,1)S(1)}, bf16[512,256]{1,0:T(8,128)(2,1)}, u32[]{:S(2)}, u32[]{:S(2)}) collective-permute-start(bf16[512,256]{1,0:T(8,128)(2,1)S(1)} %get-tuple-element.346), channel_id=1, source_target_pairs={{14,0},{16,2},{18,4},{20,6},{22,8},{24,10},{26,12},{28,14},{30,16}... | collective-permute-start | bytes 786440 | tf_op jit(solution)/shard_map/ppermute | solution.py:26
  991.4 92.1 %collective-permute-start.55 = (bf16[512,256]{1,0:T(8,128)(2,1)S(1)}, bf16[512,256]{1,0:T(8,128)(2,1)}, u32[]{:S(2)}, u32[]{:S(2)}) collective-permute-start(bf16[512,256]{1,0:T(8,128)(2,1)S(1)} %get-tuple-element.347), channel_id=1, source_target_pairs={{12,0},{14,2},{16,4},{18,6},{20,8},{22,10},{24,12},{26,14},{28,16}... | collective-permute-start | bytes 786440 | tf_op jit(solution)/shard_map/ppermute | solution.py:26
  992.7 95.3 %collective-permute-start.54 = (bf16[512,256]{1,0:T(8,128)(2,1)}, bf16[512,256]{1,0:T(8,128)(2,1)}, u32[]{:S(2)}, u32[]{:S(2)}) collective-permute-start(bf16[512,256]{1,0:T(8,128)(2,1)} %get-tuple-element.348), channel_id=1, source_target_pairs={{10,0},{12,2},{14,4},{16,6},{18,8},{20,10},{22,12},{24,14},{26,16}... | collective-permute-start | bytes 786440 | tf_op jit(solution)/shard_map/ppermute | solution.py:26
  1088.0 119.8 %collective-permute-start.71 = (bf16[512,2048]{1,0:T(8,128)(2,1)}, bf16[512,2048]{1,0:T(8,128)(2,1)}, u32[]{:S(2)}, u32[]{:S(2)}) collective-permute-start(bf16[512,2048]{1,0:T(8,128)(2,1)} %convolution_convert_fusion.7), channel_id=1, source_target_pairs={{0,4},{2,6},{4,0},{6,2},{8,12},{10,14},{12,8},{14,10},{16,20},{18,... | collective-permute-start | bytes 6291464 | tf_op jit(solution)/shard_map/ppermute | solution.py:33
  1100.5 57.9 %collective-permute-start.73 = (bf16[512,2048]{1,0:T(8,128)(2,1)}, bf16[512,2048]{1,0:T(8,128)(2,1)}, u32[]{:S(2)}, u32[]{:S(2)}) collective-permute-start(bf16[512,2048]{1,0:T(8,128)(2,1)} %convolution_convert_fusion.5), channel_id=1, source_target_pairs={{0,2},{2,0},{4,6},{6,4},{8,10},{10,8},{12,14},{14,12},{16,18},{18,... | collective-permute-start | bytes 6291464 | tf_op jit(solution)/shard_map/ppermute | solution.py:33
  1108.4 140.7 %collective-permute-start.70 = (bf16[2048,512]{1,0:T(8,128)(2,1)}, bf16[2048,512]{1,0:T(8,128)(2,1)}, u32[]{:S(2)}, u32[]{:S(2)}) collective-permute-start(bf16[2048,512]{1,0:T(8,128)(2,1)} %add_convert_fusion.3), channel_id=1, source_target_pairs={{0,4},{2,6},{4,0},{6,2},{8,12},{10,14},{12,8},{14,10},{16,20},{18,... | collective-permute-start | bytes 6291464 | tf_op jit(solution)/shard_map/ppermute | solution.py:33
  1110.8 132.4 %collective-permute-start.72 = (bf16[512,2048]{1,0:T(8,128)(2,1)}, bf16[512,2048]{1,0:T(8,128)(2,1)}, u32[]{:S(2)}, u32[]{:S(2)}) collective-permute-start(bf16[512,2048]{1,0:T(8,128)(2,1)} %convolution_convert_fusion.6), channel_id=1, source_target_pairs={{0,4},{2,6},{4,0},{6,2},{8,12},{10,14},{12,8},{14,10},{16,20},{18,... | collective-permute-start | bytes 6291464 | tf_op jit(solution)/shard_map/ppermute | solution.py:33
  1119.4 84.0 %collective-permute-start.74 = (bf16[512,2048]{1,0:T(8,128)(2,1)}, bf16[512,2048]{1,0:T(8,128)(2,1)S(1)}, u32[]{:S(2)}, u32[]{:S(2)}) collective-permute-start(bf16[512,2048]{1,0:T(8,128)(2,1)} %convolution_convert_fusion.4), channel_id=1, source_target_pairs={{0,2},{2,0},{4,6},{6,4},{8,10},{10,8},{12,14},{14,12},{16,18},{18,... | collective-permute-start | bytes 6291464 | tf_op jit(solution)/shard_map/ppermute | solution.py:33
  1158.4 94.2 %collective-permute-start.66 = (bf16[2048,512]{1,0:T(8,128)(2,1)}, bf16[2048,512]{1,0:T(8,128)(2,1)S(1)}, u32[]{:S(2)}, u32[]{:S(2)}) collective-permute-start(bf16[2048,512]{1,0:T(8,128)(2,1)} %convolution_convert_fusion.11), channel_id=1, source_target_pairs={{0,2},{2,0},{4,6},{6,4},{8,10},{10,8},{12,14},{14,12},{16,18},{18,... | collective-permute-start | bytes 6291464 | tf_op jit(solution)/shard_map/ppermute | solution.py:33
  1203.4 89.5 %collective-permute-start.67 = (bf16[2048,512]{1,0:T(8,128)(2,1)}, bf16[2048,512]{1,0:T(8,128)(2,1)}, u32[]{:S(2)}, u32[]{:S(2)}) collective-permute-start(bf16[2048,512]{1,0:T(8,128)(2,1)} %convolution_convert_fusion.10), channel_id=1, source_target_pairs={{0,2},{2,0},{4,6},{6,4},{8,10},{10,8},{12,14},{14,12},{16,18},{18,... | collective-permute-start | bytes 6291464 | tf_op jit(solution)/shard_map/ppermute | solution.py:33
  1207.8 112.2 %collective-permute-start.64 = (bf16[512,1536]{1,0:T(8,128)(2,1)}, bf16[512,1536]{1,0:T(8,128)(2,1)S(1)}, u32[]{:S(2)}, u32[]{:S(2)}) collective-permute-start(bf16[512,1536]{1,0:T(8,128)(2,1)} %convolution_convert_fusion.3), channel_id=1, source_target_pairs={{0,4},{2,6},{4,0},{6,2},{8,12},{10,14},{12,8},{14,10},{16,20},{18,... | collective-permute-start | bytes 4718600 | tf_op jit(solution)/shard_map/ppermute | solution.py:33
  1243.2 81.8 %collective-permute-start.65 = (bf16[512,1536]{1,0:T(8,128)(2,1)}, bf16[512,1536]{1,0:T(8,128)(2,1)}, u32[]{:S(2)}, u32[]{:S(2)}) collective-permute-start(bf16[512,1536]{1,0:T(8,128)(2,1)} %convolution_convert_fusion.2), channel_id=1, source_target_pairs={{0,4},{2,6},{4,0},{6,2},{8,12},{10,14},{12,8},{14,10},{16,20},{18,... | collective-permute-start | bytes 4718600 | tf_op jit(solution)/shard_map/ppermute | solution.py:33
  1249.1 96.5 %collective-permute-start.57 = (bf16[528,2048]{1,0:T(8,128)(2,1)}, bf16[528,2048]{1,0:T(8,128)(2,1)S(1)}, u32[]{:S(2)}, u32[]{:S(2)}) collective-permute-start(bf16[528,2048]{1,0:T(8,128)(2,1)} %get-tuple-element.456), channel_id=1, source_target_pairs={{0,1},{1,0},{2,3},{3,2},{4,5},{5,4},{6,7},{7,6},{8,9},{9,8},{10,11... | collective-permute-start | bytes 6488072 | tf_op jit(solution)/shard_map/ppermute | solution.py:37
  1252.6 78.9 %collective-permute-start.106 = (bf16[2048,128]{1,0:T(8,128)(2,1)S(1)}, bf16[2048,128]{1,0:T(8,128)(2,1)S(1)}, u32[]{:S(2)}, u32[]{:S(2)}) collective-permute-start(bf16[2048,128]{1,0:T(8,128)(2,1)S(1)} %get-tuple-element.342), channel_id=1, source_target_pairs={{0,24},{2,26},{4,28},{6,30},{8,16},{10,18},{12,20},{14,22},{16,8},... | collective-permute-start | bytes 1572872 | tf_op jit(solution)/shard_map/ppermute | solution.py:33
  1292.8 48.0 %collective-permute-start.105 = (bf16[2048,128]{1,0:T(8,128)(2,1)S(1)}, bf16[2048,128]{1,0:T(8,128)(2,1)S(1)}, u32[]{:S(2)}, u32[]{:S(2)}) collective-permute-start(bf16[2048,128]{1,0:T(8,128)(2,1)S(1)} %get-tuple-element.343), channel_id=1, source_target_pairs={{0,16},{2,18},{4,20},{6,22},{8,24},{10,26},{12,28},{14,30},{16,0},... | collective-permute-start | bytes 1572872 | tf_op jit(solution)/shard_map/ppermute | solution.py:33
  1325.0 228.1 %collective-permute-start.76 = (bf16[512,1536]{1,0:T(8,128)(2,1)}, bf16[512,1536]{1,0:T(8,128)(2,1)}, u32[]{:S(2)}, u32[]{:S(2)}) collective-permute-start(bf16[512,1536]{1,0:T(8,128)(2,1)} %convolution_convert_fusion.1), channel_id=1, source_target_pairs={{0,2},{2,0},{4,6},{6,4},{8,10},{10,8},{12,14},{14,12},{16,18},{18,... | collective-permute-start | bytes 4718600 | tf_op jit(solution)/shard_map/ppermute | solution.py:33
  1331.5 221.6 %collective-permute-start.77 = (bf16[512,1536]{1,0:T(8,128)(2,1)}, bf16[512,1536]{1,0:T(8,128)(2,1)}, u32[]{:S(2)}, u32[]{:S(2)}) collective-permute-start(bf16[512,1536]{1,0:T(8,128)(2,1)} %convolution_convert_fusion), channel_id=1, source_target_pairs={{0,2},{2,0},{4,6},{6,4},{8,10},{10,8},{12,14},{14,12},{16,18},{18,... | collective-permute-start | bytes 4718600 | tf_op jit(solution)/shard_map/ppermute | solution.py:33
  1340.8 154.6 %collective-permute-start.81 = (bf16[512,2048]{1,0:T(8,128)(2,1)}, bf16[512,2048]{1,0:T(8,128)(2,1)}, u32[]{:S(2)}, u32[]{:S(2)}) collective-permute-start(bf16[512,2048]{1,0:T(8,128)(2,1)} %add_convert_fusion.1), channel_id=1, source_target_pairs={{0,2},{2,0},{4,6},{6,4},{8,10},{10,8},{12,14},{14,12},{16,18},{18,... | collective-permute-start | bytes 6291464 | tf_op jit(solution)/shard_map/ppermute | solution.py:33
  1344.4 143.3 %collective-permute-start.82 = (bf16[512,2048]{1,0:T(8,128)(2,1)}, bf16[512,2048]{1,0:T(8,128)(2,1)}, u32[]{:S(2)}, u32[]{:S(2)}) collective-permute-start(bf16[512,2048]{1,0:T(8,128)(2,1)} %add_convert_fusion.2), channel_id=1, source_target_pairs={{0,4},{2,6},{4,0},{6,2},{8,12},{10,14},{12,8},{14,10},{16,20},{18,... | collective-permute-start | bytes 6291464 | tf_op jit(solution)/shard_map/ppermute | solution.py:33
  1358.3 83.5 %collective-permute-start.60 = (f32[120,128]{1,0:T(8,128)S(1)}, f32[120,128]{1,0:T(8,128)S(1)}, u32[]{:S(2)}, u32[]{:S(2)}) collective-permute-start(f32[120,128]{1,0:T(8,128)S(1)} %pad_bitcast_fusion), channel_id=1, source_target_pairs={{0,2},{2,0},{4,6},{6,4},{8,10},{10,8},{12,14},{14,12},{16,18},{18,... | collective-permute-start | bytes 184328 | tf_op jit(solution)/shard_map/ppermute | solution.py:33
  1487.7 59.8 %collective-permute-start.80 = (bf16[512,1408]{1,0:T(8,128)(2,1)}, bf16[512,1408]{1,0:T(8,128)(2,1)S(1)}, u32[]{:S(2)}, u32[]{:S(2)}) collective-permute-start(bf16[512,1408]{1,0:T(8,128)(2,1)} %convolution_convert_fusion.12), channel_id=1, source_target_pairs={{0,4},{2,6},{4,0},{6,2},{8,12},{10,14},{12,8},{14,10},{16,20},{18,... | collective-permute-start | bytes 4325384 | tf_op jit(solution)/shard_map/ppermute | solution.py:33
  1496.1 61.4 %collective-permute-start.75 = (bf16[512,1536]{1,0:T(8,128)(2,1)S(1)}, bf16[512,1536]{1,0:T(8,128)(2,1)}, u32[]{:S(2)}, u32[]{:S(2)}) collective-permute-start(bf16[512,1536]{1,0:T(8,128)(2,1)S(1)} %copy-done.121), channel_id=1, source_target_pairs={{0,2},{2,0},{4,6},{6,4},{8,10},{10,8},{12,14},{14,12},{16,18},{18,... | collective-permute-start | bytes 4718600 | tf_op jit(solution)/shard_map/ppermute | solution.py:33
  1516.7 75.7 %collective-permute-start.88 = (bf16[2048,512]{1,0:T(8,128)(2,1)}, bf16[2048,512]{1,0:T(8,128)(2,1)S(1)}, u32[]{:S(2)}, u32[]{:S(2)}) collective-permute-start(bf16[2048,512]{1,0:T(8,128)(2,1)} %add_convert_fusion), channel_id=1, source_target_pairs={{0,4},{2,6},{4,0},{6,2},{8,12},{10,14},{12,8},{14,10},{16,20},{18,... | collective-permute-start | bytes 6291464 | tf_op jit(solution)/shard_map/ppermute | solution.py:33
  1549.9 179.5 %collective-permute-start.87 = (bf16[512,1408]{1,0:T(8,128)(2,1)}, bf16[512,1408]{1,0:T(8,128)(2,1)}, u32[]{:S(2)}, u32[]{:S(2)}) collective-permute-start(bf16[512,1408]{1,0:T(8,128)(2,1)} %add_convert_fusion.6), channel_id=1, source_target_pairs={{0,2},{2,0},{4,6},{6,4},{8,10},{10,8},{12,14},{14,12},{16,18},{18,... | collective-permute-start | bytes 4325384 | tf_op jit(solution)/shard_map/ppermute | solution.py:33
  1557.1 179.3 %collective-permute-start.86 = (bf16[512,1536]{1,0:T(8,128)(2,1)}, bf16[512,1536]{1,0:T(8,128)(2,1)}, u32[]{:S(2)}, u32[]{:S(2)}) collective-permute-start(bf16[512,1536]{1,0:T(8,128)(2,1)} %add_convert_fusion.4), channel_id=1, source_target_pairs={{0,4},{2,6},{4,0},{6,2},{8,12},{10,14},{12,8},{14,10},{16,20},{18,... | collective-permute-start | bytes 4718600 | tf_op jit(solution)/shard_map/ppermute | solution.py:33
  1560.7 36.2 %collective-permute-start.85 = (bf16[128,1536]{1,0:T(8,128)(2,1)S(1)}, bf16[128,1536]{1,0:T(8,128)(2,1)S(1)}, u32[]{:S(2)}, u32[]{:S(2)}) collective-permute-start(bf16[128,1536]{1,0:T(8,128)(2,1)S(1)} %get-tuple-element.356), channel_id=1, source_target_pairs={{0,24},{2,26},{4,28},{6,30},{8,16},{10,18},{12,20},{14,22},{16,8},... | collective-permute-start | bytes 1179656 | tf_op jit(solution)/shard_map/ppermute | solution.py:33
  1560.8 37.9 %collective-permute-start.84 = (bf16[128,1536]{1,0:T(8,128)(2,1)S(1)}, bf16[128,1536]{1,0:T(8,128)(2,1)}, u32[]{:S(2)}, u32[]{:S(2)}) collective-permute-start(bf16[128,1536]{1,0:T(8,128)(2,1)S(1)} %get-tuple-element.357), channel_id=1, source_target_pairs={{0,16},{2,18},{4,20},{6,22},{8,24},{10,26},{12,28},{14,30},{16,0},... | collective-permute-start | bytes 1179656 | tf_op jit(solution)/shard_map/ppermute | solution.py:33
  1598.7 70.4 %collective-permute-start.96 = (bf16[2048,128]{1,0:T(8,128)(2,1)S(1)}, bf16[2048,128]{1,0:T(8,128)(2,1)S(1)}, u32[]{:S(2)}, u32[]{:S(2)}) collective-permute-start(bf16[2048,128]{1,0:T(8,128)(2,1)S(1)} %get-tuple-element.334), channel_id=1, source_target_pairs={{0,16},{2,18},{4,20},{6,22},{8,24},{10,26},{12,28},{14,30},{16,0},... | collective-permute-start | bytes 1572872 | tf_op jit(solution)/shard_map/ppermute | solution.py:33
  1610.3 58.8 %collective-permute-start.95 = (bf16[2048,128]{1,0:T(8,128)(2,1)S(1)}, bf16[2048,128]{1,0:T(8,128)(2,1)S(1)}, u32[]{:S(2)}, u32[]{:S(2)}) collective-permute-start(bf16[2048,128]{1,0:T(8,128)(2,1)S(1)} %get-tuple-element.335), channel_id=1, source_target_pairs={{0,8},{2,10},{4,12},{6,14},{8,0},{10,2},{12,4},{14,6},{16,24},{18,... | collective-permute-start | bytes 1572872 | tf_op jit(solution)/shard_map/ppermute | solution.py:33
  1616.9 52.5 %collective-permute-start.100 = (bf16[128,2048]{1,0:T(8,128)(2,1)S(1)}, bf16[128,2048]{1,0:T(8,128)(2,1)S(1)}, u32[]{:S(2)}, u32[]{:S(2)}) collective-permute-start(bf16[128,2048]{1,0:T(8,128)(2,1)S(1)} %copy-done.80), channel_id=1, source_target_pairs={{0,24},{2,26},{4,28},{6,30},{8,16},{10,18},{12,20},{14,22},{16,8},... | collective-permute-start | bytes 1572872 | tf_op jit(solution)/shard_map/ppermute | solution.py:33
  1669.1 37.0 %collective-permute-start.99 = (bf16[128,2048]{1,0:T(8,128)(2,1)S(1)}, bf16[128,2048]{1,0:T(8,128)(2,1)S(1)}, u32[]{:S(2)}, u32[]{:S(2)}) collective-permute-start(bf16[128,2048]{1,0:T(8,128)(2,1)S(1)} %copy-done.79), channel_id=1, source_target_pairs={{0,16},{2,18},{4,20},{6,22},{8,24},{10,26},{12,28},{14,30},{16,0},... | collective-permute-start | bytes 1572872 | tf_op jit(solution)/shard_map/ppermute | solution.py:33
  1669.1 37.0 %collective-permute-start.98 = (bf16[128,2048]{1,0:T(8,128)(2,1)S(1)}, bf16[128,2048]{1,0:T(8,128)(2,1)S(1)}, u32[]{:S(2)}, u32[]{:S(2)}) collective-permute-start(bf16[128,2048]{1,0:T(8,128)(2,1)S(1)} %copy-done.78), channel_id=1, source_target_pairs={{0,8},{2,10},{4,12},{6,14},{8,0},{10,2},{12,4},{14,6},{16,24},{18,... | collective-permute-start | bytes 1572872 | tf_op jit(solution)/shard_map/ppermute | solution.py:33
  1669.4 38.0 %collective-permute-start.103 = (bf16[128,2048]{1,0:T(8,128)(2,1)S(1)}, bf16[128,2048]{1,0:T(8,128)(2,1)S(1)}, u32[]{:S(2)}, u32[]{:S(2)}) collective-permute-start(bf16[128,2048]{1,0:T(8,128)(2,1)S(1)} %copy-done.77), channel_id=1, source_target_pairs={{0,24},{2,26},{4,28},{6,30},{8,16},{10,18},{12,20},{14,22},{16,8},... | collective-permute-start | bytes 1572872 | tf_op jit(solution)/shard_map/ppermute | solution.py:33
  1733.3 46.5 %collective-permute-start.93 = (bf16[128,1408]{1,0:T(8,128)(2,1)S(1)}, bf16[128,1408]{1,0:T(8,128)(2,1)S(1)}, u32[]{:S(2)}, u32[]{:S(2)}) collective-permute-start(bf16[128,1408]{1,0:T(8,128)(2,1)S(1)} %get-tuple-element.359), channel_id=1, source_target_pairs={{0,16},{2,18},{4,20},{6,22},{8,24},{10,26},{12,28},{14,30},{16,0},... | collective-permute-start | bytes 1081352 | tf_op jit(solution)/shard_map/ppermute | solution.py:33
  1733.3 46.5 %collective-permute-start.92 = (bf16[128,1408]{1,0:T(8,128)(2,1)S(1)}, bf16[128,1408]{1,0:T(8,128)(2,1)S(1)}, u32[]{:S(2)}, u32[]{:S(2)}) collective-permute-start(bf16[128,1408]{1,0:T(8,128)(2,1)S(1)} %get-tuple-element.360), channel_id=1, source_target_pairs={{0,8},{2,10},{4,12},{6,14},{8,0},{10,2},{12,4},{14,6},{16,24},{18,... | collective-permute-start | bytes 1081352 | tf_op jit(solution)/shard_map/ppermute | solution.py:33
  1741.0 45.5 %collective-permute-start.91 = (bf16[128,1536]{1,0:T(8,128)(2,1)}, bf16[128,1536]{1,0:T(8,128)(2,1)}, u32[]{:S(2)}, u32[]{:S(2)}) collective-permute-start(bf16[128,1536]{1,0:T(8,128)(2,1)} %get-tuple-element.353), channel_id=1, source_target_pairs={{0,24},{2,26},{4,28},{6,30},{8,16},{10,18},{12,20},{14,22},{16,8},... | collective-permute-start | bytes 1179656 | tf_op jit(solution)/shard_map/ppermute | solution.py:33
  1742.3 51.2 %collective-permute-start.90 = (bf16[128,1536]{1,0:T(8,128)(2,1)}, bf16[128,1536]{1,0:T(8,128)(2,1)}, u32[]{:S(2)}, u32[]{:S(2)}) collective-permute-start(bf16[128,1536]{1,0:T(8,128)(2,1)} %get-tuple-element.354), channel_id=1, source_target_pairs={{0,16},{2,18},{4,20},{6,22},{8,24},{10,26},{12,28},{14,30},{16,0},... | collective-permute-start | bytes 1179656 | tf_op jit(solution)/shard_map/ppermute | solution.py:33
  1745.1 48.4 %collective-permute-start.89 = (bf16[128,1536]{1,0:T(8,128)(2,1)S(1)}, bf16[128,1536]{1,0:T(8,128)(2,1)}, u32[]{:S(2)}, u32[]{:S(2)}) collective-permute-start(bf16[128,1536]{1,0:T(8,128)(2,1)S(1)} %get-tuple-element.352), channel_id=1, source_target_pairs={{0,8},{2,10},{4,12},{6,14},{8,0},{10,2},{12,4},{14,6},{16,24},{18,... | collective-permute-start | bytes 1179656 | tf_op jit(solution)/shard_map/ppermute | solution.py:33
  (178 other events, 4873.2 us)
Sparse Core Ops, SparseCore 0:
  185.2 173.4 all-gather.5
  361.3 212.6 all-gather.7
  576.8 157.3 all-gather.3

commit v3 on v2

--- a/solution.py
+++ b/solution.py
@@ -113,11 +113,9 @@
         return total
 
 
-def summed(value):
-    bit = 1
-    while bit < lax.axis_size("ctx"):
+def summed(value, bits):
+    for bit in bits:
         value = value + hop(value, bit)
-        bit *= 2
     return value
 
 
@@ -851,7 +849,7 @@
     near = (input_held[-1][1], mix_held[-1][1])
     input_held = spread(input_held, 0, [2])
     mix_held = spread(mix_held, 0, [1])
-    ffn_gate_weight = lax.all_gather(after(ffn_gate_proj, *near), "ctx", axis=0, tiled=True)
+    ffn_gate_weight = lax.all_gather(after(ffn_gate_proj, first_held[-1][1]), "ctx", axis=0, tiled=True)
     out_held = spread([([0], out_here)], 1, across, near)
     input_weight = joined(input_held, 0)
     mix_weights = joined(mix_held, 0)
@@ -1034,7 +1032,24 @@
     )
     up_sum.onward(norm_one_part)
     swish_sum.onward(up_sum.far_low)
-    down_sum.last(swish_sum.far_low)
+    norm_one_grad = reordered(pair_sum(norm_one_part), to_whole)
+    conv_bc_grads = jnp.concatenate([bc_tap_grad[:KW].T.reshape(-1), bc_tap_grad[KW]])
+    conv_bc_grads = conv_bc_grads + swap(conv_bc_grads)
+    longer = tokens_longer.astype(jnp.float32)
+    scale_one = lax.rsqrt(jnp.mean(longer * longer, axis=1, keepdims=True) + epsilon)
+    gain_one_grad = jnp.sum(norm_one_grad * longer * scale_one, axis=0)
+    small = [
+        tap_sums[0].reshape(-1),
+        *tap_sums[1:],
+        conv_bc_grads,
+        gain_one_grad,
+        gain_two_grad,
+    ]
+    packed = jnp.concatenate(small)
+    filled = -packed.shape[0] % 1024
+    high_bits = [bit for bit in (32, 16, 8, 4) if bit < devices]
+    packed = summed(jnp.pad(packed, (0, filled)).reshape(-1, 128), high_bits)
+    down_sum.last(packed)
     out_sum.onward(*down_sum.blocks_low)
     gate_sum.onward(out_sum.far_low)
     up_sum.last(gate_sum.far_low)
@@ -1045,26 +1060,12 @@
     out_sum.last(*gate_sum.blocks_low)
     mix_sum.last(*out_sum.blocks_low)
     input_sum.last(*mix_sum.blocks_low)
-    norm_one_grad = reordered(pair_sum(norm_one_part), to_whole)
-    conv_bc_grads = jnp.concatenate([bc_tap_grad[:KW].T.reshape(-1), bc_tap_grad[KW]])
-    conv_bc_grads = conv_bc_grads + swap(conv_bc_grads)
-    longer = tokens_longer.astype(jnp.float32)
-    scale_one = lax.rsqrt(jnp.mean(longer * longer, axis=1, keepdims=True) + epsilon)
-    gain_one_grad = jnp.sum(norm_one_grad * longer * scale_one, axis=0)
-    edge_back = shifted(keep_state * norm_one_grad[block_rows + EXTRA - 8 :], "ctx", -1)
+    edge_grad = after(norm_one_grad[block_rows + EXTRA - 8 :], *input_sum.blocks_low)
+    edge_back = shifted(keep_state * edge_grad, "ctx", -1)
     norm_one_grad = norm_one_grad[:block_rows] + jnp.pad(edge_back, ((block_rows - 8, 0), (0, 0)))
     _, norm_one_back = jax.vjp(lambda v: rms_scale(v, whole_order(mix_gain).reshape(-1)), inputs)
     tokens_grad = hidden_grad + norm_one_back(norm_one_grad)[0]
-    small = [
-        tap_sums[0].reshape(-1),
-        *tap_sums[1:],
-        conv_bc_grads,
-        gain_one_grad,
-        gain_two_grad,
-    ]
-    packed = jnp.concatenate(small)
-    filled = -packed.shape[0] % 1024
-    packed = summed(jnp.pad(packed, (0, filled)).reshape(-1, 128)).reshape(-1)
+    packed = summed(after(packed, *input_sum.blocks_low), (2, 1)).reshape(-1)
     sums, at = ([], 0)
     for part in small:
         sums.append(packed[at : at + part.shape[0]])

time: 1810 us -> 1720 us (0.950)
  waiting for transfers between devices: 824 us -> 682 us
  starting transfers between devices: 375 us -> 417 us
    ppermute x79, waiting for transfers between devices: 750 us -> 574 us  [hop(): lax.ppermute(value, 'ctx', [(source, source ^ code) for source in range(c...]
    ppermute x79, starting transfers between devices: 308 us -> 350 us  [hop(): lax.ppermute(value, 'ctx', [(source, source ^ code) for source in range(c...]
    ppermute x22, waiting for transfers between devices: 74.4 us -> 107 us  [shifted(): lax.ppermute(value, axis, [(source, source + steps) for source in range(l...]
    unnamed x295 -> x293, local copies, waits for them, and re-layouts: 49.5 us -> 50.5 us
  transfers between devices with their start and end apart: 110 -> 110, of which waited for: 39 -> 38; matrix products, arithmetic and copies ran while one was open for 20% -> 20% of each run, Pallas kernels for 8% -> 8%
where the time goes in v3:
time: 1720 us; the launch traced here: 1710 us
  waiting for transfers between devices  682 us (40%)
  starting transfers between devices  417 us (24%)
  matrix products  211 us (12%)
  Pallas kernels  149 us (9%)
  local copies, waits for them, and re-layouts  119 us (7%)
  other arithmetic  112 us (7%)
  between operations  18.3 us (1%)
    ppermute x79, waiting for transfers between devices, hop(): lax.ppermute(value, 'ctx', [(source, source ^ code) for source in range(c...  574 us
    ppermute x79, starting transfers between devices, hop(): lax.ppermute(value, 'ctx', [(source, source ^ code) for source in range(c...  350 us
    ppermute x22, waiting for transfers between devices, shifted(): lax.ppermute(value, axis, [(source, source + steps) for source in range(l...  107 us
    dot_general x28, matrix products, product_of_cols(): lax.dot_general(left_side, right_side, (((0,), (0,)), ((), ())), preferre...  88.6 us
    ppermute x22, starting transfers between devices, shifted(): lax.ppermute(value, axis, [(source, source + steps) for source in range(l...  65.9 us
    dot_general x7, matrix products, product_by_rows(): lax.dot_general(left_side, right_side, (((1,), (1,)), ((), ())), preferre...  60.1 us
    pallas_call x1, Pallas kernels, scan_back(): pl.pallas_call(body, grid=(pairs,), out_shape=(wide_low, eight_f32, table...  59.6 us
    dot_general x7, matrix products, plain_product(): return jnp.dot(left_side, right_side, preferred_element_type=jnp.float32)  59.2 us
  transfers between devices with their start and end apart: 110, of which 38 were waited for; matrix products, arithmetic and copies ran while one was open for 20% of the time, Pallas kernels for 8%

profile of v3, /device:TPU:0, one launch (start us, length us, event | category | flops | bytes accessed | tf_op | source)
XLA Modules:
  0.0 1707.9 jit_solution(10983220975792194262)
XLA Ops:
  23.7 46.5 %collective-permute-done.1 = bf16[128,4480]{1,0:T(8,128)(2,1)S(1)} collective-permute-done((bf16[128,4480]{1,0:T(8,128)(2,1)S(1)}, bf16[128,4480]{1,0:T(8,128)(2,1)S(1)}, u32[]{:S(2)}, u32[]{:S(2)}) %collective-permute-start.1) | collective-permute-done | bytes 1146912 | tf_op jit(solution)/shard_map/ppermute | solution.py:33
  71.1 28.2 %collective-permute-done.2 = bf16[128,4480]{1,0:T(8,128)(2,1)S(1)} collective-permute-done((bf16[128,4480]{1,0:T(8,128)(2,1)S(1)}, bf16[128,4480]{1,0:T(8,128)(2,1)S(1)}, u32[]{:S(2)}, u32[]{:S(2)}) %collective-permute-start.2) | collective-permute-done | bytes 1146912 | tf_op jit(solution)/shard_map/ppermute | solution.py:33
  113.1 21.0 %collective-permute-done.5 = bf16[512,1408]{1,0:T(8,128)(2,1)S(1)} collective-permute-done((bf16[512,1408]{1,0:T(8,128)(2,1)}, bf16[512,1408]{1,0:T(8,128)(2,1)S(1)}, u32[]{:S(2)}, u32[]{:S(2)}) %collective-permute-start.5) | collective-permute-done | bytes 1441824 | tf_op jit(solution)/shard_map/ppermute | solution.py:33
  150.5 22.8 %collective-permute-done.6 = bf16[512,1408]{1,0:T(8,128)(2,1)} collective-permute-done((bf16[512,1408]{1,0:T(8,128)(2,1)S(1)}, bf16[512,1408]{1,0:T(8,128)(2,1)}, u32[]{:S(2)}, u32[]{:S(2)}) %collective-permute-start.6) | collective-permute-done | bytes 1441824 | tf_op jit(solution)/shard_map/ppermute | solution.py:33
  193.3 24.9 %collective-permute-start.8 = (bf16[512,1536]{1,0:T(8,128)(2,1)}, bf16[512,1536]{1,0:T(8,128)(2,1)}, u32[]{:S(2)}, u32[]{:S(2)}) collective-permute-start(bf16[512,1536]{1,0:T(8,128)(2,1)} %pad_maximum_fusion.2), channel_id=1, source_target_pairs={{0,4},{2,6},{4,0},{6,2},{8,12},{10,14},{12,8},{14,10},{16,20},{18,... | collective-permute-start | bytes 4718600 | tf_op jit(solution)/shard_map/ppermute | solution.py:33
  219.2 8.8 collective-permute-done.7
  228.0 39.3 %collective-permute-start.9 = (bf16[512,1536]{1,0:T(8,128)(2,1)}, bf16[512,1536]{1,0:T(8,128)(2,1)}, u32[]{:S(2)}, u32[]{:S(2)}) collective-permute-start(bf16[512,1536]{1,0:T(8,128)(2,1)} %collective-permute-done.7), channel_id=1, source_target_pairs={{0,4},{2,6},{4,0},{6,2},{8,12},{10,14},{12,8},{14,10},{16,20},{18,... | collective-permute-start | bytes 4718600 | tf_op jit(solution)/shard_map/ppermute | solution.py:33
  283.9 30.2 %collective-permute-done.9 = bf16[512,1536]{1,0:T(8,128)(2,1)} collective-permute-done((bf16[512,1536]{1,0:T(8,128)(2,1)}, bf16[512,1536]{1,0:T(8,128)(2,1)}, u32[]{:S(2)}, u32[]{:S(2)}) %collective-permute-start.9) | collective-permute-done | bytes 1572896 | tf_op jit(solution)/shard_map/ppermute | solution.py:33
  316.8 8.0 fusion.174.in_ref.rim_ref
  324.8 22.0 %scan_forward.1 = (f32[512,1536]{1,0:T(8,128)}, bf16[256,1536]{1,0:T(8,128)(2,1)S(1)}, bf16[512,512]{1,0:T(8,128)(2,1)S(1)}) custom-call(f32[528,1536]{1,0:T(8,128)} %fusion.174.in_ref.rim_ref, f32[528,1536]{1,0:T(8,128)} %fusion.174.in_ref.rim_ref, f32[8,1536]{1,0:T(8,128)S(1)} %copy-done.14, f32[528,1408]{1,0:T(8,128)S(1)} %fusion.175.bc_ref.bc_rim_ref.query_ref, ...), custom_call_target="tpu_custom_call" | custom-call | tf_op jit(solution)/shard_map/scan_forward/pallas_call | solution.py:336
  369.1 13.3 collective-permute-done.33
  396.4 14.9 collective-permute-start.25
  453.6 6.8 collective-permute-start.31
  460.6 7.2 collective-permute-start.35
  468.9 21.9 %collective-permute-done.30 = bf16[512,256]{1,0:T(8,128)(2,1)S(1)} collective-permute-done((bf16[512,256]{1,0:T(8,128)(2,1)}, bf16[512,256]{1,0:T(8,128)(2,1)S(1)}, u32[]{:S(2)}, u32[]{:S(2)}) %collective-permute-start.30) | collective-permute-done | bytes 262176 | tf_op jit(solution)/shard_map/ppermute | solution.py:26
  498.6 86.3 %collective-permute-done.21 = bf16[256,384]{1,0:T(8,128)(2,1)S(1)} collective-permute-done((bf16[256,384]{1,0:T(8,128)(2,1)S(1)}, bf16[256,384]{1,0:T(8,128)(2,1)S(1)}, u32[]{:S(2)}, u32[]{:S(2)}) %collective-permute-start.21) | collective-permute-done | bytes 196640 | tf_op jit(solution)/shard_map/ppermute | solution.py:33
  584.9 11.0 collective-permute-start.19
  611.6 8.8 collective-permute-start.37
  623.4 28.3 %collective-permute-done.24 = bf16[512,1536]{1,0:T(8,128)(2,1)S(1)} collective-permute-done((bf16[512,1536]{1,0:T(8,128)(2,1)S(1)}, bf16[512,1536]{1,0:T(8,128)(2,1)S(1)}, u32[]{:S(2)}, u32[]{:S(2)}) %collective-permute-start.24) | collective-permute-done | bytes 1572896 | tf_op jit(solution)/shard_map/ppermute | solution.py:33
  657.1 9.4 scan_gated.1
  668.9 10.1 reduce-precision_convert_fusion.2
  691.1 10.0 collective-permute-done.45
  723.8 9.4 fusion.177
  733.3 10.5 fusion.178
  743.8 11.4 multiply_convert_fusion.1
  772.5 6.2 fusion.179
  778.7 10.4 fusion.171
  789.2 9.2 reduce-precision_convert_fusion.1
  829.3 10.7 fusion.180.grad_ref
  848.6 10.3 scan_gated_back.1
  863.7 8.2 fusion.181
  880.1 41.4 %collective-permute-done.44 = bf16[256,384]{1,0:T(8,128)(2,1)S(1)} collective-permute-done((bf16[256,384]{1,0:T(8,128)(2,1)S(1)}, bf16[256,384]{1,0:T(8,128)(2,1)S(1)}, u32[]{:S(2)}, u32[]{:S(2)}) %collective-permute-start.44) | collective-permute-done | bytes 196640 | tf_op jit(solution)/shard_map/ppermute | solution.py:26
  921.5 9.9 collective-permute-done.46
  935.4 10.6 attention_back.1
  956.2 59.6 %scan_back.1 = (bf16[528,1536]{1,0:T(8,128)(2,1)}, f32[8,1536]{1,0:T(8,128)}, f32[12,512,2]{2,1,0:T(8,128)}, f32[12,512,2]{2,1,0:T(8,128)}, f32[528,512]{1,0:T(8,128)}, /*index=5*/f32[8,512]{1,0:T(8,128)}) custom-call(f32[528,1536]{1,0:T(8,128)} %fusion.174.in_ref.rim_ref, f32[528,1536]{1,0:T(8,128)} %fusion.174.in_ref.rim_ref, ...), custom_call_target="tpu_custom_call" | custom-call | tf_op jit(solution)/shard_map/scan_back/pallas_call | solution.py:568
  1036.1 6.6 collective-permute-start.73
  1044.8 19.8 %collective-permute-done.55 = bf16[512,256]{1,0:T(8,128)(2,1)S(1)} collective-permute-done((bf16[512,256]{1,0:T(8,128)(2,1)S(1)}, bf16[512,256]{1,0:T(8,128)(2,1)S(1)}, u32[]{:S(2)}, u32[]{:S(2)}) %collective-permute-start.55) | collective-permute-done | bytes 262176 | tf_op jit(solution)/shard_map/ppermute | solution.py:26
  1082.6 8.3 reduce-precision_convert_fusion
  1095.1 13.7 collective-permute-start.63
  1108.8 31.3 %collective-permute-done.74 = bf16[2048,512]{1,0:T(8,128)(2,1)} collective-permute-done((bf16[2048,512]{1,0:T(8,128)(2,1)}, bf16[2048,512]{1,0:T(8,128)(2,1)}, u32[]{:S(2)}, u32[]{:S(2)}) %collective-permute-start.74) | collective-permute-done | bytes 2097184 | tf_op jit(solution)/shard_map/ppermute | solution.py:33
  1146.8 13.7 collective-permute-start.64
  1170.0 15.0 collective-permute-done.65
  1185.0 13.7 collective-permute-start.75
  1198.7 28.6 %collective-permute-done.66 = bf16[512,2048]{1,0:T(8,128)(2,1)} collective-permute-done((bf16[512,2048]{1,0:T(8,128)(2,1)}, bf16[512,2048]{1,0:T(8,128)(2,1)}, u32[]{:S(2)}, u32[]{:S(2)}) %collective-permute-start.66) | collective-permute-done | bytes 2097184 | tf_op jit(solution)/shard_map/ppermute | solution.py:33
  1233.5 6.3 reordered.9
  1243.5 19.1 %collective-permute-start.77 = (f32[120,128]{1,0:T(8,128)S(1)}, f32[120,128]{1,0:T(8,128)S(1)}, u32[]{:S(2)}, u32[]{:S(2)}) collective-permute-start(f32[120,128]{1,0:T(8,128)S(1)} %pad_bitcast_fusion), channel_id=1, source_target_pairs={{0,16},{2,18},{4,20},{6,22},{8,24},{10,26},{12,28},{14,30},{16,0},... | collective-permute-start | bytes 184328 | tf_op jit(solution)/shard_map/ppermute | solution.py:33
  1266.6 17.5 %collective-permute-start.69 = (bf16[512,1536]{1,0:T(8,128)(2,1)}, bf16[512,1536]{1,0:T(8,128)(2,1)S(1)}, u32[]{:S(2)}, u32[]{:S(2)}) collective-permute-start(bf16[512,1536]{1,0:T(8,128)(2,1)} %convolution_convert_fusion.1), channel_id=1, source_target_pairs={{0,4},{2,6},{4,0},{6,2},{8,12},{10,14},{12,8},{14,10},{16,20},{18,... | collective-permute-start | bytes 4718600 | tf_op jit(solution)/shard_map/ppermute | solution.py:33
  1296.3 21.1 %collective-permute-done.72 = bf16[2048,512]{1,0:T(8,128)(2,1)S(1)} collective-permute-done((bf16[2048,512]{1,0:T(8,128)(2,1)S(1)}, bf16[2048,512]{1,0:T(8,128)(2,1)S(1)}, u32[]{:S(2)}, u32[]{:S(2)}) %collective-permute-start.72) | collective-permute-done | bytes 2097184 | tf_op jit(solution)/shard_map/ppermute | solution.py:33
  1317.4 19.0 %collective-permute-start.105 = (bf16[2048,128]{1,0:T(8,128)(2,1)S(1)}, bf16[2048,128]{1,0:T(8,128)(2,1)S(1)}, u32[]{:S(2)}, u32[]{:S(2)}) collective-permute-start(bf16[2048,128]{1,0:T(8,128)(2,1)S(1)} %get-tuple-element.347), channel_id=1, source_target_pairs={{0,16},{2,18},{4,20},{6,22},{8,24},{10,26},{12,28},{14,30},{16,0},... | collective-permute-start | bytes 1572872 | tf_op jit(solution)/shard_map/ppermute | solution.py:33
  1336.5 14.7 collective-permute-start.106
  1362.4 7.0 collective-permute-done.106
  1369.3 14.8 collective-permute-start.62
  1385.3 12.9 collective-permute-done.68
  1407.9 21.3 %collective-permute-done.62 = bf16[512,1408]{1,0:T(8,128)(2,1)} collective-permute-done((bf16[512,1408]{1,0:T(8,128)(2,1)}, bf16[512,1408]{1,0:T(8,128)(2,1)}, u32[]{:S(2)}, u32[]{:S(2)}) %collective-permute-start.62) | collective-permute-done | bytes 1441824 | tf_op jit(solution)/shard_map/ppermute | solution.py:33
  1431.2 28.8 %collective-permute-done.61 = bf16[512,1408]{1,0:T(8,128)(2,1)S(1)} collective-permute-done((bf16[512,1408]{1,0:T(8,128)(2,1)}, bf16[512,1408]{1,0:T(8,128)(2,1)S(1)}, u32[]{:S(2)}, u32[]{:S(2)}) %collective-permute-start.61) | collective-permute-done | bytes 1441824 | tf_op jit(solution)/shard_map/ppermute | solution.py:33
  1465.1 6.7 collective-permute-done.58
  1476.4 23.9 %collective-permute-done.82 = bf16[512,1536]{1,0:T(8,128)(2,1)S(1)} collective-permute-done((bf16[512,1536]{1,0:T(8,128)(2,1)}, bf16[512,1536]{1,0:T(8,128)(2,1)S(1)}, u32[]{:S(2)}, u32[]{:S(2)}) %collective-permute-start.82) | collective-permute-done | bytes 1572896 | tf_op jit(solution)/shard_map/ppermute | solution.py:33
  1511.1 7.1 collective-permute-done.100
  1518.3 32.6 %collective-permute-start.86 = (bf16[128,1536]{1,0:T(8,128)(2,1)S(1)}, bf16[128,1536]{1,0:T(8,128)(2,1)S(1)}, u32[]{:S(2)}, u32[]{:S(2)}) collective-permute-start(bf16[128,1536]{1,0:T(8,128)(2,1)S(1)} %get-tuple-element.361), channel_id=1, source_target_pairs={{0,8},{2,10},{4,12},{6,14},{8,0},{10,2},{12,4},{14,6},{16,24},{18,... | collective-permute-start | bytes 1179656 | tf_op jit(solution)/shard_map/ppermute | solution.py:33
  1550.9 19.1 %collective-permute-done.99 = bf16[128,2048]{1,0:T(8,128)(2,1)S(1)} collective-permute-done((bf16[128,2048]{1,0:T(8,128)(2,1)S(1)}, bf16[128,2048]{1,0:T(8,128)(2,1)S(1)}, u32[]{:S(2)}, u32[]{:S(2)}) %collective-permute-start.99) | collective-permute-done | bytes 524320 | tf_op jit(solution)/shard_map/ppermute | solution.py:33
  1574.6 8.0 collective-permute-done.87
  1612.3 18.4 %collective-permute-done.96 = bf16[2048,128]{1,0:T(8,128)(2,1)S(1)} collective-permute-done((bf16[2048,128]{1,0:T(8,128)(2,1)S(1)}, bf16[2048,128]{1,0:T(8,128)(2,1)S(1)}, u32[]{:S(2)}, u32[]{:S(2)}) %collective-permute-start.96) | collective-permute-done | bytes 524320 | tf_op jit(solution)/shard_map/ppermute | solution.py:33
  1632.6 8.2 collective-permute-start.92
  1676.1 22.5 %collective-permute-done.90 = bf16[128,1536]{1,0:T(8,128)(2,1)} collective-permute-done((bf16[128,1536]{1,0:T(8,128)(2,1)}, bf16[128,1536]{1,0:T(8,128)(2,1)}, u32[]{:S(2)}, u32[]{:S(2)}) %collective-permute-start.90) | collective-permute-done | bytes 393248 | tf_op jit(solution)/shard_map/ppermute | solution.py:33
  (700 shorter events, 522.2 us)
Async XLA Ops:
  7.2 716.6 %all-gather.6.cloned.1.call-start = ((), (), s32[]{:S(2)}) async-start(), calls=%async_computation.1 | async-start | bytes 8912896 | tf_op jit(solution)/shard_map/all_gather | solution.py:876
  18.1 52.2 %collective-permute-start.1 = (bf16[128,4480]{1,0:T(8,128)(2,1)S(1)}, bf16[128,4480]{1,0:T(8,128)(2,1)S(1)}, u32[]{:S(2)}, u32[]{:S(2)}) collective-permute-start(bf16[128,4480]{1,0:T(8,128)(2,1)S(1)} %get-tuple-element.405), channel_id=1, source_target_pairs={{0,8},{2,10},{4,12},{6,14},{8,0},{10,2},{12,4},{14,6},{16,24},{18,... | collective-permute-start | bytes 3440648 | tf_op jit(solution)/shard_map/ppermute | solution.py:33
  21.1 78.2 %collective-permute-start.2 = (bf16[128,4480]{1,0:T(8,128)(2,1)S(1)}, bf16[128,4480]{1,0:T(8,128)(2,1)S(1)}, u32[]{:S(2)}, u32[]{:S(2)}) collective-permute-start(bf16[128,4480]{1,0:T(8,128)(2,1)S(1)} %get-tuple-element.405), channel_id=1, source_target_pairs={{0,16},{2,18},{4,20},{6,22},{8,24},{10,26},{12,28},{14,30},{16,0},... | collective-permute-start | bytes 3440648 | tf_op jit(solution)/shard_map/ppermute | solution.py:33
  23.7 76.5 %collective-permute-start.3 = (bf16[128,4480]{1,0:T(8,128)(2,1)S(1)}, bf16[128,4480]{1,0:T(8,128)(2,1)S(1)}, u32[]{:S(2)}, u32[]{:S(2)}) collective-permute-start(bf16[128,4480]{1,0:T(8,128)(2,1)S(1)} %get-tuple-element.405), channel_id=1, source_target_pairs={{0,24},{2,26},{4,28},{6,30},{8,16},{10,18},{12,20},{14,22},{16,8},... | collective-permute-start | bytes 3440648 | tf_op jit(solution)/shard_map/ppermute | solution.py:33
  111.8 34.8 %collective-permute-start.4 = (bf16[512,1408]{1,0:T(8,128)(2,1)}, bf16[512,1408]{1,0:T(8,128)(2,1)}, u32[]{:S(2)}, u32[]{:S(2)}) collective-permute-start(bf16[512,1408]{1,0:T(8,128)(2,1)} %pad_maximum_fusion.5), channel_id=1, source_target_pairs={{0,2},{2,0},{4,6},{6,4},{8,10},{10,8},{12,14},{14,12},{16,18},{18,... | collective-permute-start | bytes 4325384 | tf_op jit(solution)/shard_map/ppermute | solution.py:33
  134.1 39.2 %collective-permute-start.6 = (bf16[512,1408]{1,0:T(8,128)(2,1)S(1)}, bf16[512,1408]{1,0:T(8,128)(2,1)}, u32[]{:S(2)}, u32[]{:S(2)}) collective-permute-start(bf16[512,1408]{1,0:T(8,128)(2,1)S(1)} %collective-permute-done.5), channel_id=1, source_target_pairs={{0,2},{2,0},{4,6},{6,4},{8,10},{10,8},{12,14},{14,12},{16,18},{18,... | collective-permute-start | bytes 4325384 | tf_op jit(solution)/shard_map/ppermute | solution.py:33
  185.1 548.2 %all-gather.8.cloned.1.call-start = ((), (), s32[]{:S(2)}) async-start(), calls=%async_computation.2 | async-start | bytes 8912896 | tf_op jit(solution)/shard_map/all_gather | solution.py:912
  191.8 36.2 %collective-permute-start.7 = (bf16[512,1536]{1,0:T(8,128)(2,1)}, bf16[512,1536]{1,0:T(8,128)(2,1)}, u32[]{:S(2)}, u32[]{:S(2)}) collective-permute-start(bf16[512,1536]{1,0:T(8,128)(2,1)} %pad_maximum_fusion.2), channel_id=1, source_target_pairs={{0,2},{2,0},{4,6},{6,4},{8,10},{10,8},{12,14},{14,12},{16,18},{18,... | collective-permute-start | bytes 4718600 | tf_op jit(solution)/shard_map/ppermute | solution.py:33
  193.3 76.7 %collective-permute-start.8 = (bf16[512,1536]{1,0:T(8,128)(2,1)}, bf16[512,1536]{1,0:T(8,128)(2,1)}, u32[]{:S(2)}, u32[]{:S(2)}) collective-permute-start(bf16[512,1536]{1,0:T(8,128)(2,1)} %pad_maximum_fusion.2), channel_id=1, source_target_pairs={{0,4},{2,6},{4,0},{6,2},{8,12},{10,14},{12,8},{14,10},{16,20},{18,... | collective-permute-start | bytes 4718600 | tf_op jit(solution)/shard_map/ppermute | solution.py:33
  228.0 86.2 %collective-permute-start.9 = (bf16[512,1536]{1,0:T(8,128)(2,1)}, bf16[512,1536]{1,0:T(8,128)(2,1)}, u32[]{:S(2)}, u32[]{:S(2)}) collective-permute-start(bf16[512,1536]{1,0:T(8,128)(2,1)} %collective-permute-done.7), channel_id=1, source_target_pairs={{0,4},{2,6},{4,0},{6,2},{8,12},{10,14},{12,8},{14,10},{16,20},{18,... | collective-permute-start | bytes 4718600 | tf_op jit(solution)/shard_map/ppermute | solution.py:33
  347.7 396.1 %all-gather.4.cloned.1.call-start = ((), (), s32[]{:S(2)}) async-start(), calls=%async_computation | async-start | bytes 8912896 | tf_op jit(solution)/shard_map/all_gather | solution.py:852
  396.4 39.0 %collective-permute-start.25 = (bf16[512,256]{1,0:T(8,128)(2,1)}, bf16[512,256]{1,0:T(8,128)(2,1)S(1)}, u32[]{:S(2)}, u32[]{:S(2)}) collective-permute-start(bf16[512,256]{1,0:T(8,128)(2,1)} %pad_maximum_fusion.7), channel_id=1, source_target_pairs={{0,14},{2,16},{4,18},{6,20},{8,22},{10,24},{12,26},{14,28},{16,30}... | collective-permute-start | bytes 786440 | tf_op jit(solution)/shard_map/ppermute | solution.py:26
  446.6 156.6 %collective-permute-start.23 = (bf16[512,1536]{1,0:T(8,128)(2,1)}, bf16[512,1536]{1,0:T(8,128)(2,1)S(1)}, u32[]{:S(2)}, u32[]{:S(2)}) collective-permute-start(bf16[512,1536]{1,0:T(8,128)(2,1)} %pad_maximum_fusion.3), channel_id=1, source_target_pairs={{0,4},{2,6},{4,0},{6,2},{8,12},{10,14},{12,8},{14,10},{16,20},{18,... | collective-permute-start | bytes 4718600 | tf_op jit(solution)/shard_map/ppermute | solution.py:33
  451.6 39.2 %collective-permute-start.30 = (bf16[512,256]{1,0:T(8,128)(2,1)}, bf16[512,256]{1,0:T(8,128)(2,1)S(1)}, u32[]{:S(2)}, u32[]{:S(2)}) collective-permute-start(bf16[512,256]{1,0:T(8,128)(2,1)} %pad_maximum_fusion.7), channel_id=1, source_target_pairs={{0,4},{2,6},{4,8},{6,10},{8,12},{10,14},{12,16},{14,18},{16,20},{1... | collective-permute-start | bytes 786440 | tf_op jit(solution)/shard_map/ppermute | solution.py:26
  453.6 40.6 %collective-permute-start.31 = (bf16[512,256]{1,0:T(8,128)(2,1)}, bf16[512,256]{1,0:T(8,128)(2,1)S(1)}, u32[]{:S(2)}, u32[]{:S(2)}) collective-permute-start(bf16[512,256]{1,0:T(8,128)(2,1)} %pad_maximum_fusion.7), channel_id=1, source_target_pairs={{0,2},{2,4},{4,6},{6,8},{8,10},{10,12},{12,14},{14,16},{16,18},{18... | collective-permute-start | bytes 786440 | tf_op jit(solution)/shard_map/ppermute | solution.py:26
  460.6 151.0 %collective-permute-start.35 = (bf16[2048,512]{1,0:T(8,128)(2,1)S(1)}, bf16[2048,512]{1,0:T(8,128)(2,1)S(1)}, u32[]{:S(2)}, u32[]{:S(2)}) collective-permute-start(bf16[2048,512]{1,0:T(8,128)(2,1)S(1)} %copy-done.46), channel_id=1, source_target_pairs={{0,2},{2,0},{4,6},{6,4},{8,10},{10,8},{12,14},{14,12},{16,18},{18,... | collective-permute-start | bytes 6291464 | tf_op jit(solution)/shard_map/ppermute | solution.py:33
  467.8 139.4 %collective-permute-start.22 = (bf16[512,1536]{1,0:T(8,128)(2,1)S(1)}, bf16[512,1536]{1,0:T(8,128)(2,1)}, u32[]{:S(2)}, u32[]{:S(2)}) collective-permute-start(bf16[512,1536]{1,0:T(8,128)(2,1)S(1)} %copy-done.56), channel_id=1, source_target_pairs={{0,2},{2,0},{4,6},{6,4},{8,10},{10,8},{12,14},{14,12},{16,18},{18,... | collective-permute-start | bytes 4718600 | tf_op jit(solution)/shard_map/ppermute | solution.py:33
  494.2 127.7 %collective-permute-start.36 = (bf16[2048,512]{1,0:T(8,128)(2,1)S(1)}, bf16[2048,512]{1,0:T(8,128)(2,1)S(1)}, u32[]{:S(2)}, u32[]{:S(2)}) collective-permute-start(bf16[2048,512]{1,0:T(8,128)(2,1)S(1)} %copy-done.46), channel_id=1, source_target_pairs={{0,4},{2,6},{4,0},{6,2},{8,12},{10,14},{12,8},{14,10},{16,20},{18,... | collective-permute-start | bytes 6291464 | tf_op jit(solution)/shard_map/ppermute | solution.py:33
  498.5 86.4 %collective-permute-start.21 = (bf16[256,384]{1,0:T(8,128)(2,1)S(1)}, bf16[256,384]{1,0:T(8,128)(2,1)S(1)}, u32[]{:S(2)}, u32[]{:S(2)}) collective-permute-start(bf16[256,384]{1,0:T(8,128)(2,1)S(1)} %get-tuple-element.408), channel_id=1, source_target_pairs={{0,2},{2,0},{4,6},{6,4},{8,10},{10,8},{12,14},{14,12},{16,18},{18,... | collective-permute-start | bytes 589832 | tf_op jit(solution)/shard_map/ppermute | solution.py:33
  603.2 48.5 %collective-permute-start.24 = (bf16[512,1536]{1,0:T(8,128)(2,1)S(1)}, bf16[512,1536]{1,0:T(8,128)(2,1)S(1)}, u32[]{:S(2)}, u32[]{:S(2)}) collective-permute-start(bf16[512,1536]{1,0:T(8,128)(2,1)S(1)} %collective-permute-done.23), channel_id=1, source_target_pairs={{0,2},{2,0},{4,6},{6,4},{8,10},{10,8},{12,14},{14,12},{16,18},{18,... | collective-permute-start | bytes 4718600 | tf_op jit(solution)/shard_map/ppermute | solution.py:33
  611.6 55.2 %collective-permute-start.37 = (bf16[2048,512]{1,0:T(8,128)(2,1)S(1)}, bf16[2048,512]{1,0:T(8,128)(2,1)S(1)}, u32[]{:S(2)}, u32[]{:S(2)}) collective-permute-start(bf16[2048,512]{1,0:T(8,128)(2,1)S(1)} %collective-permute-done.35), channel_id=1, source_target_pairs={{0,4},{2,6},{4,0},{6,2},{8,12},{10,14},{12,8},{14,10},{16,20},{18,... | collective-permute-start | bytes 6291464 | tf_op jit(solution)/shard_map/ppermute | solution.py:33
  874.9 46.6 %collective-permute-start.44 = (bf16[256,384]{1,0:T(8,128)(2,1)S(1)}, bf16[256,384]{1,0:T(8,128)(2,1)S(1)}, u32[]{:S(2)}, u32[]{:S(2)}) collective-permute-start(bf16[256,384]{1,0:T(8,128)(2,1)S(1)} %get-tuple-element.308), channel_id=1, source_target_pairs={{8,0},{10,2},{12,4},{14,6},{16,8},{18,10},{20,12},{22,14},{24,16},... | collective-permute-start | bytes 589832 | tf_op jit(solution)/shard_map/ppermute | solution.py:26
  876.2 55.3 %collective-permute-start.46 = (bf16[256,384]{1,0:T(8,128)(2,1)S(1)}, bf16[256,384]{1,0:T(8,128)(2,1)S(1)}, u32[]{:S(2)}, u32[]{:S(2)}) collective-permute-start(bf16[256,384]{1,0:T(8,128)(2,1)S(1)} %get-tuple-element.308), channel_id=1, source_target_pairs={{16,0},{18,2},{20,4},{22,6},{24,8},{26,10},{28,12},{30,14},{17,1},... | collective-permute-start | bytes 589832 | tf_op jit(solution)/shard_map/ppermute | solution.py:26
  948.5 84.1 %collective-permute-start.50 = (bf16[512,256]{1,0:T(8,128)(2,1)}, bf16[512,256]{1,0:T(8,128)(2,1)}, u32[]{:S(2)}, u32[]{:S(2)}) collective-permute-start(bf16[512,256]{1,0:T(8,128)(2,1)} %get-tuple-element.349), channel_id=1, source_target_pairs={{2,0},{4,2},{6,4},{8,6},{10,8},{12,10},{14,12},{16,14},{18,16},{20... | collective-permute-start | bytes 786440 | tf_op jit(solution)/shard_map/ppermute | solution.py:26
  949.8 84.1 %collective-permute-start.51 = (bf16[512,256]{1,0:T(8,128)(2,1)}, bf16[512,256]{1,0:T(8,128)(2,1)}, u32[]{:S(2)}, u32[]{:S(2)}) collective-permute-start(bf16[512,256]{1,0:T(8,128)(2,1)} %get-tuple-element.355), channel_id=1, source_target_pairs={{4,0},{6,2},{8,4},{10,6},{12,8},{14,10},{16,12},{18,14},{20,16},{2... | collective-permute-start | bytes 786440 | tf_op jit(solution)/shard_map/ppermute | solution.py:26
  951.1 85.0 %collective-permute-start.52 = (bf16[512,256]{1,0:T(8,128)(2,1)}, bf16[512,256]{1,0:T(8,128)(2,1)}, u32[]{:S(2)}, u32[]{:S(2)}) collective-permute-start(bf16[512,256]{1,0:T(8,128)(2,1)} %get-tuple-element.354), channel_id=1, source_target_pairs={{6,0},{8,2},{10,4},{12,6},{14,8},{16,10},{18,12},{20,14},{22,16},{... | collective-permute-start | bytes 786440 | tf_op jit(solution)/shard_map/ppermute | solution.py:26
  952.4 90.3 %collective-permute-start.53 = (bf16[512,256]{1,0:T(8,128)(2,1)}, bf16[512,256]{1,0:T(8,128)(2,1)}, u32[]{:S(2)}, u32[]{:S(2)}) collective-permute-start(bf16[512,256]{1,0:T(8,128)(2,1)} %get-tuple-element.353), channel_id=1, source_target_pairs={{8,0},{10,2},{12,4},{14,6},{16,8},{18,10},{20,12},{22,14},{24,16},... | collective-permute-start | bytes 786440 | tf_op jit(solution)/shard_map/ppermute | solution.py:26
  953.7 89.1 %collective-permute-start.54 = (bf16[512,256]{1,0:T(8,128)(2,1)}, bf16[512,256]{1,0:T(8,128)(2,1)}, u32[]{:S(2)}, u32[]{:S(2)}) collective-permute-start(bf16[512,256]{1,0:T(8,128)(2,1)} %get-tuple-element.352), channel_id=1, source_target_pairs={{10,0},{12,2},{14,4},{16,6},{18,8},{20,10},{22,12},{24,14},{26,16}... | collective-permute-start | bytes 786440 | tf_op jit(solution)/shard_map/ppermute | solution.py:26
  1034.0 34.9 %collective-permute-start.56 = (bf16[512,256]{1,0:T(8,128)(2,1)S(1)}, bf16[512,256]{1,0:T(8,128)(2,1)S(1)}, u32[]{:S(2)}, u32[]{:S(2)}) collective-permute-start(bf16[512,256]{1,0:T(8,128)(2,1)S(1)} %get-tuple-element.350), channel_id=1, source_target_pairs={{14,0},{16,2},{18,4},{20,6},{22,8},{24,10},{26,12},{28,14},{30,16}... | collective-permute-start | bytes 786440 | tf_op jit(solution)/shard_map/ppermute | solution.py:26
  1036.1 59.0 %collective-permute-start.73 = (bf16[2048,512]{1,0:T(8,128)(2,1)}, bf16[2048,512]{1,0:T(8,128)(2,1)}, u32[]{:S(2)}, u32[]{:S(2)}) collective-permute-start(bf16[2048,512]{1,0:T(8,128)(2,1)} %convolution_convert_fusion.5), channel_id=1, source_target_pairs={{0,2},{2,0},{4,6},{6,4},{8,10},{10,8},{12,14},{14,12},{16,18},{18,... | collective-permute-start | bytes 6291464 | tf_op jit(solution)/shard_map/ppermute | solution.py:33
  1042.7 97.3 %collective-permute-start.74 = (bf16[2048,512]{1,0:T(8,128)(2,1)}, bf16[2048,512]{1,0:T(8,128)(2,1)}, u32[]{:S(2)}, u32[]{:S(2)}) collective-permute-start(bf16[2048,512]{1,0:T(8,128)(2,1)} %convolution_convert_fusion.4), channel_id=1, source_target_pairs={{0,2},{2,0},{4,6},{6,4},{8,10},{10,8},{12,14},{14,12},{16,18},{18,... | collective-permute-start | bytes 6291464 | tf_op jit(solution)/shard_map/ppermute | solution.py:33
  1042.8 142.2 %collective-permute-start.65 = (bf16[512,2048]{1,0:T(8,128)(2,1)}, bf16[512,2048]{1,0:T(8,128)(2,1)}, u32[]{:S(2)}, u32[]{:S(2)}) collective-permute-start(bf16[512,2048]{1,0:T(8,128)(2,1)} %convolution_convert_fusion.9), channel_id=1, source_target_pairs={{0,2},{2,0},{4,6},{6,4},{8,10},{10,8},{12,14},{14,12},{16,18},{18,... | collective-permute-start | bytes 6291464 | tf_op jit(solution)/shard_map/ppermute | solution.py:33
  1090.9 138.1 %collective-permute-start.57 = (bf16[528,2048]{1,0:T(8,128)(2,1)}, bf16[528,2048]{1,0:T(8,128)(2,1)}, u32[]{:S(2)}, u32[]{:S(2)}) collective-permute-start(bf16[528,2048]{1,0:T(8,128)(2,1)} %get-tuple-element.460), channel_id=1, source_target_pairs={{0,1},{1,0},{2,3},{3,2},{4,5},{5,4},{6,7},{7,6},{8,9},{9,8},{10,11... | collective-permute-start | bytes 6488072 | tf_op jit(solution)/shard_map/ppermute | solution.py:37
  1091.3 136.0 %collective-permute-start.66 = (bf16[512,2048]{1,0:T(8,128)(2,1)}, bf16[512,2048]{1,0:T(8,128)(2,1)}, u32[]{:S(2)}, u32[]{:S(2)}) collective-permute-start(bf16[512,2048]{1,0:T(8,128)(2,1)} %convolution_convert_fusion.8), channel_id=1, source_target_pairs={{0,2},{2,0},{4,6},{6,4},{8,10},{10,8},{12,14},{14,12},{16,18},{18,... | collective-permute-start | bytes 6291464 | tf_op jit(solution)/shard_map/ppermute | solution.py:33
  1095.1 171.2 %collective-permute-start.63 = (bf16[512,2048]{1,0:T(8,128)(2,1)}, bf16[512,2048]{1,0:T(8,128)(2,1)}, u32[]{:S(2)}, u32[]{:S(2)}) collective-permute-start(bf16[512,2048]{1,0:T(8,128)(2,1)} %convolution_convert_fusion.11), channel_id=1, source_target_pairs={{0,4},{2,6},{4,0},{6,2},{8,12},{10,14},{12,8},{14,10},{16,20},{18,... | collective-permute-start | bytes 6291464 | tf_op jit(solution)/shard_map/ppermute | solution.py:33
  1146.8 119.8 %collective-permute-start.64 = (bf16[512,2048]{1,0:T(8,128)(2,1)}, bf16[512,2048]{1,0:T(8,128)(2,1)}, u32[]{:S(2)}, u32[]{:S(2)}) collective-permute-start(bf16[512,2048]{1,0:T(8,128)(2,1)} %convolution_convert_fusion.10), channel_id=1, source_target_pairs={{0,4},{2,6},{4,0},{6,2},{8,12},{10,14},{12,8},{14,10},{16,20},{18,... | collective-permute-start | bytes 6291464 | tf_op jit(solution)/shard_map/ppermute | solution.py:33
  1185.0 104.0 %collective-permute-start.75 = (bf16[2048,512]{1,0:T(8,128)(2,1)}, bf16[2048,512]{1,0:T(8,128)(2,1)}, u32[]{:S(2)}, u32[]{:S(2)}) collective-permute-start(bf16[2048,512]{1,0:T(8,128)(2,1)} %add_convert_fusion.1), channel_id=1, source_target_pairs={{0,4},{2,6},{4,0},{6,2},{8,12},{10,14},{12,8},{14,10},{16,20},{18,... | collective-permute-start | bytes 6291464 | tf_op jit(solution)/shard_map/ppermute | solution.py:33
  1227.3 67.3 %collective-permute-start.71 = (bf16[2048,512]{1,0:T(8,128)(2,1)}, bf16[2048,512]{1,0:T(8,128)(2,1)}, u32[]{:S(2)}, u32[]{:S(2)}) collective-permute-start(bf16[2048,512]{1,0:T(8,128)(2,1)} %convolution_convert_fusion.7), channel_id=1, source_target_pairs={{0,2},{2,0},{4,6},{6,4},{8,10},{10,8},{12,14},{14,12},{16,18},{18,... | collective-permute-start | bytes 6291464 | tf_op jit(solution)/shard_map/ppermute | solution.py:33
  1243.5 40.6 %collective-permute-start.77 = (f32[120,128]{1,0:T(8,128)S(1)}, f32[120,128]{1,0:T(8,128)S(1)}, u32[]{:S(2)}, u32[]{:S(2)}) collective-permute-start(f32[120,128]{1,0:T(8,128)S(1)} %pad_bitcast_fusion), channel_id=1, source_target_pairs={{0,16},{2,18},{4,20},{6,22},{8,24},{10,26},{12,28},{14,30},{16,0},... | collective-permute-start | bytes 184328 | tf_op jit(solution)/shard_map/ppermute | solution.py:33
  1266.3 51.1 %collective-permute-start.72 = (bf16[2048,512]{1,0:T(8,128)(2,1)S(1)}, bf16[2048,512]{1,0:T(8,128)(2,1)S(1)}, u32[]{:S(2)}, u32[]{:S(2)}) collective-permute-start(bf16[2048,512]{1,0:T(8,128)(2,1)S(1)} %copy-done.116), channel_id=1, source_target_pairs={{0,2},{2,0},{4,6},{6,4},{8,10},{10,8},{12,14},{14,12},{16,18},{18,... | collective-permute-start | bytes 6291464 | tf_op jit(solution)/shard_map/ppermute | solution.py:33
  1266.6 69.8 %collective-permute-start.69 = (bf16[512,1536]{1,0:T(8,128)(2,1)}, bf16[512,1536]{1,0:T(8,128)(2,1)S(1)}, u32[]{:S(2)}, u32[]{:S(2)}) collective-permute-start(bf16[512,1536]{1,0:T(8,128)(2,1)} %convolution_convert_fusion.1), channel_id=1, source_target_pairs={{0,4},{2,6},{4,0},{6,2},{8,12},{10,14},{12,8},{14,10},{16,20},{18,... | collective-permute-start | bytes 4718600 | tf_op jit(solution)/shard_map/ppermute | solution.py:33
  1288.4 67.1 %collective-permute-start.70 = (bf16[512,1536]{1,0:T(8,128)(2,1)}, bf16[512,1536]{1,0:T(8,128)(2,1)}, u32[]{:S(2)}, u32[]{:S(2)}) collective-permute-start(bf16[512,1536]{1,0:T(8,128)(2,1)} %convolution_convert_fusion), channel_id=1, source_target_pairs={{0,4},{2,6},{4,0},{6,2},{8,12},{10,14},{12,8},{14,10},{16,20},{18,... | collective-permute-start | bytes 4718600 | tf_op jit(solution)/shard_map/ppermute | solution.py:33
  1289.1 109.1 %collective-permute-start.68 = (bf16[512,2048]{1,0:T(8,128)(2,1)S(1)}, bf16[512,2048]{1,0:T(8,128)(2,1)S(1)}, u32[]{:S(2)}, u32[]{:S(2)}) collective-permute-start(bf16[512,2048]{1,0:T(8,128)(2,1)S(1)} %add_convert_fusion.3), channel_id=1, source_target_pairs={{0,4},{2,6},{4,0},{6,2},{8,12},{10,14},{12,8},{14,10},{16,20},{18,... | collective-permute-start | bytes 6291464 | tf_op jit(solution)/shard_map/ppermute | solution.py:33
  1294.6 65.7 %collective-permute-start.104 = (bf16[2048,128]{1,0:T(8,128)(2,1)S(1)}, bf16[2048,128]{1,0:T(8,128)(2,1)S(1)}, u32[]{:S(2)}, u32[]{:S(2)}) collective-permute-start(bf16[2048,128]{1,0:T(8,128)(2,1)S(1)} %get-tuple-element.348), channel_id=1, source_target_pairs={{0,8},{2,10},{4,12},{6,14},{8,0},{10,2},{12,4},{14,6},{16,24},{18,... | collective-permute-start | bytes 1572872 | tf_op jit(solution)/shard_map/ppermute | solution.py:33
  1317.4 44.3 %collective-permute-start.105 = (bf16[2048,128]{1,0:T(8,128)(2,1)S(1)}, bf16[2048,128]{1,0:T(8,128)(2,1)S(1)}, u32[]{:S(2)}, u32[]{:S(2)}) collective-permute-start(bf16[2048,128]{1,0:T(8,128)(2,1)S(1)} %get-tuple-element.347), channel_id=1, source_target_pairs={{0,16},{2,18},{4,20},{6,22},{8,24},{10,26},{12,28},{14,30},{16,0},... | collective-permute-start | bytes 1572872 | tf_op jit(solution)/shard_map/ppermute | solution.py:33
  1355.5 49.0 %collective-permute-start.67 = (bf16[512,2048]{1,0:T(8,128)(2,1)}, bf16[512,2048]{1,0:T(8,128)(2,1)S(1)}, u32[]{:S(2)}, u32[]{:S(2)}) collective-permute-start(bf16[512,2048]{1,0:T(8,128)(2,1)} %add_convert_fusion.2), channel_id=1, source_target_pairs={{0,2},{2,0},{4,6},{6,4},{8,10},{10,8},{12,14},{14,12},{16,18},{18,... | collective-permute-start | bytes 6291464 | tf_op jit(solution)/shard_map/ppermute | solution.py:33
  1360.3 104.8 %collective-permute-start.59 = (bf16[512,1536]{1,0:T(8,128)(2,1)}, bf16[512,1536]{1,0:T(8,128)(2,1)}, u32[]{:S(2)}, u32[]{:S(2)}) collective-permute-start(bf16[512,1536]{1,0:T(8,128)(2,1)} %convolution_convert_fusion.2), channel_id=1, source_target_pairs={{0,2},{2,0},{4,6},{6,4},{8,10},{10,8},{12,14},{14,12},{16,18},{18,... | collective-permute-start | bytes 4718600 | tf_op jit(solution)/shard_map/ppermute | solution.py:33
  1361.8 110.0 %collective-permute-start.58 = (bf16[512,1536]{1,0:T(8,128)(2,1)}, bf16[512,1536]{1,0:T(8,128)(2,1)}, u32[]{:S(2)}, u32[]{:S(2)}) collective-permute-start(bf16[512,1536]{1,0:T(8,128)(2,1)} %convolution_convert_fusion.3), channel_id=1, source_target_pairs={{0,2},{2,0},{4,6},{6,4},{8,10},{10,8},{12,14},{14,12},{16,18},{18,... | collective-permute-start | bytes 4718600 | tf_op jit(solution)/shard_map/ppermute | solution.py:33
  1369.3 59.9 %collective-permute-start.62 = (bf16[512,1408]{1,0:T(8,128)(2,1)}, bf16[512,1408]{1,0:T(8,128)(2,1)}, u32[]{:S(2)}, u32[]{:S(2)}) collective-permute-start(bf16[512,1408]{1,0:T(8,128)(2,1)} %convolution_convert_fusion.12), channel_id=1, source_target_pairs={{0,4},{2,6},{4,0},{6,2},{8,12},{10,14},{12,8},{14,10},{16,20},{18,... | collective-permute-start | bytes 4325384 | tf_op jit(solution)/shard_map/ppermute | solution.py:33
  1398.2 61.8 %collective-permute-start.61 = (bf16[512,1408]{1,0:T(8,128)(2,1)}, bf16[512,1408]{1,0:T(8,128)(2,1)S(1)}, u32[]{:S(2)}, u32[]{:S(2)}) collective-permute-start(bf16[512,1408]{1,0:T(8,128)(2,1)} %convolution_convert_fusion.13), channel_id=1, source_target_pairs={{0,4},{2,6},{4,0},{6,2},{8,12},{10,14},{12,8},{14,10},{16,20},{18,... | collective-permute-start | bytes 4325384 | tf_op jit(solution)/shard_map/ppermute | solution.py:33
  1404.5 95.8 %collective-permute-start.82 = (bf16[512,1536]{1,0:T(8,128)(2,1)}, bf16[512,1536]{1,0:T(8,128)(2,1)S(1)}, u32[]{:S(2)}, u32[]{:S(2)}) collective-permute-start(bf16[512,1536]{1,0:T(8,128)(2,1)} %add_convert_fusion.5), channel_id=1, source_target_pairs={{0,2},{2,0},{4,6},{6,4},{8,10},{10,8},{12,14},{14,12},{16,18},{18,... | collective-permute-start | bytes 4718600 | tf_op jit(solution)/shard_map/ppermute | solution.py:33
  1429.2 154.5 %collective-permute-start.81 = (bf16[2048,512]{1,0:T(8,128)(2,1)S(1)}, bf16[2048,512]{1,0:T(8,128)(2,1)S(1)}, u32[]{:S(2)}, u32[]{:S(2)}) collective-permute-start(bf16[2048,512]{1,0:T(8,128)(2,1)S(1)} %copy-done.117), channel_id=1, source_target_pairs={{0,4},{2,6},{4,0},{6,2},{8,12},{10,14},{12,8},{14,10},{16,20},{18,... | collective-permute-start | bytes 6291464 | tf_op jit(solution)/shard_map/ppermute | solution.py:33
  1460.0 45.7 %collective-permute-start.101 = (bf16[128,2048]{1,0:T(8,128)(2,1)}, bf16[128,2048]{1,0:T(8,128)(2,1)S(1)}, u32[]{:S(2)}, u32[]{:S(2)}) collective-permute-start(bf16[128,2048]{1,0:T(8,128)(2,1)} %get-tuple-element.345), channel_id=1, source_target_pairs={{0,8},{2,10},{4,12},{6,14},{8,0},{10,2},{12,4},{14,6},{16,24},{18,... | collective-permute-start | bytes 1572872 | tf_op jit(solution)/shard_map/ppermute | solution.py:33
  1465.1 40.8 %collective-permute-start.102 = (bf16[128,2048]{1,0:T(8,128)(2,1)}, bf16[128,2048]{1,0:T(8,128)(2,1)S(1)}, u32[]{:S(2)}, u32[]{:S(2)}) collective-permute-start(bf16[128,2048]{1,0:T(8,128)(2,1)} %get-tuple-element.344), channel_id=1, source_target_pairs={{0,16},{2,18},{4,20},{6,22},{8,24},{10,26},{12,28},{14,30},{16,0},... | collective-permute-start | bytes 1572872 | tf_op jit(solution)/shard_map/ppermute | solution.py:33
  1471.8 37.5 %collective-permute-start.103 = (bf16[128,2048]{1,0:T(8,128)(2,1)}, bf16[128,2048]{1,0:T(8,128)(2,1)S(1)}, u32[]{:S(2)}, u32[]{:S(2)}) collective-permute-start(bf16[128,2048]{1,0:T(8,128)(2,1)} %get-tuple-element.343), channel_id=1, source_target_pairs={{0,24},{2,26},{4,28},{6,30},{8,16},{10,18},{12,20},{14,22},{16,8},... | collective-permute-start | bytes 1572872 | tf_op jit(solution)/shard_map/ppermute | solution.py:33
  1505.7 45.2 %collective-permute-start.98 = (bf16[128,2048]{1,0:T(8,128)(2,1)S(1)}, bf16[128,2048]{1,0:T(8,128)(2,1)S(1)}, u32[]{:S(2)}, u32[]{:S(2)}) collective-permute-start(bf16[128,2048]{1,0:T(8,128)(2,1)S(1)} %get-tuple-element.342), channel_id=1, source_target_pairs={{0,8},{2,10},{4,12},{6,14},{8,0},{10,2},{12,4},{14,6},{16,24},{18,... | collective-permute-start | bytes 1572872 | tf_op jit(solution)/shard_map/ppermute | solution.py:33
  1505.9 64.1 %collective-permute-start.99 = (bf16[128,2048]{1,0:T(8,128)(2,1)S(1)}, bf16[128,2048]{1,0:T(8,128)(2,1)S(1)}, u32[]{:S(2)}, u32[]{:S(2)}) collective-permute-start(bf16[128,2048]{1,0:T(8,128)(2,1)S(1)} %get-tuple-element.341), channel_id=1, source_target_pairs={{0,16},{2,18},{4,20},{6,22},{8,24},{10,26},{12,28},{14,30},{16,0},... | collective-permute-start | bytes 1572872 | tf_op jit(solution)/shard_map/ppermute | solution.py:33
  1509.3 85.8 %collective-permute-start.80 = (bf16[512,1408]{1,0:T(8,128)(2,1)}, bf16[512,1408]{1,0:T(8,128)(2,1)S(1)}, u32[]{:S(2)}, u32[]{:S(2)}) collective-permute-start(bf16[512,1408]{1,0:T(8,128)(2,1)} %add_convert_fusion.6), channel_id=1, source_target_pairs={{0,2},{2,0},{4,6},{6,4},{8,10},{10,8},{12,14},{14,12},{16,18},{18,... | collective-permute-start | bytes 4325384 | tf_op jit(solution)/shard_map/ppermute | solution.py:33
  1518.3 54.9 %collective-permute-start.86 = (bf16[128,1536]{1,0:T(8,128)(2,1)S(1)}, bf16[128,1536]{1,0:T(8,128)(2,1)S(1)}, u32[]{:S(2)}, u32[]{:S(2)}) collective-permute-start(bf16[128,1536]{1,0:T(8,128)(2,1)S(1)} %get-tuple-element.361), channel_id=1, source_target_pairs={{0,8},{2,10},{4,12},{6,14},{8,0},{10,2},{12,4},{14,6},{16,24},{18,... | collective-permute-start | bytes 1179656 | tf_op jit(solution)/shard_map/ppermute | solution.py:33
  1592.6 38.2 %collective-permute-start.96 = (bf16[2048,128]{1,0:T(8,128)(2,1)S(1)}, bf16[2048,128]{1,0:T(8,128)(2,1)S(1)}, u32[]{:S(2)}, u32[]{:S(2)}) collective-permute-start(bf16[2048,128]{1,0:T(8,128)(2,1)S(1)} %get-tuple-element.338), channel_id=1, source_target_pairs={{0,16},{2,18},{4,20},{6,22},{8,24},{10,26},{12,28},{14,30},{16,0},... | collective-permute-start | bytes 1572872 | tf_op jit(solution)/shard_map/ppermute | solution.py:33
  1592.6 38.2 %collective-permute-start.97 = (bf16[2048,128]{1,0:T(8,128)(2,1)S(1)}, bf16[2048,128]{1,0:T(8,128)(2,1)S(1)}, u32[]{:S(2)}, u32[]{:S(2)}) collective-permute-start(bf16[2048,128]{1,0:T(8,128)(2,1)S(1)} %get-tuple-element.337), channel_id=1, source_target_pairs={{0,24},{2,26},{4,28},{6,30},{8,16},{10,18},{12,20},{14,22},{16,8},... | collective-permute-start | bytes 1572872 | tf_op jit(solution)/shard_map/ppermute | solution.py:33
  1603.8 39.4 %collective-permute-start.84 = (f32[120,128]{1,0:T(8,128)S(1)}, f32[120,128]{1,0:T(8,128)S(1)}, u32[]{:S(2)}, u32[]{:S(2)}) collective-permute-start(f32[120,128]{1,0:T(8,128)S(1)} %copy-done.80), channel_id=1, source_target_pairs={{0,4},{2,6},{4,0},{6,2},{8,12},{10,14},{12,8},{14,10},{16,20},{18,... | collective-permute-start | bytes 184328 | tf_op jit(solution)/shard_map/ppermute | solution.py:33
  1605.2 39.1 %collective-permute-start.83 = (f32[8,2048]{1,0:T(8,128)S(1)}, f32[8,2048]{1,0:T(8,128)S(1)}, u32[]{:S(2)}, u32[]{:S(2)}) collective-permute-start(f32[8,2048]{1,0:T(8,128)S(1)} %broadcast_multiply_fusion.1), channel_id=1, source_target_pairs={{2,0},{4,2},{6,4},{8,6},{10,8},{12,10},{14,12},{16,14},{18,16},{20... | collective-permute-start | bytes 196616 | tf_op jit(solution)/shard_map/ppermute | solution.py:26
  1649.5 49.2 %collective-permute-start.90 = (bf16[128,1536]{1,0:T(8,128)(2,1)}, bf16[128,1536]{1,0:T(8,128)(2,1)}, u32[]{:S(2)}, u32[]{:S(2)}) collective-permute-start(bf16[128,1536]{1,0:T(8,128)(2,1)} %get-tuple-element.357), channel_id=1, source_target_pairs={{0,16},{2,18},{4,20},{6,22},{8,24},{10,26},{12,28},{14,30},{16,0},... | collective-permute-start | bytes 1179656 | tf_op jit(solution)/shard_map/ppermute | solution.py:33
  (178 other events, 4580.7 us)
Sparse Core Ops, SparseCore 0:
  185.2 173.5 all-gather.5
  361.5 211.7 all-gather.7
  576.0 150.6 all-gather.3
